TPU v7x, 128 devices: a whole 4x4x4 slice. The times are simulated.
128 devices in a mesh: ao: 8 (over z, core), mo: 16 (over x, y).
Axes of the slice: x: 4, y: 4, z: 4, core: 2. Of those that a mesh axis runs over, the one named last changes fastest.
Arguments:
- pair_ints: bfloat16 [128, 4096, 256], P(('ao', 'mo')), may hold values from -6 to 6
- shell_pairs: int32 [128, 2], replicated, may hold values from 0 to 31, as said below
- occ_lam: bfloat16 [16, 32], replicated, may hold values from -1.5 to 1.5
- occ_sig: bfloat16 [16, 8], replicated, may hold values from -1.5 to 1.5
- coef_act: bfloat16 [2048, 2048], P(None, 'mo'), may hold values from -0.1875 to 0.1875
- slabs: int32 [2], replicated, may hold values from 0 to 7, as said below
Outputs:
- mo_ints: bfloat16 [2, 8, 4, 2048, 2048], P(None, 'ao', None, 'mo')
Inputs may be any that keep to these rules, and one draw needn't show every extreme that they name: `shell_pairs`: each row holds two shell numbers P <= Q, no two rows are equal, and some row holds 0 and 31. `slabs`: the two slab numbers differ.
All inputs are finite; a program needn't handle non-finite values.
Results may differ from a plain program's by a relative error of at most 0.0066.
Values may be sent and summed in bfloat16 or wider, within the bound.
No kernel may reach another device: no remote copies, remote signals or barrier semaphores. Data moves between devices by JAX's collectives and lax.ppermute only.
A program may use at most 128 MiB of HBM per device.

v0:
```python
import jax
import jax.numpy as jnp
from jax import lax
from jax.sharding import PartitionSpec as P

SH = 64
NSH = 32
ACT = 2048
KL = 16
KS = 16
NI = 4


def ket_transform(pair_ints, occ_lam, occ_sig, slab_index):
    blocks_here = pair_ints.shape[0]
    nj_all = occ_sig.shape[1]
    lam_cols = lax.dynamic_slice_in_dim(occ_lam, slab_index * NI, NI, 1).astype(jnp.float32)
    pair_coef = occ_sig.astype(jnp.float32).T[:, None, None, :] * lam_cols.T[None, :, :, None]
    pair_coef = pair_coef.reshape(nj_all * NI, KL * KS).astype(jnp.bfloat16)
    half_ints = jnp.einsum("bqw,xw->bxq", pair_ints, pair_coef, preferred_element_type=jnp.float32)
    return half_ints.astype(jnp.bfloat16).reshape(blocks_here, nj_all, NI, SH * SH)


def remap_pairs(stacked):
    owned = lax.all_to_all(stacked, "ao", split_axis=2, concat_axis=1, tiled=True)
    return lax.all_gather(owned, "mo", axis=1, tiled=True)


def body(pair_ints, shell_pairs, occ_lam, occ_sig, coef_act, slabs):
    ao_count = lax.axis_size("ao")
    mo_count = lax.axis_size("mo")
    blocks_here = pair_ints.shape[0]
    panel_width = coef_act.shape[1]
    ao_width = coef_act.shape[0]
    first_half = ket_transform(pair_ints, occ_lam, occ_sig, slabs[0])
    second_half = ket_transform(pair_ints, occ_lam, occ_sig, slabs[1])
    ordered_pairs = (
        shell_pairs.reshape(ao_count, mo_count, blocks_here, 2).transpose(1, 0, 2, 3).reshape(-1, 2)
    )
    gathered_slabs = [remap_pairs(single[None])[0] for single in (first_half, second_half)]
    coef_shells = coef_act.reshape(NSH, SH, panel_width)
    shell_numbers = jnp.arange(NSH, dtype=jnp.int32)

    def bra_transform(gathered):
        block_count = gathered.shape[0]
        pair_rows = gathered.shape[1] * gathered.shape[2]
        grouped = gathered.reshape(block_count // 16, 16, pair_rows, SH, SH)
        grouped_pairs = ordered_pairs.reshape(block_count // 16, 16, 2)

        def accumulate(running, group_item):
            block_vals, block_pairs = group_item
            shell_one = block_pairs[:, 0]
            shell_two = block_pairs[:, 1]
            coef_one = jnp.take(coef_shells, shell_one, axis=0)
            coef_two = jnp.take(coef_shells, shell_two, axis=0)
            term_one = jnp.einsum(
                "prmn,pma->pran", block_vals, coef_one, preferred_element_type=jnp.float32
            )
            term_two = jnp.einsum(
                "prmn,pna->pram", block_vals, coef_two, preferred_element_type=jnp.float32
            )
            differs = (shell_one != shell_two).astype(jnp.float32)
            place_two = (shell_two[:, None] == shell_numbers[None, :]).astype(jnp.float32)
            place_one = (shell_one[:, None] == shell_numbers[None, :]).astype(
                jnp.float32
            ) * differs[:, None]
            added = jnp.einsum(
                "ps,pran->rasn", place_two, term_one, precision=lax.Precision.HIGHEST
            )
            added = added + jnp.einsum(
                "ps,pram->rasm", place_one, term_two, precision=lax.Precision.HIGHEST
            )
            return (running + added, None)

        start_terms = jnp.zeros((pair_rows, panel_width, NSH, SH), jnp.float32)
        left_terms = lax.scan(accumulate, start_terms, (grouped, grouped_pairs))[0]
        left_rounded = left_terms.astype(jnp.bfloat16).reshape(pair_rows * panel_width, ao_width)
        product = jnp.dot(
            left_rounded,
            lax.all_gather(coef_act, "mo", axis=1, tiled=True),
            preferred_element_type=jnp.float32,
        )
        return product.astype(jnp.bfloat16).reshape(gathered.shape[1], NI, panel_width, ACT)

    results = [bra_transform(gathered) for gathered in gathered_slabs]
    return jnp.stack(results)


def solution(mesh):
    return jax.shard_map(
        body,
        mesh=mesh,
        in_specs=(P(("ao", "mo"), None, None), P(), P(), P(), P(None, "mo"), P()),
        out_specs=P(None, "ao", None, "mo", None),
        check_vma=False,
    )
```

profile of v0, /device:TPU:0, one launch (start us, length us, event | category | flops | bytes accessed | tf_op | source)
XLA Modules:
  0.0 472.3 jit_solution(15201697235260343080)
XLA Ops:
  12.2 12.8 %all_to_all.24 = bf16[1,1,8,4,4096]{4,3,1,0,2:T(4,128)(2,1)} all-to-all(bf16[1,1,8,4,4096]{4,3,1,0,2:T(4,128)(2,1)S(1)} %bitcast.198), channel_id=1, replica_groups=mesh['ao'=8,'mo'=16] {'ao'}, dimensions={2} | all-to-all | bytes 524288 | tf_op jit(solution)/shard_map/all_to_all | solution.py:25
  26.1 10.6 %all_to_all.25 = bf16[1,1,8,4,4096]{4,3,1,0,2:T(4,128)(2,1)} all-to-all(bf16[1,1,8,4,4096]{4,3,1,0,2:T(4,128)(2,1)S(1)} %bitcast.199), channel_id=1, replica_groups=mesh['ao'=8,'mo'=16] {'ao'}, dimensions={2} | all-to-all | bytes 524288 | tf_op jit(solution)/shard_map/all_to_all | solution.py:25
  37.8 38.4 %all-gather.8.cloned.1.call-done = bf16[1,1,128,4,4096]{4,3,1,0,2:T(4,128)(2,1)} async-done(((bf16[1,1,8,4,4096]{4,3,1,0,2:T(4,128)(2,1)}), bf16[1,1,128,4,4096]{4,3,1,0,2:T(4,128)(2,1)}) %all-gather.8.cloned.1.call-update) | async-done | bytes 4194320 | tf_op jit(solution)/shard_map/all_gather | solution.py:26
  76.1 12.7 %reshape_squeeze.6 = bf16[8,16,4,64,64]{4,3,2,1,0:T(8,128)(2,1)} reshape(bf16[1,1,128,4,4096]{4,3,1,0,2:T(4,128)(2,1)} %all-gather.8.cloned.1.call-done) | data formatting | bytes 8388608 | tf_op jit(solution)/shard_map/reshape;squeeze | solution.py:47
  88.8 168.9 %while.24 = (s32[]{:T(128)}, f32[4,128,32,64]{1,2,3,0:T(8,128)}, s32[8,16,2]{1,2,0:T(2,128)S(1)}, bf16[32,64,128]{2,1,0:T(8,128)(2,1)S(1)}, bf16[8,16,4,64,64]{4,3,2,1,0:T(8,128)(2,1)}, /*index=5*/s32[]{:T(128)}, s32[]{:T(128)}) while((s32[]{:T(128)}, f32[4,128,32,64]{1,2,3,0:T(8,128)}, s32[8,16,2]{1,2,0:T(2,128)S(1)}, ...), condition=%wide.region_1.3_spmd.clone.clone, body=%wide.region_0.2_spmd.clone.clone.sunk | while | flops 540282624 | bytes 29894176 | solution.py:76
  99.3 9.5 %bitcast_add_fusion.4 = f32[4,128,32,64]{1,2,3,0:T(8,128)} fusion(f32[4,128,32,64]{1,2,3,0:T(8,128)} %get-tuple-element.339, f32[4,128,64,32]{1,3,2,0:T(8,128)} %fusion.96, f32[16,4,128,64]{2,3,1,0:T(8,128)} %convolution_bitcast_fusion.4, pred[]{:T(512)S(6)} %compare.6, f32[16]{0:T(128)S(1)} %fusion.97, s32[16]{0:T(128)S(1)} %get-tuple-element.296), kind=kOutput, calls=%fused_computation.6.clone.1 | convolution fusion | flops 204473344 | bytes 14680193 | tf_op jit(solution)/shard_map/while/body/eval_jaxpr/ps,pram->rasm/dot_general | solution.py:70
  119.2 10.8 %bitcast_add_fusion.4 = f32[4,128,32,64]{1,2,3,0:T(8,128)} fusion(f32[4,128,32,64]{1,2,3,0:T(8,128)} %get-tuple-element.339, f32[4,128,64,32]{1,3,2,0:T(8,128)} %fusion.96, f32[16,4,128,64]{2,3,1,0:T(8,128)} %convolution_bitcast_fusion.4, pred[]{:T(512)S(6)} %compare.6, f32[16]{0:T(128)S(1)} %fusion.97, s32[16]{0:T(128)S(1)} %get-tuple-element.296), kind=kOutput, calls=%fused_computation.6.clone.1 | convolution fusion | flops 204473344 | bytes 14680193 | tf_op jit(solution)/shard_map/while/body/eval_jaxpr/ps,pram->rasm/dot_general | solution.py:70
  140.6 11.0 %bitcast_add_fusion.4 = f32[4,128,32,64]{1,2,3,0:T(8,128)} fusion(f32[4,128,32,64]{1,2,3,0:T(8,128)} %get-tuple-element.339, f32[4,128,64,32]{1,3,2,0:T(8,128)} %fusion.96, f32[16,4,128,64]{2,3,1,0:T(8,128)} %convolution_bitcast_fusion.4, pred[]{:T(512)S(6)} %compare.6, f32[16]{0:T(128)S(1)} %fusion.97, s32[16]{0:T(128)S(1)} %get-tuple-element.296), kind=kOutput, calls=%fused_computation.6.clone.1 | convolution fusion | flops 204473344 | bytes 14680193 | tf_op jit(solution)/shard_map/while/body/eval_jaxpr/ps,pram->rasm/dot_general | solution.py:70
  162.0 10.7 %bitcast_add_fusion.4 = f32[4,128,32,64]{1,2,3,0:T(8,128)} fusion(f32[4,128,32,64]{1,2,3,0:T(8,128)} %get-tuple-element.339, f32[4,128,64,32]{1,3,2,0:T(8,128)} %fusion.96, f32[16,4,128,64]{2,3,1,0:T(8,128)} %convolution_bitcast_fusion.4, pred[]{:T(512)S(6)} %compare.6, f32[16]{0:T(128)S(1)} %fusion.97, s32[16]{0:T(128)S(1)} %get-tuple-element.296), kind=kOutput, calls=%fused_computation.6.clone.1 | convolution fusion | flops 204473344 | bytes 14680193 | tf_op jit(solution)/shard_map/while/body/eval_jaxpr/ps,pram->rasm/dot_general | solution.py:70
  183.2 11.1 %bitcast_add_fusion.4 = f32[4,128,32,64]{1,2,3,0:T(8,128)} fusion(f32[4,128,32,64]{1,2,3,0:T(8,128)} %get-tuple-element.339, f32[4,128,64,32]{1,3,2,0:T(8,128)} %fusion.96, f32[16,4,128,64]{2,3,1,0:T(8,128)} %convolution_bitcast_fusion.4, pred[]{:T(512)S(6)} %compare.6, f32[16]{0:T(128)S(1)} %fusion.97, s32[16]{0:T(128)S(1)} %get-tuple-element.296), kind=kOutput, calls=%fused_computation.6.clone.1 | convolution fusion | flops 204473344 | bytes 14680193 | tf_op jit(solution)/shard_map/while/body/eval_jaxpr/ps,pram->rasm/dot_general | solution.py:70
  204.8 10.7 %bitcast_add_fusion.4 = f32[4,128,32,64]{1,2,3,0:T(8,128)} fusion(f32[4,128,32,64]{1,2,3,0:T(8,128)} %get-tuple-element.339, f32[4,128,64,32]{1,3,2,0:T(8,128)} %fusion.96, f32[16,4,128,64]{2,3,1,0:T(8,128)} %convolution_bitcast_fusion.4, pred[]{:T(512)S(6)} %compare.6, f32[16]{0:T(128)S(1)} %fusion.97, s32[16]{0:T(128)S(1)} %get-tuple-element.296), kind=kOutput, calls=%fused_computation.6.clone.1 | convolution fusion | flops 204473344 | bytes 14680193 | tf_op jit(solution)/shard_map/while/body/eval_jaxpr/ps,pram->rasm/dot_general | solution.py:70
  225.9 10.7 %bitcast_add_fusion.4 = f32[4,128,32,64]{1,2,3,0:T(8,128)} fusion(f32[4,128,32,64]{1,2,3,0:T(8,128)} %get-tuple-element.339, f32[4,128,64,32]{1,3,2,0:T(8,128)} %fusion.96, f32[16,4,128,64]{2,3,1,0:T(8,128)} %convolution_bitcast_fusion.4, pred[]{:T(512)S(6)} %compare.6, f32[16]{0:T(128)S(1)} %fusion.97, s32[16]{0:T(128)S(1)} %get-tuple-element.296), kind=kOutput, calls=%fused_computation.6.clone.1 | convolution fusion | flops 204473344 | bytes 14680193 | tf_op jit(solution)/shard_map/while/body/eval_jaxpr/ps,pram->rasm/dot_general | solution.py:70
  247.1 10.7 %bitcast_add_fusion.4 = f32[4,128,32,64]{1,2,3,0:T(8,128)} fusion(f32[4,128,32,64]{1,2,3,0:T(8,128)} %get-tuple-element.339, f32[4,128,64,32]{1,3,2,0:T(8,128)} %fusion.96, f32[16,4,128,64]{2,3,1,0:T(8,128)} %convolution_bitcast_fusion.4, pred[]{:T(512)S(6)} %compare.6, f32[16]{0:T(128)S(1)} %fusion.97, s32[16]{0:T(128)S(1)} %get-tuple-element.296), kind=kOutput, calls=%fused_computation.6.clone.1 | convolution fusion | flops 204473344 | bytes 14680193 | tf_op jit(solution)/shard_map/while/body/eval_jaxpr/ps,pram->rasm/dot_general | solution.py:70
  263.4 12.7 %reshape_squeeze.7 = bf16[8,16,4,64,64]{4,3,2,1,0:T(8,128)(2,1)} reshape(bf16[1,1,128,4,4096]{4,3,1,0,2:T(4,128)(2,1)} %all-gather.10.cloned.1.call-done) | data formatting | bytes 8388608 | tf_op jit(solution)/shard_map/reshape;squeeze | solution.py:47
  276.1 168.1 %while.25 = (s32[]{:T(128)}, f32[4,128,32,64]{1,2,3,0:T(8,128)}, s32[8,16,2]{1,2,0:T(2,128)S(1)}, bf16[32,64,128]{2,1,0:T(8,128)(2,1)S(1)}, bf16[8,16,4,64,64]{4,3,2,1,0:T(8,128)(2,1)}, /*index=5*/s32[]{:T(128)}, s32[]{:T(128)}) while((s32[]{:T(128)}, f32[4,128,32,64]{1,2,3,0:T(8,128)}, s32[8,16,2]{1,2,0:T(2,128)S(1)}, ...), condition=%wide.region_3.5_spmd.clone.clone, body=%wide.region_2.4_spmd.clone.clone.sunk | while | flops 540282624 | bytes 29894176 | solution.py:76
  286.5 9.5 %bitcast_add_fusion.5 = f32[4,128,32,64]{1,2,3,0:T(8,128)} fusion(f32[4,128,32,64]{1,2,3,0:T(8,128)} %get-tuple-element.318, f32[4,128,64,32]{1,3,2,0:T(8,128)} %fusion.107, f32[16,4,128,64]{2,3,1,0:T(8,128)} %convolution_bitcast_fusion.5, pred[]{:T(512)S(6)} %compare.7, f32[16]{0:T(128)S(1)} %fusion.108, s32[16]{0:T(128)S(1)} %get-tuple-element.309), kind=kOutput, calls=%fused_computation.44.clone.1 | convolution fusion | flops 204473344 | bytes 14680193 | tf_op jit(solution)/shard_map/while/body/eval_jaxpr/ps,pram->rasm/dot_general | solution.py:70
  306.5 10.7 %bitcast_add_fusion.5 = f32[4,128,32,64]{1,2,3,0:T(8,128)} fusion(f32[4,128,32,64]{1,2,3,0:T(8,128)} %get-tuple-element.318, f32[4,128,64,32]{1,3,2,0:T(8,128)} %fusion.107, f32[16,4,128,64]{2,3,1,0:T(8,128)} %convolution_bitcast_fusion.5, pred[]{:T(512)S(6)} %compare.7, f32[16]{0:T(128)S(1)} %fusion.108, s32[16]{0:T(128)S(1)} %get-tuple-element.309), kind=kOutput, calls=%fused_computation.44.clone.1 | convolution fusion | flops 204473344 | bytes 14680193 | tf_op jit(solution)/shard_map/while/body/eval_jaxpr/ps,pram->rasm/dot_general | solution.py:70
  327.7 10.7 %bitcast_add_fusion.5 = f32[4,128,32,64]{1,2,3,0:T(8,128)} fusion(f32[4,128,32,64]{1,2,3,0:T(8,128)} %get-tuple-element.318, f32[4,128,64,32]{1,3,2,0:T(8,128)} %fusion.107, f32[16,4,128,64]{2,3,1,0:T(8,128)} %convolution_bitcast_fusion.5, pred[]{:T(512)S(6)} %compare.7, f32[16]{0:T(128)S(1)} %fusion.108, s32[16]{0:T(128)S(1)} %get-tuple-element.309), kind=kOutput, calls=%fused_computation.44.clone.1 | convolution fusion | flops 204473344 | bytes 14680193 | tf_op jit(solution)/shard_map/while/body/eval_jaxpr/ps,pram->rasm/dot_general | solution.py:70
  348.8 10.7 %bitcast_add_fusion.5 = f32[4,128,32,64]{1,2,3,0:T(8,128)} fusion(f32[4,128,32,64]{1,2,3,0:T(8,128)} %get-tuple-element.318, f32[4,128,64,32]{1,3,2,0:T(8,128)} %fusion.107, f32[16,4,128,64]{2,3,1,0:T(8,128)} %convolution_bitcast_fusion.5, pred[]{:T(512)S(6)} %compare.7, f32[16]{0:T(128)S(1)} %fusion.108, s32[16]{0:T(128)S(1)} %get-tuple-element.309), kind=kOutput, calls=%fused_computation.44.clone.1 | convolution fusion | flops 204473344 | bytes 14680193 | tf_op jit(solution)/shard_map/while/body/eval_jaxpr/ps,pram->rasm/dot_general | solution.py:70
  370.0 10.7 %bitcast_add_fusion.5 = f32[4,128,32,64]{1,2,3,0:T(8,128)} fusion(f32[4,128,32,64]{1,2,3,0:T(8,128)} %get-tuple-element.318, f32[4,128,64,32]{1,3,2,0:T(8,128)} %fusion.107, f32[16,4,128,64]{2,3,1,0:T(8,128)} %convolution_bitcast_fusion.5, pred[]{:T(512)S(6)} %compare.7, f32[16]{0:T(128)S(1)} %fusion.108, s32[16]{0:T(128)S(1)} %get-tuple-element.309), kind=kOutput, calls=%fused_computation.44.clone.1 | convolution fusion | flops 204473344 | bytes 14680193 | tf_op jit(solution)/shard_map/while/body/eval_jaxpr/ps,pram->rasm/dot_general | solution.py:70
  391.2 10.7 %bitcast_add_fusion.5 = f32[4,128,32,64]{1,2,3,0:T(8,128)} fusion(f32[4,128,32,64]{1,2,3,0:T(8,128)} %get-tuple-element.318, f32[4,128,64,32]{1,3,2,0:T(8,128)} %fusion.107, f32[16,4,128,64]{2,3,1,0:T(8,128)} %convolution_bitcast_fusion.5, pred[]{:T(512)S(6)} %compare.7, f32[16]{0:T(128)S(1)} %fusion.108, s32[16]{0:T(128)S(1)} %get-tuple-element.309), kind=kOutput, calls=%fused_computation.44.clone.1 | convolution fusion | flops 204473344 | bytes 14680193 | tf_op jit(solution)/shard_map/while/body/eval_jaxpr/ps,pram->rasm/dot_general | solution.py:70
  412.3 10.7 %bitcast_add_fusion.5 = f32[4,128,32,64]{1,2,3,0:T(8,128)} fusion(f32[4,128,32,64]{1,2,3,0:T(8,128)} %get-tuple-element.318, f32[4,128,64,32]{1,3,2,0:T(8,128)} %fusion.107, f32[16,4,128,64]{2,3,1,0:T(8,128)} %convolution_bitcast_fusion.5, pred[]{:T(512)S(6)} %compare.7, f32[16]{0:T(128)S(1)} %fusion.108, s32[16]{0:T(128)S(1)} %get-tuple-element.309), kind=kOutput, calls=%fused_computation.44.clone.1 | convolution fusion | flops 204473344 | bytes 14680193 | tf_op jit(solution)/shard_map/while/body/eval_jaxpr/ps,pram->rasm/dot_general | solution.py:70
  433.5 10.7 %bitcast_add_fusion.5 = f32[4,128,32,64]{1,2,3,0:T(8,128)} fusion(f32[4,128,32,64]{1,2,3,0:T(8,128)} %get-tuple-element.318, f32[4,128,64,32]{1,3,2,0:T(8,128)} %fusion.107, f32[16,4,128,64]{2,3,1,0:T(8,128)} %convolution_bitcast_fusion.5, pred[]{:T(512)S(6)} %compare.7, f32[16]{0:T(128)S(1)} %fusion.108, s32[16]{0:T(128)S(1)} %get-tuple-element.309), kind=kOutput, calls=%fused_computation.44.clone.1 | convolution fusion | flops 204473344 | bytes 14680193 | tf_op jit(solution)/shard_map/while/body/eval_jaxpr/ps,pram->rasm/dot_general | solution.py:70
  449.8 8.7 %convolution_convert_fusion.3 = bf16[512,2048]{1,0:T(8,128)(2,1)S(1)} fusion(bf16[2048,2048]{1,0:T(8,128)(2,1)} %all-gather.6.cloned.1.call-done, bf16[256,8,4,128]{3,2,1,0:T(4,128)(2,1)} %bitcast.194), kind=kOutput, calls=%fused_computation.86 | convolution fusion | flops 4296015872 | bytes 12582912 | tf_op jit(solution)/shard_map/dot_general | solution.py:78
  (236 shorter events, 191.5 us)
Async XLA Ops:
  6.5 4.8 %copy-start = (bf16[1,4096,256]{2,1,0:T(8,128)(2,1)S(1)}, bf16[1,4096,256]{2,1,0:T(8,128)(2,1)}, u32[]{:S(2)}) copy-start(bf16[1,4096,256]{2,1,0:T(8,128)(2,1)} %param.12) | copy-start | bytes 6291460
  6.5 69.6 %all-gather.8.cloned.1.call-start = ((), (), s32[]{:S(2)}) async-start(), calls=%async_computation.3 | async-start | bytes 4456448 | tf_op jit(solution)/shard_map/all_gather | solution.py:26
  25.1 238.3 %all-gather.10.cloned.1.call-start = ((), (), s32[]{:S(2)}) async-start(), calls=%async_computation.4 | async-start | bytes 4456448 | tf_op jit(solution)/shard_map/all_gather | solution.py:26
  25.3 12.2 %copy-start.4 = (s32[128,2]{0,1:T(2,128)S(1)}, s32[128,2]{0,1:T(2,128)}, u32[]{:S(2)}) copy-start(s32[128,2]{0,1:T(2,128)} %param.13) | copy-start | bytes 3076
  36.7 413.1 %all-gather.6.cloned.1.call-start = ((), (), s32[]{:S(2)}) async-start(), calls=%async_computation.2 | async-start | bytes 8912896 | tf_op jit(solution)/shard_map/all_gather | solution.py:80
  37.8 51.1 %copy-start.2 = (bf16[2048,128]{1,0:T(8,128)(2,1)S(1)}, bf16[2048,128]{1,0:T(8,128)(2,1)}, u32[]{:S(2)}) copy-start(bf16[2048,128]{1,0:T(8,128)(2,1)} %param.16) | copy-start | bytes 1572868
  449.8 8.7 %copy-start.3 = (bf16[4,128,32,64]{1,0,3,2:T(4,128)(2,1)S(1)}, bf16[4,128,32,64]{1,0,3,2:T(4,128)(2,1)}, u32[]{:S(2)}) copy-start(bf16[4,128,32,64]{1,0,3,2:T(4,128)(2,1)} %copy.32) | copy-start | bytes 6291460
  449.8 8.8 %copy-start.5 = (bf16[2048,2048]{1,0:T(8,128)(2,1)S(1)}, bf16[2048,2048]{1,0:T(8,128)(2,1)}, u32[]{:S(2)}) copy-start(bf16[2048,2048]{1,0:T(8,128)(2,1)} %all-gather.6.cloned.1.call-done) | copy-start | bytes 25165828
  463.4 2.4 copy-start.1
Sparse Core Ops, SparseCore 0:
  25.2 50.9 all-gather.7
  78.3 51.1 all-gather.9
  131.6 77.9 all-gather.5
where the time goes:
time: 475 us; the launch traced here: 472 us
  matrix products  300 us (63%)
  local copies, waits for them, and re-layouts  84.5 us (18%)
  waiting for transfers between devices  39.1 us (8%)
  blocking collectives  23.4 us (5%)
  between operations  14.6 us (3%)
  other arithmetic  9.74 us (2%)
    dot_general x16, matrix products, accumulate(): jnp.einsum('ps,pram->rasm', place_one, term_two, precision=lax.Precision....  169 us
    dot_general x16, matrix products, accumulate(): jnp.einsum('ps,pran->rasn', place_two, term_one, precision=lax.Precision....  78.3 us
    all_gather x2, waiting for transfers between devices, remap_pairs(): return lax.all_gather(owned, 'mo', axis=1, tiled=True)  38.4 us
    dynamic_slice x32, local copies, waits for them, and re-layouts, bra_transform(): left_terms = lax.scan(accumulate, start_terms, (grouped, grouped_pairs))[0]  31.6 us
    dot_general x16, matrix products, accumulate(): jnp.einsum('prmn,pna->pram', block_vals, coef_two, preferred_element_type...  29.5 us
    another operation x2, local copies, waits for them, and re-layouts, bra_transform(): grouped = gathered.reshape(block_count // 16, 16, pair_rows, SH, SH)  25.4 us
    all_to_all x2, blocking collectives, remap_pairs(): lax.all_to_all(stacked, 'ao', split_axis=2, concat_axis=1, tiled=True)  23.4 us
    dot_general x2, matrix products, bra_transform(): jnp.dot(left_rounded, lax.all_gather(coef_act, 'mo', axis=1, tiled=True),...  13.6 us
  transfers between devices with their start and end apart: 3, of which 1 were waited for; matrix products, arithmetic and copies ran while one was open for 79% of the time, Pallas kernels for 0%

commit v1 on v0

v1 whole, which is shorter than its diff:
```python
import functools

import jax
import jax.numpy as jnp
from jax import lax
from jax.experimental import pallas as pl
from jax.experimental.pallas import tpu as pltpu
from jax.sharding import PartitionSpec as P

SH = 64
NSH = 32
NAO = 2048
ACT = 2048
KL = 16
KS = 16
NI = 4
NJ = 8
PANEL = 128
ROWS = NI * PANEL
AXES = ("ao", "mo")
OFFSETS = (0, 3, 1, 2)


def device_pairs(move):
    pairs = []
    for z in range(4):
        for c in range(2):
            for x in range(4):
                for y in range(4):
                    x2, y2, z2, c2 = move(x, y, z, c)
                    source = (z * 2 + c) * 16 + x * 4 + y
                    target = ((z2 % 4) * 2 + c2) * 16 + (x2 % 4) * 4 + y2 % 4
                    pairs.append((source, target))
    return pairs


def plane_pairs(step, phase):
    return device_pairs(
        lambda x, y, z, c: (x + step, y, z, c) if c == phase else (x, y + step, z, c)
    )


def z_pairs(step):
    return device_pairs(lambda x, y, z, c: (x, y, z + step, c))


def send(value, pairs):
    return lax.ppermute(value, AXES, pairs)


def ring(value, pairs_up, pairs_down, axis):
    half = value.shape[axis] // 2
    from_left = send(value, pairs_up)
    from_right = send(value, pairs_down)
    far_first = send(lax.slice_in_dim(from_left, 0, half, axis=axis), pairs_up)
    far_second = send(lax.slice_in_dim(from_right, half, 2 * half, axis=axis), pairs_down)
    return value, from_left, from_right, far_first, far_second


def plane_ring(value, phase, axis):
    return ring(value, plane_pairs(1, phase), plane_pairs(-1, phase), axis)


def gather_coefs(chunk):
    own, left, right, far_a, far_b = plane_ring(chunk[None], 0, 1)
    row = jnp.concatenate([own, left, right, jnp.concatenate([far_a, far_b], axis=1)], axis=0)
    whole = jnp.concatenate(plane_ring(row, 1, 0), axis=0)
    column = ring(whole, z_pairs(1), z_pairs(-1), 0)
    swap = device_pairs(lambda x, y, z, c: (x, y, z, 1 - c))
    return list(column), [send(piece, swap) for piece in column]


def slab_kernel(slab, n_in, *refs):
    pairs_ref, place_ref = refs[:2]
    halves = refs[2:7]
    coefs_own = refs[7:12]
    coefs_other = refs[12:17]
    lhs_hbm = refs[17]
    (out_ref, blocks, coefs, lhs, acc_one, acc_two, left, staged, sem_blocks, sem_coefs,
     sem_lhs, sem_out) = refs[n_in:]
    x = place_ref[0]
    y = place_ref[1]
    z = place_ref[2]
    core = place_ref[3]

    def source(slot, which_core):
        first = jnp.where(which_core == 0, x, y)
        second = jnp.where(which_core == 0, y, x)
        inner = slot % 4
        outer = slot // 4
        if isinstance(slot, int):
            first = (first + OFFSETS[inner]) & 3
            second = (second + OFFSETS[outer]) & 3
        else:
            first = (first + jnp.where(inner == 0, 0, jnp.where(inner == 3, 2, (inner * 2 + 1) & 3))) & 3
            second = (second + jnp.where(outer == 0, 0, jnp.where(outer == 3, 2, (outer * 2 + 1) & 3))) & 3
        return jnp.where(which_core == 0, first * 4 + second, second * 4 + first)

    copy_lhs = pltpu.make_async_copy(lhs_hbm, lhs, sem_lhs)
    copy_lhs.start()
    starts = (0, 32, 64, 96, 112, 128)
    copies = [
        pltpu.make_async_copy(
            halves[i], blocks.at[pl.ds(starts[i], starts[i + 1] - starts[i])], sem_blocks.at[i]
        )
        for i in range(5)
    ]
    for copy in copies:
        copy.start()
    for pieces, which_core in ((coefs_own, core), (coefs_other, 1 - core)):
        for piece, offset, slots, base in (
            (pieces[0], 0, 16, 0), (pieces[1], 3, 16, 0), (pieces[2], 1, 16, 0),
            (pieces[3], 2, 8, 0), (pieces[4], 2, 8, 8),
        ):
            row = pl.multiple_of((((z + offset) & 3) * 2 + which_core) * 256, 256)
            for s in range(slots):
                pltpu.make_async_copy(
                    piece.at[s],
                    coefs.at[source(base + s, which_core), pl.ds(row, 256)],
                    sem_coefs,
                ).start()

    @pl.loop(0, NSH)
    def _(shell):
        acc_one[shell] = jnp.zeros(acc_one.shape[1:], jnp.float32)
        acc_two[shell] = jnp.zeros(acc_two.shape[1:], jnp.float32)

    copy_lhs.wait()

    def add_group(group):
        came_from = source(group, core)
        for i in range(8):
            p = i * 16 + came_from
            one = pairs_ref[2 * p]
            two = pairs_ref[2 * p + 1]
            block = blocks[group * 8 + i]
            term_one = jnp.dot(
                lhs[one, 0:PANEL, 0:SH], block, preferred_element_type=jnp.float32
            )
            stacked = jnp.concatenate([block[:, 0:128], block[:, 128:256]], axis=0)
            term_two = lax.dot_general(
                lhs[two], stacked, (((1,), (1,)), ((), ())), preferred_element_type=jnp.float32
            )
            acc_one[two] += term_one
            spare = jnp.where(one == two, NSH, one)
            acc_two[spare] += term_two

    for i in range(5):
        copies[i].wait()

        @pl.loop(starts[i] // 8, starts[i + 1] // 8)
        def _(group):
            add_group(group)

    low = lax.broadcasted_iota(jnp.int32, (PANEL, 128), 1) < SH

    @pl.loop(0, NSH // 2)
    def _(t):
        for rp in range(2):
            one_a = acc_one[2 * t, :, rp * 128:rp * 128 + 128]
            one_b = acc_one[2 * t + 1, :, rp * 128:rp * 128 + 128]
            for r01 in range(2):
                two_a = acc_two[2 * t, r01 * PANEL:(r01 + 1) * PANEL, :]
                two_b = acc_two[2 * t + 1, r01 * PANEL:(r01 + 1) * PANEL, :]
                if r01 == 0:
                    part = jnp.where(low, one_a, pltpu.roll(one_b, SH, 1))
                else:
                    part = jnp.where(low, pltpu.roll(one_a, SH, 1), one_b)
                if rp == 0:
                    part += jnp.where(low, two_a, pltpu.roll(two_b, SH, 1))
                else:
                    part += jnp.where(low, pltpu.roll(two_a, SH, 1), two_b)
                r = rp * 2 + r01
                left[r * PANEL:(r + 1) * PANEL, pl.ds(pl.multiple_of(t * 128, 128), 128)] = (
                    part.astype(jnp.bfloat16)
                )

    pltpu.make_async_copy(coefs, coefs, sem_coefs).wait()

    def out_copy(n, slot):
        return pltpu.make_async_copy(
            staged.at[slot],
            out_ref.at[slab, :, pl.ds(pl.multiple_of(n * 256, 256), 256)],
            sem_out.at[slot],
        )

    @pl.loop(0, ACT // 256)
    def _(n):
        slot = n % 2

        @pl.when(n >= 2)
        def _():
            out_copy(n - 2, slot).wait()

        rhs = jnp.concatenate([coefs[2 * n], coefs[2 * n + 1]], axis=1)
        for h in range(2):
            product = jnp.dot(
                left[h * 256:(h + 1) * 256, :], rhs, preferred_element_type=jnp.float32
            )
            staged[slot, h * 256:(h + 1) * 256, :] = product.astype(jnp.bfloat16)
        out_copy(n, slot).start()

    out_copy(ACT // 256 - 2, 0).wait()
    out_copy(ACT // 256 - 1, 1).wait()


def finish_slab(slab, pairs, place, halves, coefs_own, coefs_other, lhs, previous):
    operands = [pairs, place, *halves, *coefs_own, *coefs_other, lhs]
    specs = [pl.BlockSpec(memory_space=pltpu.SMEM)] * 2
    specs += [pl.BlockSpec(memory_space=pl.ANY)] * (len(operands) - 2)
    aliases = {}
    if previous is not None:
        aliases = {len(operands): 0}
        operands.append(previous)
        specs.append(pl.BlockSpec(memory_space=pl.ANY))
    return pl.pallas_call(
        functools.partial(slab_kernel, slab, len(operands)),
        out_shape=jax.ShapeDtypeStruct((2, ROWS, ACT), jnp.bfloat16),
        in_specs=specs,
        out_specs=pl.BlockSpec(memory_space=pl.ANY),
        scratch_shapes=[
            pltpu.VMEM((128, SH, NI * SH), jnp.bfloat16),
            pltpu.VMEM((16, NAO, PANEL), jnp.bfloat16),
            pltpu.VMEM((NSH, 2 * PANEL, 2 * SH), jnp.bfloat16),
            pltpu.VMEM((NSH, PANEL, NI * SH), jnp.float32),
            pltpu.VMEM((NSH + 1, 2 * PANEL, 2 * SH), jnp.float32),
            pltpu.VMEM((ROWS, NAO), jnp.bfloat16),
            pltpu.VMEM((2, ROWS, 256), jnp.bfloat16),
            pltpu.SemaphoreType.DMA((5,)),
            pltpu.SemaphoreType.DMA,
            pltpu.SemaphoreType.DMA,
            pltpu.SemaphoreType.DMA((2,)),
        ],
        input_output_aliases=aliases,
        compiler_params=pltpu.CompilerParams(vmem_limit_bytes=48 << 20),
        cost_estimate=pl.CostEstimate(
            flops=9_000_000_000, bytes_accessed=18_000_000, transcendentals=0
        ),
        name="finish_slab",
    )(*operands)


def body(pair_ints, shell_pairs, occ_lam, occ_sig, coef_act, slabs):
    ao_index = lax.axis_index("ao")
    mo_index = lax.axis_index("mo")
    place = jnp.stack([mo_index // 4, mo_index % 4, ao_index // 2, ao_index % 2]).astype(jnp.int32)
    chunk = lax.dynamic_slice_in_dim(coef_act, ao_index * 256, 256, 0)
    coefs_own, coefs_other = gather_coefs(chunk)

    lam = occ_lam.astype(jnp.float32).reshape(KL, -1, NI)
    lam = jnp.take(lam, slabs, axis=1)
    pair_coef = occ_sig.astype(jnp.float32).T[:, None, None, None, :] * lam.transpose(1, 2, 0)[None, :, :, :, None]
    pair_coef = pair_coef.reshape(NJ * 2 * NI, KL * KS).astype(jnp.bfloat16)
    half = jnp.dot(pair_coef, pair_ints[0].T, preferred_element_type=jnp.float32).astype(jnp.bfloat16)
    half = half.reshape(NJ, 2, NI, SH, SH).transpose(0, 1, 3, 2, 4).reshape(NJ, 2, SH, NI * SH)
    owned = lax.all_to_all(half, "ao", split_axis=0, concat_axis=0, tiled=True)
    near = plane_ring(owned, 0, 0)
    rows = [jnp.concatenate([piece[:, k] for piece in near], axis=0) for k in range(2)]

    coef_t = coef_act.T.reshape(PANEL, NSH, SH).transpose(1, 0, 2)
    nothing = jnp.zeros_like(coef_t)
    lhs = jnp.concatenate(
        [jnp.concatenate([coef_t, nothing], axis=2), jnp.concatenate([nothing, coef_t], axis=2)], axis=1
    )
    pairs = shell_pairs.reshape(-1)
    out = None
    for k in range(2):
        halves = plane_ring(rows[k], 1, 0)
        out = finish_slab(k, pairs, place, halves, coefs_own, coefs_other, lhs, out)
    return out.reshape(2, 1, NI, PANEL, ACT)


def solution(mesh):
    return jax.shard_map(
        body,
        mesh=mesh,
        in_specs=(P(("ao", "mo"), None, None), P(), P(), P(), P(None, "mo"), P()),
        out_specs=P(None, "ao", None, "mo", None),
        check_vma=False,
    )
```

time: 475 us -> 157 us (0.33)
  matrix products: 300 us -> 1.55 us
  local copies, waits for them, and re-layouts: 84.5 us -> 24.8 us
  starting transfers between devices: 0.09 us -> 40.7 us
  Pallas kernels: 0 us -> 39.6 us
  blocking collectives: 23.4 us -> 0 us
  between operations: 14.6 us -> 0.57 us
    dot_general x52 -> x1, matrix products: 292 us -> 1.55 us  [body(): jnp.dot(pair_coef, pair_ints[0].T, preferred_element_type=jnp.float32)]
    ppermute x0 -> x29, waiting for transfers between devices: none -> 43.4 us  [send(): return lax.ppermute(value, AXES, pairs)]
    pallas_call x0 -> x2, Pallas kernels: none -> 39.6 us  [finish_slab(): pl.pallas_call(functools.partial(slab_kernel, slab, len(operands)), out_s...]
    all_gather x3 -> x0, waiting for transfers between devices: 38.4 us -> none  [the longest x2 38.4 us: remap_pairs(): return lax.all_gather(owned, 'mo', axis=1, tiled=True)]
    ppermute x0 -> x29, starting transfers between devices: none -> 35.4 us  [send(): return lax.ppermute(value, AXES, pairs)]
    dynamic_slice x32 -> x0, local copies, waits for them, and re-layouts: 31.6 us -> none  [bra_transform(): left_terms = lax.scan(accumulate, start_terms, (grouped, grouped_pairs))[0]]
    another operation x5 -> x0, local copies, waits for them, and re-layouts: 25.7 us -> none  [the longest x2 25.4 us: bra_transform(): grouped = gathered.reshape(block_count // 16, 16, pair_rows, SH, SH)]
    all_to_all x2 -> x0, blocking collectives: 23.4 us -> none  [remap_pairs(): lax.all_to_all(stacked, 'ao', split_axis=2, concat_axis=1, tiled=True)]
  transfers between devices with their start and end apart: 3 -> 30, of which waited for: 1 -> 10; matrix products, arithmetic and copies ran while one was open for 79% -> 18% of each run, Pallas kernels for 0% -> 13%
where the time goes in v1:
time: 157 us
  waiting for transfers between devices  43.4 us (28%)
  starting transfers between devices  40.7 us (26%)
  Pallas kernels  39.6 us (25%)
  local copies, waits for them, and re-layouts  24.8 us (16%)
  other arithmetic  6 us (4%)
    ppermute x29, waiting for transfers between devices, send(): return lax.ppermute(value, AXES, pairs)  43.4 us
    pallas_call x2, Pallas kernels, finish_slab(): pl.pallas_call(functools.partial(slab_kernel, slab, len(operands)), out_s...  39.6 us
    ppermute x29, starting transfers between devices, send(): return lax.ppermute(value, AXES, pairs)  35.4 us
    unnamed x42, local copies, waits for them, and re-layouts  9.13 us
    all_to_all x1, starting transfers between devices, body(): owned = lax.all_to_all(half, 'ao', split_axis=0, concat_axis=0, tiled=True)  5.32 us
    reshape x2, local copies, waits for them, and re-layouts, body(): half.reshape(NJ, 2, NI, SH, SH).transpose(0, 1, 3, 2, 4)  4.79 us
    concatenate x1, other arithmetic, body(): jnp.concatenate([jnp.concatenate([coef_t, nothing], axis=2), jnp.concaten...  3.69 us
  transfers between devices with their start and end apart: 30, of which 10 were waited for; matrix products, arithmetic and copies ran while one was open for 18% of the time, Pallas kernels for 13%

profile of v1, /device:TPU:0, one launch (start us, length us, event | category | flops | bytes accessed | tf_op | source)
XLA Modules:
  0.0 156.5 jit_solution(490991658051421815)
XLA Ops:
  1.6 2.8 %collective-permute-start.9 = (bf16[1,256,128]{2,1,0:T(8,128)(2,1)S(1)}, bf16[1,256,128]{2,1,0:T(8,128)(2,1)S(1)}, u32[]{:S(2)}, u32[]{:S(2)}) collective-permute-start(bf16[1,256,128]{2,1,0:T(8,128)(2,1)S(1)} %get-tuple-element.6), channel_id=1, source_target_pairs={{0,12},{1,13},{2,14},{3,15},{4,0},{5,1},{6,2},{7,3},{8,4},{9,5},{1... | collective-permute-start | bytes 196616 | tf_op jit(solution)/shard_map/ppermute | solution.py:48
  9.9 2.1 %reshape.44 = bf16[8,2,4,64,64]{4,3,2,1,0:T(8,128)(2,1)S(1)} reshape(bf16[64,4096]{1,0:T(8,128)(2,1)} %convolution_convert_fusion) | data formatting | bytes 1048576 | tf_op jit(solution)/shard_map/reshape | solution.py:255
  13.8 2.7 %reshape.45 = bf16[8,2,64,256]{3,2,1,0:T(8,128)(2,1)} reshape(bf16[8,2,64,4,64]{4,3,2,1,0:T(4,128)(2,1)} %copy.18) | data formatting | bytes 1048576 | tf_op jit(solution)/shard_map/reshape | solution.py:255
  16.5 5.3 %all-to-all-start = ((bf16[8,2,64,256]{3,2,1,0:T(8,128)(2,1)}), bf16[8,2,64,256]{3,2,1,0:T(8,128)(2,1)S(1)}, u32[]{:S(2)}, u32[]{:S(2)}) async-start(bf16[8,2,64,256]{3,2,1,0:T(8,128)(2,1)} %reshape.45), calls=%async_computation | async-start | bytes 1048576 | tf_op jit(solution)/shard_map/all_to_all | solution.py:256
  21.8 3.3 %collective-permute-start.11 = (bf16[1,128,128]{2,1,0:T(8,128)(2,1)S(1)}, bf16[1,128,128]{2,1,0:T(8,128)(2,1)S(1)}, u32[]{:S(2)}, u32[]{:S(2)}) collective-permute-start(bf16[1,128,128]{2,1,0:T(8,128)(2,1)S(1)} %slice.100), channel_id=1, source_target_pairs={{0,12},{1,13},{2,14},{3,15},{4,0},{5,1},{6,2},{7,3},{8,4},{9,5},{1... | collective-permute-start | bytes 98312 | tf_op jit(solution)/shard_map/ppermute | solution.py:48
  26.7 3.5 %collective-permute-done.10 = bf16[1,128,128]{2,1,0:T(8,128)(2,1)S(1)} collective-permute-done((bf16[1,128,128]{2,1,0:T(8,128)(2,1)S(1)}, bf16[1,128,128]{2,1,0:T(8,128)(2,1)S(1)}, u32[]{:S(2)}, u32[]{:S(2)}) %collective-permute-start.10) | collective-permute-done | bytes 32800 | tf_op jit(solution)/shard_map/ppermute | solution.py:48
  30.3 3.1 %collective-permute-start.13 = (bf16[4,256,128]{2,1,0:T(8,128)(2,1)S(1)}, bf16[4,256,128]{2,1,0:T(8,128)(2,1)S(1)}, u32[]{:S(2)}, u32[]{:S(2)}) collective-permute-start(bf16[4,256,128]{2,1,0:T(8,128)(2,1)S(1)} %maximum_maximum_fusion), channel_id=1, source_target_pairs={{0,3},{1,0},{2,1},{3,2},{4,7},{5,4},{6,5},{7,6},{8,11},{9,8},{10,9... | collective-permute-start | bytes 786440 | tf_op jit(solution)/shard_map/ppermute | solution.py:48
  35.2 2.0 %collective-permute-done.13 = bf16[4,256,128]{2,1,0:T(8,128)(2,1)S(1)} collective-permute-done((bf16[4,256,128]{2,1,0:T(8,128)(2,1)S(1)}, bf16[4,256,128]{2,1,0:T(8,128)(2,1)S(1)}, u32[]{:S(2)}, u32[]{:S(2)}) %collective-permute-start.13) | collective-permute-done | bytes 262176 | tf_op jit(solution)/shard_map/ppermute | solution.py:48
  37.3 3.8 %collective-permute-start.15 = (bf16[2,256,128]{2,1,0:T(8,128)(2,1)S(1)}, bf16[2,256,128]{2,1,0:T(8,128)(2,1)S(1)}, u32[]{:S(2)}, u32[]{:S(2)}) collective-permute-start(bf16[2,256,128]{2,1,0:T(8,128)(2,1)S(1)} %slice.102), channel_id=1, source_target_pairs={{0,3},{1,0},{2,1},{3,2},{4,7},{5,4},{6,5},{7,6},{8,11},{9,8},{10,9... | collective-permute-start | bytes 393224 | tf_op jit(solution)/shard_map/ppermute | solution.py:48
  42.0 3.2 %collective-permute-start.1 = (bf16[8,2,64,256]{3,2,0,1:T(8,128)(2,1)S(1)}, bf16[8,2,64,256]{3,2,0,1:T(8,128)(2,1)S(1)}, u32[]{:S(2)}, u32[]{:S(2)}) collective-permute-start(bf16[8,2,64,256]{3,2,0,1:T(8,128)(2,1)S(1)} %copy.19), channel_id=1, source_target_pairs={{0,12},{1,13},{2,14},{3,15},{4,0},{5,1},{6,2},{7,3},{8,4},{9,5},{1... | collective-permute-start | bytes 1572872 | tf_op jit(solution)/shard_map/ppermute | solution.py:48
  45.9 2.8 %collective-permute-done.14 = bf16[2,256,128]{2,1,0:T(8,128)(2,1)S(1)} collective-permute-done((bf16[2,256,128]{2,1,0:T(8,128)(2,1)S(1)}, bf16[2,256,128]{2,1,0:T(8,128)(2,1)S(1)}, u32[]{:S(2)}, u32[]{:S(2)}) %collective-permute-start.14) | collective-permute-done | bytes 131104 | tf_op jit(solution)/shard_map/ppermute | solution.py:48
  50.1 3.2 %collective-permute-start.17 = (bf16[16,256,128]{2,1,0:T(8,128)(2,1)}, bf16[16,256,128]{2,1,0:T(8,128)(2,1)}, u32[]{:S(2)}, u32[]{:S(2)}) collective-permute-start(bf16[16,256,128]{2,1,0:T(8,128)(2,1)} %constant_dynamic-update-slice_fusion.refs_7_), channel_id=1, source_target_pairs={{0,96},{1,97},{2,98},{3,99},{4,100},{5,101},{6,102},{7,103},{8,104... | collective-permute-start | bytes 3145736 | tf_op jit(solution)/shard_map/ppermute | solution.py:48
  53.7 3.3 %collective-permute-start.3 = (bf16[4,2,64,256]{3,2,0,1:T(8,128)(2,1)S(1)}, bf16[4,2,64,256]{3,2,0,1:T(8,128)(2,1)S(1)}, u32[]{:S(2)}, u32[]{:S(2)}) collective-permute-start(bf16[4,2,64,256]{3,2,0,1:T(8,128)(2,1)S(1)} %slice.95), channel_id=1, source_target_pairs={{0,12},{1,13},{2,14},{3,15},{4,0},{5,1},{6,2},{7,3},{8,4},{9,5},{1... | collective-permute-start | bytes 786440 | tf_op jit(solution)/shard_map/ppermute | solution.py:48
  57.1 4.2 %collective-permute-done.2 = bf16[4,2,64,256]{3,2,0,1:T(8,128)(2,1)S(1)} collective-permute-done((bf16[4,2,64,256]{3,2,0,1:T(8,128)(2,1)S(1)}, bf16[4,2,64,256]{3,2,0,1:T(8,128)(2,1)S(1)}, u32[]{:S(2)}, u32[]{:S(2)}) %collective-permute-start.2) | collective-permute-done | bytes 262176 | tf_op jit(solution)/shard_map/ppermute | solution.py:48
  61.4 2.1 %collective-permute-start.26 = (bf16[32,64,256]{2,1,0:T(8,128)(2,1)S(1)}, bf16[32,64,256]{2,1,0:T(8,128)(2,1)S(1)}, u32[]{:S(2)}, u32[]{:S(2)}) collective-permute-start(bf16[32,64,256]{2,1,0:T(8,128)(2,1)S(1)} %get-tuple-element.13.refs_2_), channel_id=1, source_target_pairs={{0,3},{1,0},{2,1},{3,2},{4,7},{5,4},{6,5},{7,6},{8,11},{9,8},{10,9... | collective-permute-start | bytes 3145736 | tf_op jit(solution)/shard_map/ppermute | solution.py:48
  63.4 9.1 %collective-permute-done.17.refs_9_ = bf16[16,256,128]{2,1,0:T(8,128)(2,1)} collective-permute-done((bf16[16,256,128]{2,1,0:T(8,128)(2,1)}, bf16[16,256,128]{2,1,0:T(8,128)(2,1)}, u32[]{:S(2)}, u32[]{:S(2)}) %collective-permute-start.17) | collective-permute-done | bytes 1048608 | tf_op jit(solution)/shard_map/ppermute | solution.py:48
  73.6 3.3 %collective-permute-start.19 = (bf16[8,256,128]{2,1,0:T(8,128)(2,1)S(1)}, bf16[8,256,128]{2,1,0:T(8,128)(2,1)S(1)}, u32[]{:S(2)}, u32[]{:S(2)}) collective-permute-start(bf16[8,256,128]{2,1,0:T(8,128)(2,1)S(1)} %slice.104), channel_id=1, source_target_pairs={{0,96},{1,97},{2,98},{3,99},{4,100},{5,101},{6,102},{7,103},{8,104... | collective-permute-start | bytes 1572872 | tf_op jit(solution)/shard_map/ppermute | solution.py:48
  76.9 3.7 %collective-permute-done.16.refs_8_ = bf16[16,256,128]{2,1,0:T(8,128)(2,1)} collective-permute-done((bf16[16,256,128]{2,1,0:T(8,128)(2,1)}, bf16[16,256,128]{2,1,0:T(8,128)(2,1)}, u32[]{:S(2)}, u32[]{:S(2)}) %collective-permute-start.16) | collective-permute-done | bytes 1048608 | tf_op jit(solution)/shard_map/ppermute | solution.py:48
  84.8 11.7 %collective-permute-done.18.refs_10_ = bf16[8,256,128]{2,1,0:T(8,128)(2,1)} collective-permute-done((bf16[8,256,128]{2,1,0:T(8,128)(2,1)S(1)}, bf16[8,256,128]{2,1,0:T(8,128)(2,1)}, u32[]{:S(2)}, u32[]{:S(2)}) %collective-permute-start.18) | collective-permute-done | bytes 524320 | tf_op jit(solution)/shard_map/ppermute | solution.py:48
  99.4 4.9 %collective-permute-done.4.refs_3_ = bf16[32,64,256]{2,1,0:T(8,128)(2,1)} collective-permute-done((bf16[32,64,256]{2,1,0:T(8,128)(2,1)S(1)}, bf16[32,64,256]{2,1,0:T(8,128)(2,1)}, u32[]{:S(2)}, u32[]{:S(2)}) %collective-permute-start.4) | collective-permute-done | bytes 1048608 | tf_op jit(solution)/shard_map/ppermute | solution.py:48
  107.3 2.4 %copy.22 = bf16[128,32,64]{2,0,1:T(8,128)(2,1)} copy(bf16[128,32,64]{0,2,1:T(8,128)(2,1)} %bitcast.69) | data formatting | bytes 1048576 | tf_op jit(solution)/shard_map/reshape | solution.py:260
  109.8 3.7 %fusion.2.refs_17_ = bf16[32,256,128]{2,1,0:T(8,128)(2,1)} fusion(bf16[32,128,64]{2,1,0:T(8,128)(2,1)} %bitcast.67), kind=kLoop, calls=%fused_computation.6 | loop fusion | flops 8388608 | bytes 2621440 | tf_op jit(solution)/shard_map/concatenate | solution.py:262
  116.8 19.8 %finish_slab.2.refs_18_ = bf16[2,512,2048]{2,1,0:T(8,128)(2,1)} custom-call(s32[256]{0:T(256)S(1)} %reshape.41.refs_0_, s32[4]{0:T(128)S(1)} %pad_add_fusion.refs_1_, bf16[32,64,256]{2,1,0:T(8,128)(2,1)S(1)} %copy-done.2, bf16[32,64,256]{2,1,0:T(8,128)(2,1)S(1)} %collective-permute-done.25.refs_3_, bf16[32,64,256]{2,1,0:T(8,128)(2,1)} %copy-done.9, ...), custom_call_target="tpu_custom_call" | custom-call | flops 8999999488 | bytes 18000000 | tf_op jit(solution)/shard_map/finish_slab/pallas_call | solution.py:216
  136.6 19.8 %finish_slab.3 = bf16[2,512,2048]{2,1,0:T(8,128)(2,1)} custom-call(s32[256]{0:T(256)S(1)} %reshape.41.refs_0_, s32[4]{0:T(128)S(1)} %pad_add_fusion.refs_1_, bf16[32,64,256]{2,1,0:T(8,128)(2,1)S(1)} %copy-done.4, bf16[32,64,256]{2,1,0:T(8,128)(2,1)} %collective-permute-done.4.refs_3_, ...), custom_call_target="tpu_custom_call", output_to_operand_aliasing={{}: (18, {})} | custom-call | flops 8999999488 | bytes 18000000 | tf_op jit(solution)/shard_map/finish_slab/pallas_call | solution.py:216
  (113 shorter events, 30.2 us)
Async XLA Ops:
  1.6 20.2 %collective-permute-start.9 = (bf16[1,256,128]{2,1,0:T(8,128)(2,1)S(1)}, bf16[1,256,128]{2,1,0:T(8,128)(2,1)S(1)}, u32[]{:S(2)}, u32[]{:S(2)}) collective-permute-start(bf16[1,256,128]{2,1,0:T(8,128)(2,1)S(1)} %get-tuple-element.6), channel_id=1, source_target_pairs={{0,12},{1,13},{2,14},{3,15},{4,0},{5,1},{6,2},{7,3},{8,4},{9,5},{1... | collective-permute-start | bytes 196616 | tf_op jit(solution)/shard_map/ppermute | solution.py:48
  4.5 20.6 %collective-permute-start.8 = (bf16[1,256,128]{2,1,0:T(8,128)(2,1)S(1)}, bf16[1,256,128]{2,1,0:T(8,128)(2,1)S(1)}, u32[]{:S(2)}, u32[]{:S(2)}) collective-permute-start(bf16[1,256,128]{2,1,0:T(8,128)(2,1)S(1)} %get-tuple-element.6), channel_id=1, source_target_pairs={{0,4},{1,5},{2,6},{3,7},{4,8},{5,9},{6,10},{7,11},{8,12},{9,13},{1... | collective-permute-start | bytes 196616 | tf_op jit(solution)/shard_map/ppermute | solution.py:48
  16.5 25.4 %all-to-all-start = ((bf16[8,2,64,256]{3,2,1,0:T(8,128)(2,1)}), bf16[8,2,64,256]{3,2,1,0:T(8,128)(2,1)S(1)}, u32[]{:S(2)}, u32[]{:S(2)}) async-start(bf16[8,2,64,256]{3,2,1,0:T(8,128)(2,1)} %reshape.45), calls=%async_computation | async-start | bytes 1048576 | tf_op jit(solution)/shard_map/all_to_all | solution.py:256
  33.4 7.7 %collective-permute-start.12 = (bf16[4,256,128]{2,1,0:T(8,128)(2,1)S(1)}, bf16[4,256,128]{2,1,0:T(8,128)(2,1)S(1)}, u32[]{:S(2)}, u32[]{:S(2)}) collective-permute-start(bf16[4,256,128]{2,1,0:T(8,128)(2,1)S(1)} %maximum_maximum_fusion), channel_id=1, source_target_pairs={{0,1},{1,2},{2,3},{3,0},{4,5},{5,6},{6,7},{7,4},{8,9},{9,10},{10,1... | collective-permute-start | bytes 786440 | tf_op jit(solution)/shard_map/ppermute | solution.py:48
  37.3 12.2 %collective-permute-start.15 = (bf16[2,256,128]{2,1,0:T(8,128)(2,1)S(1)}, bf16[2,256,128]{2,1,0:T(8,128)(2,1)S(1)}, u32[]{:S(2)}, u32[]{:S(2)}) collective-permute-start(bf16[2,256,128]{2,1,0:T(8,128)(2,1)S(1)} %slice.102), channel_id=1, source_target_pairs={{0,3},{1,0},{2,1},{3,2},{4,7},{5,4},{6,5},{7,6},{8,11},{9,8},{10,9... | collective-permute-start | bytes 393224 | tf_op jit(solution)/shard_map/ppermute | solution.py:48
  41.1 7.7 %collective-permute-start.14 = (bf16[2,256,128]{2,1,0:T(8,128)(2,1)S(1)}, bf16[2,256,128]{2,1,0:T(8,128)(2,1)S(1)}, u32[]{:S(2)}, u32[]{:S(2)}) collective-permute-start(bf16[2,256,128]{2,1,0:T(8,128)(2,1)S(1)} %slice.101), channel_id=1, source_target_pairs={{0,1},{1,2},{2,3},{3,0},{4,5},{5,6},{6,7},{7,4},{8,9},{9,10},{10,1... | collective-permute-start | bytes 393224 | tf_op jit(solution)/shard_map/ppermute | solution.py:48
  41.9 11.7 %collective-permute-start = (bf16[8,2,64,256]{3,2,0,1:T(8,128)(2,1)S(1)}, bf16[8,2,64,256]{3,2,0,1:T(8,128)(2,1)S(1)}, u32[]{:S(2)}, u32[]{:S(2)}) collective-permute-start(bf16[8,2,64,256]{3,2,0,1:T(8,128)(2,1)S(1)} %copy.19), channel_id=1, source_target_pairs={{0,4},{1,5},{2,6},{3,7},{4,8},{5,9},{6,10},{7,11},{8,12},{9,13},{1... | collective-permute-start | bytes 1572872 | tf_op jit(solution)/shard_map/ppermute | solution.py:48
  42.0 11.7 %collective-permute-start.1 = (bf16[8,2,64,256]{3,2,0,1:T(8,128)(2,1)S(1)}, bf16[8,2,64,256]{3,2,0,1:T(8,128)(2,1)S(1)}, u32[]{:S(2)}, u32[]{:S(2)}) collective-permute-start(bf16[8,2,64,256]{3,2,0,1:T(8,128)(2,1)S(1)} %copy.19), channel_id=1, source_target_pairs={{0,12},{1,13},{2,14},{3,15},{4,0},{5,1},{6,2},{7,3},{8,4},{9,5},{1... | collective-permute-start | bytes 1572872 | tf_op jit(solution)/shard_map/ppermute | solution.py:48
  50.1 22.4 %collective-permute-start.17 = (bf16[16,256,128]{2,1,0:T(8,128)(2,1)}, bf16[16,256,128]{2,1,0:T(8,128)(2,1)}, u32[]{:S(2)}, u32[]{:S(2)}) collective-permute-start(bf16[16,256,128]{2,1,0:T(8,128)(2,1)} %constant_dynamic-update-slice_fusion.refs_7_), channel_id=1, source_target_pairs={{0,96},{1,97},{2,98},{3,99},{4,100},{5,101},{6,102},{7,103},{8,104... | collective-permute-start | bytes 3145736 | tf_op jit(solution)/shard_map/ppermute | solution.py:48
  53.4 28.4 %collective-permute-start.20 = (bf16[16,256,128]{2,1,0:T(8,128)(2,1)}, bf16[16,256,128]{2,1,0:T(8,128)(2,1)S(1)}, u32[]{:S(2)}, u32[]{:S(2)}) collective-permute-start(bf16[16,256,128]{2,1,0:T(8,128)(2,1)} %constant_dynamic-update-slice_fusion.refs_7_), channel_id=1, source_target_pairs={{0,16},{1,17},{2,18},{3,19},{4,20},{5,21},{6,22},{7,23},{8,24},{9,... | collective-permute-start | bytes 3145736 | tf_op jit(solution)/shard_map/ppermute | solution.py:48
  53.5 27.1 %collective-permute-start.16 = (bf16[16,256,128]{2,1,0:T(8,128)(2,1)}, bf16[16,256,128]{2,1,0:T(8,128)(2,1)}, u32[]{:S(2)}, u32[]{:S(2)}) collective-permute-start(bf16[16,256,128]{2,1,0:T(8,128)(2,1)} %constant_dynamic-update-slice_fusion.refs_7_), channel_id=1, source_target_pairs={{0,32},{1,33},{2,34},{3,35},{4,36},{5,37},{6,38},{7,39},{8,40},{9,... | collective-permute-start | bytes 3145736 | tf_op jit(solution)/shard_map/ppermute | solution.py:48
  61.4 35.2 %collective-permute-start.26 = (bf16[32,64,256]{2,1,0:T(8,128)(2,1)S(1)}, bf16[32,64,256]{2,1,0:T(8,128)(2,1)S(1)}, u32[]{:S(2)}, u32[]{:S(2)}) collective-permute-start(bf16[32,64,256]{2,1,0:T(8,128)(2,1)S(1)} %get-tuple-element.13.refs_2_), channel_id=1, source_target_pairs={{0,3},{1,0},{2,1},{3,2},{4,7},{5,4},{6,5},{7,6},{8,11},{9,8},{10,9... | collective-permute-start | bytes 3145736 | tf_op jit(solution)/shard_map/ppermute | solution.py:48
  73.6 10.0 %collective-permute-start.19 = (bf16[8,256,128]{2,1,0:T(8,128)(2,1)S(1)}, bf16[8,256,128]{2,1,0:T(8,128)(2,1)S(1)}, u32[]{:S(2)}, u32[]{:S(2)}) collective-permute-start(bf16[8,256,128]{2,1,0:T(8,128)(2,1)S(1)} %slice.104), channel_id=1, source_target_pairs={{0,96},{1,97},{2,98},{3,99},{4,100},{5,101},{6,102},{7,103},{8,104... | collective-permute-start | bytes 1572872 | tf_op jit(solution)/shard_map/ppermute | solution.py:48
  76.9 20.2 %collective-permute-start.25 = (bf16[32,64,256]{2,1,0:T(8,128)(2,1)S(1)}, bf16[32,64,256]{2,1,0:T(8,128)(2,1)S(1)}, u32[]{:S(2)}, u32[]{:S(2)}) collective-permute-start(bf16[32,64,256]{2,1,0:T(8,128)(2,1)S(1)} %get-tuple-element.13.refs_2_), channel_id=1, source_target_pairs={{0,1},{1,2},{2,3},{3,0},{4,5},{5,6},{6,7},{7,4},{8,9},{9,10},{10,1... | collective-permute-start | bytes 3145736 | tf_op jit(solution)/shard_map/ppermute | solution.py:48
  81.7 14.9 %collective-permute-start.18 = (bf16[8,256,128]{2,1,0:T(8,128)(2,1)S(1)}, bf16[8,256,128]{2,1,0:T(8,128)(2,1)}, u32[]{:S(2)}, u32[]{:S(2)}) collective-permute-start(bf16[8,256,128]{2,1,0:T(8,128)(2,1)S(1)} %slice.103), channel_id=1, source_target_pairs={{0,32},{1,33},{2,34},{3,35},{4,36},{5,37},{6,38},{7,39},{8,40},{9,... | collective-permute-start | bytes 1572872 | tf_op jit(solution)/shard_map/ppermute | solution.py:48
  82.8 16.1 %collective-permute-start.5 = (bf16[32,64,256]{2,1,0:T(8,128)(2,1)S(1)}, bf16[32,64,256]{2,1,0:T(8,128)(2,1)S(1)}, u32[]{:S(2)}, u32[]{:S(2)}) collective-permute-start(bf16[32,64,256]{2,1,0:T(8,128)(2,1)S(1)} %get-tuple-element.14.refs_2_), channel_id=1, source_target_pairs={{0,3},{1,0},{2,1},{3,2},{4,7},{5,4},{6,5},{7,6},{8,11},{9,8},{10,9... | collective-permute-start | bytes 3145736 | tf_op jit(solution)/shard_map/ppermute | solution.py:48
  83.6 20.6 %collective-permute-start.4 = (bf16[32,64,256]{2,1,0:T(8,128)(2,1)S(1)}, bf16[32,64,256]{2,1,0:T(8,128)(2,1)}, u32[]{:S(2)}, u32[]{:S(2)}) collective-permute-start(bf16[32,64,256]{2,1,0:T(8,128)(2,1)S(1)} %get-tuple-element.14.refs_2_), channel_id=1, source_target_pairs={{0,1},{1,2},{2,3},{3,0},{4,5},{5,6},{6,7},{7,4},{8,9},{9,10},{10,1... | collective-permute-start | bytes 3145736 | tf_op jit(solution)/shard_map/ppermute | solution.py:48
  96.5 18.1 %collective-permute-start.22 = (bf16[16,256,128]{2,1,0:T(8,128)(2,1)}, bf16[16,256,128]{2,1,0:T(8,128)(2,1)}, u32[]{:S(2)}, u32[]{:S(2)}) collective-permute-start(bf16[16,256,128]{2,1,0:T(8,128)(2,1)} %collective-permute-done.17.refs_9_), channel_id=1, source_target_pairs={{0,16},{1,17},{2,18},{3,19},{4,20},{5,21},{6,22},{7,23},{8,24},{9,... | collective-permute-start | bytes 3145736 | tf_op jit(solution)/shard_map/ppermute | solution.py:48
  96.5 20.2 %collective-permute-start.21 = (bf16[16,256,128]{2,1,0:T(8,128)(2,1)}, bf16[16,256,128]{2,1,0:T(8,128)(2,1)}, u32[]{:S(2)}, u32[]{:S(2)}) collective-permute-start(bf16[16,256,128]{2,1,0:T(8,128)(2,1)} %collective-permute-done.16.refs_8_), channel_id=1, source_target_pairs={{0,16},{1,17},{2,18},{3,19},{4,20},{5,21},{6,22},{7,23},{8,24},{9,... | collective-permute-start | bytes 3145736 | tf_op jit(solution)/shard_map/ppermute | solution.py:48
  98.9 17.1 %collective-permute-start.23 = (bf16[8,256,128]{2,1,0:T(8,128)(2,1)}, bf16[8,256,128]{2,1,0:T(8,128)(2,1)}, u32[]{:S(2)}, u32[]{:S(2)}) collective-permute-start(bf16[8,256,128]{2,1,0:T(8,128)(2,1)} %collective-permute-done.18.refs_10_), channel_id=1, source_target_pairs={{0,16},{1,17},{2,18},{3,19},{4,20},{5,21},{6,22},{7,23},{8,24},{9,... | collective-permute-start | bytes 1572872 | tf_op jit(solution)/shard_map/ppermute | solution.py:48
  104.2 12.5 %collective-permute-start.28 = (bf16[16,64,256]{2,1,0:T(8,128)(2,1)}, bf16[16,64,256]{2,1,0:T(8,128)(2,1)}, u32[]{:S(2)}, u32[]{:S(2)}) collective-permute-start(bf16[16,64,256]{2,1,0:T(8,128)(2,1)} %slice.111), channel_id=1, source_target_pairs={{0,3},{1,0},{2,1},{3,2},{4,7},{5,4},{6,5},{7,6},{8,11},{9,8},{10,9... | collective-permute-start | bytes 1572872 | tf_op jit(solution)/shard_map/ppermute | solution.py:48
  105.1 11.7 %collective-permute-start.27 = (bf16[16,64,256]{2,1,0:T(8,128)(2,1)}, bf16[16,64,256]{2,1,0:T(8,128)(2,1)}, u32[]{:S(2)}, u32[]{:S(2)}) collective-permute-start(bf16[16,64,256]{2,1,0:T(8,128)(2,1)} %slice.110), channel_id=1, source_target_pairs={{0,1},{1,2},{2,3},{3,0},{4,5},{5,6},{6,7},{7,4},{8,9},{9,10},{10,1... | collective-permute-start | bytes 1572872 | tf_op jit(solution)/shard_map/ppermute | solution.py:48
  114.6 21.9 %collective-permute-start.7 = (bf16[16,64,256]{2,1,0:T(8,128)(2,1)S(1)}, bf16[16,64,256]{2,1,0:T(8,128)(2,1)S(1)}, u32[]{:S(2)}, u32[]{:S(2)}) collective-permute-start(bf16[16,64,256]{2,1,0:T(8,128)(2,1)S(1)} %slice.98), channel_id=1, source_target_pairs={{0,3},{1,0},{2,1},{3,2},{4,7},{5,4},{6,5},{7,6},{8,11},{9,8},{10,9... | collective-permute-start | bytes 1572872 | tf_op jit(solution)/shard_map/ppermute | solution.py:48
  115.9 20.6 %collective-permute-start.6 = (bf16[16,64,256]{2,1,0:T(8,128)(2,1)S(1)}, bf16[16,64,256]{2,1,0:T(8,128)(2,1)S(1)}, u32[]{:S(2)}, u32[]{:S(2)}) collective-permute-start(bf16[16,64,256]{2,1,0:T(8,128)(2,1)S(1)} %slice.97), channel_id=1, source_target_pairs={{0,1},{1,2},{2,3},{3,0},{4,5},{5,6},{6,7},{7,4},{8,9},{9,10},{10,1... | collective-permute-start | bytes 1572872 | tf_op jit(solution)/shard_map/ppermute | solution.py:48
  (20 other events, 250.7 us)

commit v2 on v0

v2 whole, which is shorter than its diff:
```python
import functools

import jax
import jax.numpy as jnp
from jax import lax
from jax.experimental import pallas as pl
from jax.experimental.pallas import tpu as pltpu
from jax.sharding import PartitionSpec as P

SH = 64
NSH = 32
NAO = 2048
ACT = 2048
KL = 16
KS = 16
NI = 4
NJ = 8
NOCC = 32
NBLK = 128
PANEL = 128
ROWS = NI * PANEL
VMEM_LIMIT = 60 << 20
AXES = ("ao", "mo")


def device_pairs(move):
    pairs = []
    for z in range(4):
        for c in range(2):
            for x in range(4):
                for y in range(4):
                    x2, y2, z2, c2 = move(x, y, z, c)
                    source = (z * 2 + c) * 16 + x * 4 + y
                    target = ((z2 % 4) * 2 + c2) * 16 + (x2 % 4) * 4 + y2 % 4
                    pairs.append((source, target))
    return pairs


def plane_pairs(step, phase):
    return device_pairs(
        lambda x, y, z, c: (x + step, y, z, c) if c == phase else (x, y + step, z, c)
    )


def z_pairs(step):
    return device_pairs(lambda x, y, z, c: (x, y, z + step, c))


def send(value, pairs):
    return lax.ppermute(value, AXES, pairs)


def after(value, *others):
    return lax.optimization_barrier((value, *others))[0]


def both_ways(value, pairs_up, pairs_down):
    return value, send(value, pairs_up), send(value, pairs_down)


def far_halves(pieces, pairs_up, pairs_down, *others):
    half = pieces[0].shape[0] // 2
    return (
        send(after(pieces[1], *others)[:half], pairs_up),
        send(after(pieces[2], *others)[half:], pairs_down),
    )


def direct(value, phase):
    return [value] + [send(value, plane_pairs(step, phase)) for step in (1, -1, 2)]


def ket_kernel(slabs_ref, lam_ref, sig_ref, ints_hbm, out_ref, ints, wide, sems):
    copies = [
        pltpu.make_async_copy(
            ints_hbm.at[0, pl.ds(n * 1024, 1024)], ints.at[pl.ds(n * 1024, 1024)], sems.at[n]
        )
        for n in range(4)
    ]
    for copy in copies:
        copy.start()
    rows = lax.broadcasted_iota(jnp.int32, (64, NOCC), 0)
    column = lax.broadcasted_iota(jnp.int32, (64, NOCC), 1)
    number = jnp.where((rows & 1) == 0, slabs_ref[0], slabs_ref[1]) * NI + (rows >> 4)
    pick_lam = jnp.where(column == number, 1.0, 0.0).astype(jnp.bfloat16)
    rows = lax.broadcasted_iota(jnp.int32, (64, NJ), 0)
    column = lax.broadcasted_iota(jnp.int32, (64, NJ), 1)
    pick_sig = jnp.where(column == ((rows >> 1) & 7), 1.0, 0.0).astype(jnp.bfloat16)
    line = lax.broadcasted_iota(jnp.int32, (KL, KL * KS), 0)
    word = lax.broadcasted_iota(jnp.int32, (KL, KL * KS), 1)
    spread_lam = jnp.where((word >> 4) == line, 1.0, 0.0).astype(jnp.bfloat16)
    spread_sig = jnp.where((word & 15) == line, 1.0, 0.0).astype(jnp.bfloat16)

    few_lam = lax.dot_general(
        pick_lam, lam_ref[...], (((1,), (1,)), ((), ())), preferred_element_type=jnp.float32
    )
    few_sig = jnp.dot(pick_sig, sig_ref[...], preferred_element_type=jnp.float32)

    def spread_out(few, spread):
        return jnp.dot(few.astype(jnp.bfloat16), spread, preferred_element_type=jnp.float32)

    pair_coef = spread_out(few_lam, spread_lam) * spread_out(few_sig, spread_sig)
    pair_coef = pair_coef.astype(jnp.bfloat16)
    low = lax.broadcasted_iota(jnp.int32, (16, 128), 1) < SH
    for n in range(4):
        copies[n].wait()
        for part in range(2):
            first = n * 1024 + part * 512
            result = lax.dot_general(
                pair_coef, ints[first:first + 512, :], (((1,), (1,)), ((), ())),
                preferred_element_type=jnp.float32,
            )
            for t in range(4):
                mu = first // SH + 2 * t
                for ip in range(2):
                    even = result[ip * 32:ip * 32 + 16, t * 128:t * 128 + 128]
                    odd = result[ip * 32 + 16:ip * 32 + 32, t * 128:t * 128 + 128]
                    lanes = slice(ip * 128, ip * 128 + 128)
                    wide[ip, pl.ds(mu, 16, stride=SH), :] = jnp.where(low, even, pltpu.roll(odd, SH, 1))
                    wide[ip, pl.ds(mu + 1, 16, stride=SH), :] = jnp.where(low, pltpu.roll(even, SH, 1), odd)
    for ip in range(2):
        out_ref[:, ip * 128:ip * 128 + 128] = wide[ip].astype(jnp.bfloat16)


def ket_transform(pair_ints, occ_lam, occ_sig, slabs):
    out = pl.pallas_call(
        ket_kernel,
        out_shape=jax.ShapeDtypeStruct((NJ * 2 * SH, NI * SH), jnp.bfloat16),
        in_specs=[
            pl.BlockSpec(memory_space=pltpu.SMEM),
            pl.BlockSpec(memory_space=pltpu.VMEM),
            pl.BlockSpec(memory_space=pltpu.VMEM),
            pl.BlockSpec(memory_space=pltpu.HBM),
        ],
        out_specs=pl.BlockSpec(memory_space=pltpu.VMEM),
        scratch_shapes=[
            pltpu.VMEM((SH * SH, KL * KS), jnp.bfloat16),
            pltpu.VMEM((2, NJ * 2 * SH, 128), jnp.float32),
            pltpu.SemaphoreType.DMA((4,)),
        ],
        compiler_params=pltpu.CompilerParams(vmem_limit_bytes=VMEM_LIMIT),
        cost_estimate=pl.CostEstimate(flops=140_000_000, bytes_accessed=3_000_000, transcendentals=0),
        name="ket_transform",
    )(slabs, occ_lam, occ_sig.T, pair_ints)
    return out.reshape(NJ, 2, SH, NI * SH)


def ring_place(offset):
    return jnp.where(offset == 0, 0, jnp.where(offset == 3, 1, offset + 1))


def ring_offset(place):
    return jnp.where(place == 0, 0, jnp.where(place == 3, 2, (place * 2 + 1) & 3))


def plan_kernel(place_ref, pairs_ref, across_ref, plan_ref):
    x = place_ref[0]
    y = place_ref[1]
    core = place_ref[3]
    size = (NBLK, NBLK)
    row = lax.broadcasted_iota(jnp.int32, size, 0)
    lane = lax.broadcasted_iota(jnp.int32, size, 1)
    p = row[:, 0:1]
    away_x = (((p >> 2) & 3) - x) & 3
    away_y = ((p & 3) - y) & 3
    inner = ring_place(jnp.where(core == 0, away_x, away_y))
    outer = ring_place(jnp.where(core == 0, away_y, away_x))
    slot = (outer * 4 + inner) * 8 + (p >> 4)
    wide = lax.broadcasted_iota(jnp.int32, (NBLK, 2 * NBLK), 1)

    def total(mask, value, axis):
        picked = jnp.where(mask, value.astype(jnp.float32), 0.0)
        return jnp.sum(picked, axis=axis, keepdims=True).astype(jnp.int32)

    one_down = pairs_ref[:, 0:1]
    two_down = pairs_ref[:, 1:2]
    one_across = across_ref[0:1, :]
    two_across = across_ref[1:2, :]
    lines = []
    targets = []
    for kind in range(2):
        if kind == 0:
            down, across, other = two_down, two_across, one_down
        else:
            other = two_down
            down = jnp.where(one_down == two_down, NBLK - 1, one_down)
            across = jnp.where(one_across == two_across, NBLK - 1, one_across)
        ones = jnp.ones(size, jnp.int32)
        rank = total((down == across) & (lane < row), ones, 1)
        groups_across = jnp.where(lane[0:1] < NSH, (total(down == lane, ones, 0) + 3) >> 2, 0)
        groups_down = jnp.where(row[:, 0:1] < NSH, (total(across == row, ones, 1) + 3) >> 2, 0)
        groups_square = jnp.broadcast_to(groups_across, size)
        before_term = total(lane < down, groups_square, 1)
        before_shell = total(lane < row, groups_square, 1)
        position = jnp.where(down < NSH, before_term * 4 + rank, -1)
        entry = jnp.broadcast_to(other * 256 + slot - NBLK, wide.shape)
        lines.append(total(position == wide, entry, 0) + NBLK)
        here = (lane >= before_shell) & (lane < before_shell + groups_down)
        shell = total(here, row - NSH, 0) + NSH
        number = jnp.sum(groups_across.astype(jnp.float32), axis=1, keepdims=True).astype(jnp.int32)
        targets.append(jnp.concatenate([shell, jnp.broadcast_to(number, shell.shape)], axis=1))
    plan_ref[...] = jnp.concatenate(lines + targets + lines + targets, axis=0)


def plan_terms(shell_pairs, place):
    return pl.pallas_call(
        plan_kernel,
        out_shape=jax.ShapeDtypeStruct((8, 2 * NBLK), jnp.int32),
        in_specs=[
            pl.BlockSpec(memory_space=pltpu.SMEM),
            pl.BlockSpec(memory_space=pltpu.VMEM),
            pl.BlockSpec(memory_space=pltpu.VMEM),
        ],
        out_specs=pl.BlockSpec(memory_space=pltpu.VMEM),
        compiler_params=pltpu.CompilerParams(vmem_limit_bytes=VMEM_LIMIT),
        cost_estimate=pl.CostEstimate(flops=2_000_000, bytes_accessed=10_000, transcendentals=0),
        name="plan_terms",
    )(place, shell_pairs, shell_pairs.T)


UNROLL = 8
FIRSTS = (0, 32, 64, 96, 112, 128)


def build_left(plan_ref, halves, panel_hbm, left, scratch, start_others=lambda: None):
    blocks, panel, lhs, acc, sem_blocks, sem_panel = scratch
    copy_panel = pltpu.make_async_copy(panel_hbm, panel, sem_panel)
    copy_panel.start()
    copies = [
        pltpu.make_async_copy(
            halves[i], blocks.at[pl.ds(FIRSTS[i], FIRSTS[i + 1] - FIRSTS[i])], sem_blocks.at[i]
        )
        for i in range(5)
    ]
    for copy in copies:
        copy.start()
    others = start_others()
    blocks[NBLK] = jnp.zeros(blocks.shape[1:], jnp.bfloat16)

    @pl.loop(0, NSH)
    def _(shell):
        acc[shell] = jnp.zeros(acc.shape[1:], jnp.float32)

    copy_panel.wait()
    for shell in range(NSH):
        rows = panel[shell * SH:(shell + 1) * SH, :]
        lhs[shell] = jnp.concatenate([rows, rows], axis=0).T
    low = lax.broadcasted_iota(jnp.int32, (PANEL, 128), 1) < SH
    low_rows = lax.broadcasted_iota(jnp.int32, (SH, 128), 1) < SH
    for copy in copies:
        copy.wait()

    def terms(kind, group):
        entries = [plan_ref[kind, group * 4 + k] for k in range(4)]
        target = plan_ref[2 + kind, group]
        factor = jnp.concatenate(
            [
                jnp.where(low, lhs[entries[2 * h] >> 8], lhs[entries[2 * h + 1] >> 8])
                for h in range(2)
            ],
            axis=1,
        )
        values = [blocks[entry & 255] for entry in entries]
        if kind == 0:
            return target, jnp.dot(
                factor, jnp.concatenate(values, axis=0), preferred_element_type=jnp.float32
            )
        columns = []
        for h in range(2):
            stack = []
            for rp in range(2):
                a = values[2 * h][:, rp * 128:rp * 128 + 128]
                b = values[2 * h + 1][:, rp * 128:rp * 128 + 128]
                stack.append(jnp.where(low_rows, a, pltpu.roll(b, SH, 1)))
                stack.append(jnp.where(low_rows, pltpu.roll(a, SH, 1), b))
            columns.append(jnp.concatenate(stack, axis=0))
        return target, lax.dot_general(
            factor, jnp.concatenate(columns, axis=1), (((1,), (1,)), ((), ())),
            preferred_element_type=jnp.float32,
        )

    for kind in range(2):
        steps = (plan_ref[2 + kind, NBLK] + UNROLL - 1) // UNROLL

        @pl.loop(0, steps)
        def _(step):
            for u in range(UNROLL):
                target, sums = terms(kind, step * UNROLL + u)
                acc[target] += sums

    @pl.loop(0, NSH // 2)
    def _(t):
        for rp in range(2):
            even = acc[2 * t, :, rp * 128:rp * 128 + 128]
            odd = acc[2 * t + 1, :, rp * 128:rp * 128 + 128]
            columns = pl.ds(pl.multiple_of(t * 128, 128), 128)
            left[rp * 2 * PANEL:(rp * 2 + 1) * PANEL, columns] = jnp.where(
                low, even, pltpu.roll(odd, SH, 1)
            ).astype(jnp.bfloat16)
            left[(rp * 2 + 1) * PANEL:(rp * 2 + 2) * PANEL, columns] = jnp.where(
                low, pltpu.roll(even, SH, 1), odd
            ).astype(jnp.bfloat16)
    return others


LEFT_SCRATCH = [
    pltpu.VMEM((NBLK + 1, SH, NI * SH), jnp.bfloat16),
    pltpu.VMEM((NAO, PANEL), jnp.bfloat16),
    pltpu.VMEM((NSH, PANEL, 2 * SH), jnp.bfloat16),
    pltpu.VMEM((NSH + 1, PANEL, NI * SH), jnp.float32),
    pltpu.SemaphoreType.DMA((5,)),
    pltpu.SemaphoreType.DMA,
]


def start_coefs(place_ref, pieces, coefs, sems):
    z = place_ref[2]
    core = place_ref[3]
    copies = []
    for k in range(10):
        offset = (0, 3, 1, 2, 2)[k % 5]
        base, slots = ((0, 16), (0, 16), (0, 16), (0, 8), (8, 8))[k % 5]
        chunk = ((z + offset) & 3) * 2 + (core if k < 5 else 1 - core)
        copies.append(
            pltpu.make_async_copy(pieces[k], coefs.at[chunk, pl.ds(base, slots)], sems.at[k])
        )
    for copy in copies:
        copy.start()
    return copies


def multiply(place_ref, left, coefs, out_ref, staged, sem_out):
    x = place_ref[0]
    y = place_ref[1]

    def slot_of(panel, which_core):
        there = (panel >> 2, panel & 3)
        first = (there[0] - x) & 3
        second = (there[1] - y) & 3
        if which_core == 1:
            first, second = second, first
        return ring_place(second) * 4 + ring_place(first)

    def out_copy(n, slot):
        return pltpu.make_async_copy(
            staged.at[slot],
            out_ref.at[:, :, pl.ds(pl.multiple_of(n * 256, 256), 256)],
            sem_out.at[slot],
        )

    @pl.loop(0, ACT // 256)
    def _(n):
        slot = n % 2

        @pl.when(n >= 2)
        def _():
            out_copy(n - 2, slot).wait()

        slots = [[slot_of(2 * n + h, c) for h in range(2)] for c in range(2)]
        rhs = jnp.concatenate(
            [
                jnp.concatenate([coefs[chunk, slots[chunk % 2][h]] for h in range(2)], axis=1)
                for chunk in range(8)
            ],
            axis=0,
        )
        for slab in range(2):
            product = jnp.dot(left[slab], rhs, preferred_element_type=jnp.float32)
            staged[slot, slab] = product.astype(jnp.bfloat16)
        out_copy(n, slot).start()

    out_copy(ACT // 256 - 2, 0).wait()
    out_copy(ACT // 256 - 1, 1).wait()


def left_kernel(*refs):
    build_left(refs[0], refs[1:6], refs[6], refs[7], refs[8:])


def left_of_slab(plan, halves, panel):
    return pl.pallas_call(
        left_kernel,
        out_shape=jax.ShapeDtypeStruct((ROWS, NAO), jnp.bfloat16),
        in_specs=[pl.BlockSpec(memory_space=pltpu.SMEM)] + [pl.BlockSpec(memory_space=pltpu.HBM)] * 6,
        out_specs=pl.BlockSpec(memory_space=pltpu.VMEM),
        scratch_shapes=LEFT_SCRATCH,
        compiler_params=pltpu.CompilerParams(vmem_limit_bytes=VMEM_LIMIT),
        cost_estimate=pl.CostEstimate(flops=9_000_000_000, bytes_accessed=7_000_000, transcendentals=0),
        name="left_of_slab",
    )(plan, *halves, panel)


def finish_kernel(*refs):
    plan_ref, place_ref = refs[:2]
    out_ref, coefs, left, staged, sem_coefs, sem_out, sem_left = refs[19:26]

    def start_others():
        copy_left = pltpu.make_async_copy(refs[18], left.at[0], sem_left)
        copy_left.start()
        return [copy_left] + start_coefs(place_ref, refs[8:18], coefs, sem_coefs)

    copies = build_left(plan_ref, refs[2:7], refs[7], left.at[1], refs[26:], start_others)
    for copy in copies:
        copy.wait()
    multiply(place_ref, left, coefs, out_ref, staged, sem_out)


def finish(plan, place, halves, panel, pieces, left):
    return pl.pallas_call(
        finish_kernel,
        out_shape=jax.ShapeDtypeStruct((2, ROWS, ACT), jnp.bfloat16),
        in_specs=[pl.BlockSpec(memory_space=pltpu.SMEM)] * 2 + [pl.BlockSpec(memory_space=pltpu.HBM)] * 17,
        out_specs=pl.BlockSpec(memory_space=pltpu.HBM),
        scratch_shapes=[
            pltpu.VMEM((8, 16, 256, PANEL), jnp.bfloat16),
            pltpu.VMEM((2, ROWS, NAO), jnp.bfloat16),
            pltpu.VMEM((2, 2, ROWS, 256), jnp.bfloat16),
            pltpu.SemaphoreType.DMA((10,)),
            pltpu.SemaphoreType.DMA((2,)),
            pltpu.SemaphoreType.DMA,
        ] + LEFT_SCRATCH,
        compiler_params=pltpu.CompilerParams(vmem_limit_bytes=VMEM_LIMIT),
        cost_estimate=pl.CostEstimate(flops=18_000_000_000, bytes_accessed=20_000_000, transcendentals=0),
        name="finish",
    )(plan, place, *halves, panel, *pieces, left)


def body(pair_ints, shell_pairs, occ_lam, occ_sig, coef_act, slabs):
    ao_index = lax.axis_index("ao")
    mo_index = lax.axis_index("mo")
    place = jnp.stack([mo_index >> 2, mo_index & 3, ao_index >> 1, ao_index & 1]).astype(jnp.int32)

    up, down = plane_pairs(1, 1), plane_pairs(-1, 1)
    z_up, z_down = z_pairs(1), z_pairs(-1)
    swap = device_pairs(lambda x, y, z, c: (x, y, z, 1 - c))

    half = ket_transform(pair_ints, occ_lam, occ_sig, slabs)
    owned = lax.all_to_all(half, "ao", split_axis=0, concat_axis=0, tiled=True)
    chunk = lax.dynamic_slice_in_dim(after(coef_act, half), ao_index * 256, 256, 0)
    with jax.named_scope("s_c1"):
        row = jnp.stack(direct(chunk, 0))
    with jax.named_scope("s_c2"):
        whole = jnp.concatenate(direct(row, 1), axis=0)
    with jax.named_scope("s_p1"):
        near = direct(owned, 0)
        near_first, near_second = [
            jnp.concatenate([piece[:, k] for piece in near], axis=0) for k in range(2)
        ]
    with jax.named_scope("s_p2a"):
        first = both_ways(near_first, up, down)
    plan = plan_terms(after(shell_pairs, half), place)
    with jax.named_scope("s_z1"):
        column = both_ways(after(whole, near_first, plan), z_up, z_down)
    with jax.named_scope("s_p2b"):
        second = both_ways(after(near_second, *first), up, down)
    with jax.named_scope("s_f2a"):
        first += far_halves(first, up, down)
    with jax.named_scope("s_zf"):
        column += far_halves(column, z_up, z_down, *first[3:])
    left = left_of_slab(plan, first, coef_act)
    with jax.named_scope("s_f2b"):
        second += far_halves(second, up, down, left)
    with jax.named_scope("s_swap"):
        pieces = list(column) + [send(after(piece, first[4]), swap) for piece in column]
    out = finish(plan, place, second, coef_act, pieces, left)
    return out.reshape(2, 1, NI, PANEL, ACT)


def solution(mesh):
    return jax.shard_map(
        body,
        mesh=mesh,
        in_specs=(P(("ao", "mo"), None, None), P(), P(), P(), P(None, "mo"), P()),
        out_specs=P(None, "ao", None, "mo", None),
        check_vma=False,
    )
```

time: 475 us -> 137 us (0.29)
  matrix products: 300 us -> 0 us
  local copies, waits for them, and re-layouts: 84.5 us -> 11.6 us
  Pallas kernels: 0 us -> 43.1 us
  starting transfers between devices: 0.09 us -> 41 us
  blocking collectives: 23.4 us -> 0 us
  between operations: 14.6 us -> 0.49 us
  other arithmetic: 9.74 us -> 0.96 us
    dot_general x52 -> x0, matrix products: 292 us -> none  [the longest x16 169 us: accumulate(): jnp.einsum('ps,pram->rasm', place_one, term_two, precision=lax.Precision....]
    pallas_call x0 -> x4, Pallas kernels: none -> 43.1 us  [the longest x1 24.2 us: finish(): pl.pallas_call(finish_kernel, out_shape=jax.ShapeDtypeStruct((2, ROWS, AC...]
    all_gather x3 -> x0, waiting for transfers between devices: 38.4 us -> none  [the longest x2 38.4 us: remap_pairs(): return lax.all_gather(owned, 'mo', axis=1, tiled=True)]
    ppermute x0 -> x26, waiting for transfers between devices: none -> 38.2 us  [send(): return lax.ppermute(value, AXES, pairs)]
    ppermute x0 -> x26, starting transfers between devices: none -> 35.5 us  [send(): return lax.ppermute(value, AXES, pairs)]
    dynamic_slice x32 -> x0, local copies, waits for them, and re-layouts: 31.6 us -> none  [bra_transform(): left_terms = lax.scan(accumulate, start_terms, (grouped, grouped_pairs))[0]]
    another operation x5 -> x0, local copies, waits for them, and re-layouts: 25.7 us -> none  [the longest x2 25.4 us: bra_transform(): grouped = gathered.reshape(block_count // 16, 16, pair_rows, SH, SH)]
    all_to_all x2 -> x0, blocking collectives: 23.4 us -> none  [remap_pairs(): lax.all_to_all(stacked, 'ao', split_axis=2, concat_axis=1, tiled=True)]
  transfers between devices with their start and end apart: 3 -> 27, of which waited for: 1 -> 11; matrix products, arithmetic and copies ran while one was open for 79% -> 7% of each run, Pallas kernels for 0% -> 10%
where the time goes in v2:
time: 137 us; the launch traced here: 136 us
  Pallas kernels  43.1 us (31%)
  starting transfers between devices  41 us (30%)
  waiting for transfers between devices  38.7 us (28%)
  local copies, waits for them, and re-layouts  11.6 us (8%)
    ppermute x26, waiting for transfers between devices, send(): return lax.ppermute(value, AXES, pairs)  38.2 us
    ppermute x26, starting transfers between devices, send(): return lax.ppermute(value, AXES, pairs)  35.5 us
    pallas_call x1, Pallas kernels, finish(): pl.pallas_call(finish_kernel, out_shape=jax.ShapeDtypeStruct((2, ROWS, AC...  24.2 us
    pallas_call x1, Pallas kernels, left_of_slab(): pl.pallas_call(left_kernel, out_shape=jax.ShapeDtypeStruct((ROWS, NAO), j...  12.2 us
    unnamed x40, local copies, waits for them, and re-layouts  7.6 us
    all_to_all x1, starting transfers between devices, body(): owned = lax.all_to_all(half, 'ao', split_axis=0, concat_axis=0, tiled=True)  5.41 us
    pallas_call x1, Pallas kernels, ket_transform(): pl.pallas_call(ket_kernel, out_shape=jax.ShapeDtypeStruct((NJ * 2 * SH, N...  4.64 us
  transfers between devices with their start and end apart: 27, of which 11 were waited for; matrix products, arithmetic and copies ran while one was open for 7% of the time, Pallas kernels for 10%

profile of v2, /device:TPU:0, one launch (start us, length us, event | category | flops | bytes accessed | tf_op | source)
XLA Modules:
  0.0 135.8 jit_solution(3426410905642226495)
XLA Ops:
  0.0 4.6 %ket_transform.1 = bf16[1024,256]{1,0:T(8,128)(2,1)} custom-call(s32[2]{0:T(128)} %slabs_ref.1, bf16[16,32]{1,0:T(8,128)(2,1)} %lam_ref.1, bf16[8,16]{1,0:T(8,128)(2,1)} %bitcast.40, bf16[1,4096,256]{2,1,0:T(8,128)(2,1)} %ints_hbm.1), custom_call_target="tpu_custom_call" | custom-call | flops 140000000 | bytes 3000000 | tf_op jit(solution)/shard_map/ket_transform/pallas_call | solution.py:126
  4.6 5.4 %all-to-all-start = ((bf16[8,2,64,256]{3,2,1,0:T(8,128)(2,1)}), bf16[8,2,64,256]{3,2,1,0:T(8,128)(2,1)S(1)}, u32[]{:S(2)}, u32[]{:S(2)}) async-start(bf16[8,2,64,256]{3,2,1,0:T(8,128)(2,1)} %bitcast.34), calls=%async_computation | async-start | bytes 1048576 | tf_op jit(solution)/shard_map/all_to_all | solution.py:438
  10.1 1.5 %constant_dynamic-update-slice_fusion.6 = (bf16[16,256,128]{2,1,0:T(8,128)(2,1)}, bf16[256,128]{1,0:T(8,128)(2,1)S(1)}) fusion(bf16[2048,128]{1,0:T(8,128)(2,1)} %refs_7_.1, s32[]{:T(128)S(6)} %select_n.3), kind=kLoop, calls=%fused_computation.17 | loop fusion | bytes 196612
  11.5 3.0 %collective-permute-start.13 = (bf16[256,128]{1,0:T(8,128)(2,1)S(1)}, bf16[256,128]{1,0:T(8,128)(2,1)S(1)}, u32[]{:S(2)}, u32[]{:S(2)}) collective-permute-start(bf16[256,128]{1,0:T(8,128)(2,1)S(1)} %get-tuple-element.32), channel_id=1, source_target_pairs={{0,8},{1,9},{2,10},{3,11},{4,12},{5,13},{6,14},{7,15},{8,0},{9,1},... | collective-permute-start | bytes 196616 | tf_op jit(solution)/shard_map/s_c1/ppermute | solution.py:50
  18.0 2.0 %plan_terms.1.refs_0_ = s32[8,256]{1,0:T(8,128)} custom-call(s32[4]{0:T(128)} %pad_add_fusion.place_ref.refs_1_, s32[128,2]{1,0:T(8,128)} %copy.12.pairs_ref, s32[2,128]{1,0:T(2,128)} %bitcast.39), custom_call_target="tpu_custom_call" | custom-call | flops 2000000 | bytes 10000 | tf_op jit(solution)/shard_map/plan_terms/pallas_call | solution.py:206
  20.5 2.8 %collective-permute-start.1 = (bf16[8,2,64,256]{3,2,0,1:T(8,128)(2,1)S(1)}, bf16[8,2,64,256]{3,2,0,1:T(8,128)(2,1)S(1)}, u32[]{:S(2)}, u32[]{:S(2)}) collective-permute-start(bf16[8,2,64,256]{3,2,0,1:T(8,128)(2,1)S(1)} %copy.13), channel_id=1, source_target_pairs={{0,12},{1,13},{2,14},{3,15},{4,0},{5,1},{6,2},{7,3},{8,4},{9,5},{1... | collective-permute-start | bytes 1572872 | tf_op jit(solution)/shard_map/s_p1/ppermute | solution.py:50
  23.3 3.3 %collective-permute-start.16 = (bf16[4,256,128]{2,1,0:T(8,128)(2,1)S(1)}, bf16[4,256,128]{2,1,0:T(8,128)(2,1)S(1)}, u32[]{:S(2)}, u32[]{:S(2)}) collective-permute-start(bf16[4,256,128]{2,1,0:T(8,128)(2,1)S(1)} %pad_maximum_fusion.2), channel_id=1, source_target_pairs={{0,2},{1,3},{2,0},{3,1},{4,6},{5,7},{6,4},{7,5},{8,10},{9,11},{10,... | collective-permute-start | bytes 786440 | tf_op jit(solution)/shard_map/s_c2/ppermute | solution.py:50
  28.3 2.3 %collective-permute-start.2 = (bf16[8,2,64,256]{3,2,0,1:T(8,128)(2,1)S(1)}, bf16[8,2,64,256]{3,2,0,1:T(8,128)(2,1)S(1)}, u32[]{:S(2)}, u32[]{:S(2)}) collective-permute-start(bf16[8,2,64,256]{3,2,0,1:T(8,128)(2,1)S(1)} %copy.13), channel_id=1, source_target_pairs={{0,8},{1,9},{2,10},{3,11},{4,12},{5,13},{6,14},{7,15},{8,0},{9,1},... | collective-permute-start | bytes 1572872 | tf_op jit(solution)/shard_map/s_p1/ppermute | solution.py:50
  30.6 10.6 %collective-permute-done.1 = bf16[8,2,64,256]{3,2,0,1:T(8,128)(2,1)S(1)} collective-permute-done((bf16[8,2,64,256]{3,2,0,1:T(8,128)(2,1)S(1)}, bf16[8,2,64,256]{3,2,0,1:T(8,128)(2,1)S(1)}, u32[]{:S(2)}, u32[]{:S(2)}) %collective-permute-start.1) | collective-permute-done | bytes 524320 | tf_op jit(solution)/shard_map/s_p1/ppermute | solution.py:50
  42.5 1.4 %collective-permute-done = bf16[8,2,64,256]{3,2,0,1:T(8,128)(2,1)S(1)} collective-permute-done((bf16[8,2,64,256]{3,2,0,1:T(8,128)(2,1)S(1)}, bf16[8,2,64,256]{3,2,0,1:T(8,128)(2,1)S(1)}, u32[]{:S(2)}, u32[]{:S(2)}) %collective-permute-start) | collective-permute-done | bytes 524320 | tf_op jit(solution)/shard_map/s_p1/ppermute | solution.py:50
  45.5 2.1 %collective-permute-start.3 = (bf16[32,64,256]{2,1,0:T(8,128)(2,1)S(1)}, bf16[32,64,256]{2,1,0:T(8,128)(2,1)S(1)}, u32[]{:S(2)}, u32[]{:S(2)}) collective-permute-start(bf16[32,64,256]{2,1,0:T(8,128)(2,1)S(1)} %pad_maximum_fusion.1.refs_1_), channel_id=1, source_target_pairs={{0,1},{1,2},{2,3},{3,0},{4,5},{5,6},{6,7},{7,4},{8,9},{9,10},{10,1... | collective-permute-start | bytes 3145736 | tf_op jit(solution)/shard_map/s_p2a/ppermute | solution.py:50
  51.0 2.4 %collective-permute-start.18 = (bf16[16,256,128]{2,1,0:T(8,128)(2,1)}, bf16[16,256,128]{2,1,0:T(8,128)(2,1)S(1)}, u32[]{:S(2)}, u32[]{:S(2)}) collective-permute-start(bf16[16,256,128]{2,1,0:T(8,128)(2,1)} %constant_dynamic-update-slice_fusion.refs_8_), channel_id=1, source_target_pairs={{0,96},{1,97},{2,98},{3,99},{4,100},{5,101},{6,102},{7,103},{8,104... | collective-permute-start | bytes 3145736 | tf_op jit(solution)/shard_map/s_z1/ppermute | solution.py:50
  53.4 6.3 %collective-permute-done.4.refs_3_ = bf16[32,64,256]{2,1,0:T(8,128)(2,1)S(1)} collective-permute-done((bf16[32,64,256]{2,1,0:T(8,128)(2,1)S(1)}, bf16[32,64,256]{2,1,0:T(8,128)(2,1)S(1)}, u32[]{:S(2)}, u32[]{:S(2)}) %collective-permute-start.4) | collective-permute-done | bytes 1048608 | tf_op jit(solution)/shard_map/s_p2a/ppermute | solution.py:50
  62.7 2.4 %collective-permute-start.6 = (bf16[32,64,256]{2,1,0:T(8,128)(2,1)S(1)}, bf16[32,64,256]{2,1,0:T(8,128)(2,1)}, u32[]{:S(2)}, u32[]{:S(2)}) collective-permute-start(bf16[32,64,256]{2,1,0:T(8,128)(2,1)S(1)} %pad_maximum_fusion.refs_2_), channel_id=1, source_target_pairs={{0,3},{1,0},{2,1},{3,2},{4,7},{5,4},{6,5},{7,6},{8,11},{9,8},{10,9... | collective-permute-start | bytes 3145736 | tf_op jit(solution)/shard_map/s_p2b/ppermute | solution.py:50
  65.1 3.9 %collective-permute-done.8.refs_5_ = bf16[16,64,256]{2,1,0:T(8,128)(2,1)S(1)} collective-permute-done((bf16[16,64,256]{2,1,0:T(8,128)(2,1)S(1)}, bf16[16,64,256]{2,1,0:T(8,128)(2,1)S(1)}, u32[]{:S(2)}, u32[]{:S(2)}) %collective-permute-start.8) | collective-permute-done | bytes 524320 | tf_op jit(solution)/shard_map/s_f2a/ppermute | solution.py:50
  68.9 2.0 %collective-permute-start.5 = (bf16[32,64,256]{2,1,0:T(8,128)(2,1)S(1)}, bf16[32,64,256]{2,1,0:T(8,128)(2,1)}, u32[]{:S(2)}, u32[]{:S(2)}) collective-permute-start(bf16[32,64,256]{2,1,0:T(8,128)(2,1)S(1)} %pad_maximum_fusion.refs_2_), channel_id=1, source_target_pairs={{0,1},{1,2},{2,3},{3,0},{4,5},{5,6},{6,7},{7,4},{8,9},{9,10},{10,1... | collective-permute-start | bytes 3145736 | tf_op jit(solution)/shard_map/s_p2b/ppermute | solution.py:50
  71.0 3.1 %collective-permute-done.18.refs_10_ = bf16[16,256,128]{2,1,0:T(8,128)(2,1)S(1)} collective-permute-done((bf16[16,256,128]{2,1,0:T(8,128)(2,1)}, bf16[16,256,128]{2,1,0:T(8,128)(2,1)S(1)}, u32[]{:S(2)}, u32[]{:S(2)}) %collective-permute-start.18) | collective-permute-done | bytes 1048608 | tf_op jit(solution)/shard_map/s_z1/ppermute | solution.py:50
  74.1 3.7 %collective-permute-start.20 = (bf16[8,256,128]{2,1,0:T(8,128)(2,1)S(1)}, bf16[8,256,128]{2,1,0:T(8,128)(2,1)S(1)}, u32[]{:S(2)}, u32[]{:S(2)}) collective-permute-start(bf16[8,256,128]{2,1,0:T(8,128)(2,1)S(1)} %slice.55), channel_id=1, source_target_pairs={{0,96},{1,97},{2,98},{3,99},{4,100},{5,101},{6,102},{7,103},{8,104... | collective-permute-start | bytes 1572872 | tf_op jit(solution)/shard_map/s_zf/ppermute | solution.py:50
  78.9 12.2 %left_of_slab.1.refs_18_ = bf16[512,2048]{1,0:T(8,128)(2,1)} custom-call(s32[8,256]{1,0:T(8,128)} %plan_terms.1.refs_0_, bf16[32,64,256]{2,1,0:T(8,128)(2,1)} %copy-done.1, bf16[32,64,256]{2,1,0:T(8,128)(2,1)} %copy-done.6, bf16[32,64,256]{2,1,0:T(8,128)(2,1)} %copy-done.5, bf16[16,64,256]{2,1,0:T(8,128)(2,1)} %copy-done.14, ...), custom_call_target="tpu_custom_call" | custom-call | flops 8999999488 | bytes 7000000 | tf_op jit(solution)/shard_map/left_of_slab/pallas_call | solution.py:381
  92.4 3.4 %collective-permute-start.10 = (bf16[16,64,256]{2,1,0:T(8,128)(2,1)S(1)}, bf16[16,64,256]{2,1,0:T(8,128)(2,1)S(1)}, u32[]{:S(2)}, u32[]{:S(2)}) collective-permute-start(bf16[16,64,256]{2,1,0:T(8,128)(2,1)S(1)} %slice.53), channel_id=1, source_target_pairs={{0,3},{1,0},{2,1},{3,2},{4,7},{5,4},{6,5},{7,6},{8,11},{9,8},{10,9... | collective-permute-start | bytes 1572872 | tf_op jit(solution)/shard_map/s_f2b/ppermute | solution.py:50
  97.7 4.7 %collective-permute-done.10.refs_6_ = bf16[16,64,256]{2,1,0:T(8,128)(2,1)S(1)} collective-permute-done((bf16[16,64,256]{2,1,0:T(8,128)(2,1)S(1)}, bf16[16,64,256]{2,1,0:T(8,128)(2,1)S(1)}, u32[]{:S(2)}, u32[]{:S(2)}) %collective-permute-start.10) | collective-permute-done | bytes 524320 | tf_op jit(solution)/shard_map/s_f2b/ppermute | solution.py:50
  102.5 5.0 %collective-permute-done.9.refs_5_ = bf16[16,64,256]{2,1,0:T(8,128)(2,1)S(1)} collective-permute-done((bf16[16,64,256]{2,1,0:T(8,128)(2,1)S(1)}, bf16[16,64,256]{2,1,0:T(8,128)(2,1)S(1)}, u32[]{:S(2)}, u32[]{:S(2)}) %collective-permute-start.9) | collective-permute-done | bytes 524320 | tf_op jit(solution)/shard_map/s_f2b/ppermute | solution.py:50
  107.5 2.1 %collective-permute-done.24.refs_16_ = bf16[8,256,128]{2,1,0:T(8,128)(2,1)S(1)} collective-permute-done((bf16[8,256,128]{2,1,0:T(8,128)(2,1)}, bf16[8,256,128]{2,1,0:T(8,128)(2,1)S(1)}, u32[]{:S(2)}, u32[]{:S(2)}) %collective-permute-start.24) | collective-permute-done | bytes 524320 | tf_op jit(solution)/shard_map/s_swap/ppermute | solution.py:50
  111.4 24.2 %finish.1 = bf16[2,512,2048]{2,1,0:T(8,128)(2,1)} custom-call(s32[8,256]{1,0:T(8,128)} %plan_terms.1.refs_0_, s32[4]{0:T(128)} %pad_add_fusion.place_ref.refs_1_, bf16[32,64,256]{2,1,0:T(8,128)(2,1)} %copy-done, bf16[32,64,256]{2,1,0:T(8,128)(2,1)} %collective-permute-done.5.refs_3_, bf16[32,64,256]{2,1,0:T(8,128)(2,1)} %collective-permute-done.6.refs_4_, ...), custom_call_target="tpu_custom_call" | custom-call | flops 17999998976 | bytes 20000000 | tf_op jit(solution)/shard_map/finish/pallas_call | solution.py:409
  (91 shorter events, 20.8 us)
Async XLA Ops:
  4.6 15.8 %all-to-all-start = ((bf16[8,2,64,256]{3,2,1,0:T(8,128)(2,1)}), bf16[8,2,64,256]{3,2,1,0:T(8,128)(2,1)S(1)}, u32[]{:S(2)}, u32[]{:S(2)}) async-start(bf16[8,2,64,256]{3,2,1,0:T(8,128)(2,1)} %bitcast.34), calls=%async_computation | async-start | bytes 1048576 | tf_op jit(solution)/shard_map/all_to_all | solution.py:438
  11.5 11.8 %collective-permute-start.13 = (bf16[256,128]{1,0:T(8,128)(2,1)S(1)}, bf16[256,128]{1,0:T(8,128)(2,1)S(1)}, u32[]{:S(2)}, u32[]{:S(2)}) collective-permute-start(bf16[256,128]{1,0:T(8,128)(2,1)S(1)} %get-tuple-element.32), channel_id=1, source_target_pairs={{0,8},{1,9},{2,10},{3,11},{4,12},{5,13},{6,14},{7,15},{8,0},{9,1},... | collective-permute-start | bytes 196616 | tf_op jit(solution)/shard_map/s_c1/ppermute | solution.py:50
  14.5 8.7 %collective-permute-start.12 = (bf16[256,128]{1,0:T(8,128)(2,1)S(1)}, bf16[256,128]{1,0:T(8,128)(2,1)S(1)}, u32[]{:S(2)}, u32[]{:S(2)}) collective-permute-start(bf16[256,128]{1,0:T(8,128)(2,1)S(1)} %get-tuple-element.32), channel_id=1, source_target_pairs={{0,12},{1,13},{2,14},{3,15},{4,0},{5,1},{6,2},{7,3},{8,4},{9,5},{1... | collective-permute-start | bytes 196616 | tf_op jit(solution)/shard_map/s_c1/ppermute | solution.py:50
  15.7 7.6 %collective-permute-start.11 = (bf16[256,128]{1,0:T(8,128)(2,1)S(1)}, bf16[256,128]{1,0:T(8,128)(2,1)S(1)}, u32[]{:S(2)}, u32[]{:S(2)}) collective-permute-start(bf16[256,128]{1,0:T(8,128)(2,1)S(1)} %get-tuple-element.32), channel_id=1, source_target_pairs={{0,4},{1,5},{2,6},{3,7},{4,8},{5,9},{6,10},{7,11},{8,12},{9,13},{1... | collective-permute-start | bytes 196616 | tf_op jit(solution)/shard_map/s_c1/ppermute | solution.py:50
  20.5 20.8 %collective-permute-start.1 = (bf16[8,2,64,256]{3,2,0,1:T(8,128)(2,1)S(1)}, bf16[8,2,64,256]{3,2,0,1:T(8,128)(2,1)S(1)}, u32[]{:S(2)}, u32[]{:S(2)}) collective-permute-start(bf16[8,2,64,256]{3,2,0,1:T(8,128)(2,1)S(1)} %copy.13), channel_id=1, source_target_pairs={{0,12},{1,13},{2,14},{3,15},{4,0},{5,1},{6,2},{7,3},{8,4},{9,5},{1... | collective-permute-start | bytes 1572872 | tf_op jit(solution)/shard_map/s_p1/ppermute | solution.py:50
  23.3 26.9 %collective-permute-start.16 = (bf16[4,256,128]{2,1,0:T(8,128)(2,1)S(1)}, bf16[4,256,128]{2,1,0:T(8,128)(2,1)S(1)}, u32[]{:S(2)}, u32[]{:S(2)}) collective-permute-start(bf16[4,256,128]{2,1,0:T(8,128)(2,1)S(1)} %pad_maximum_fusion.2), channel_id=1, source_target_pairs={{0,2},{1,3},{2,0},{3,1},{4,6},{5,7},{6,4},{7,5},{8,10},{9,11},{10,... | collective-permute-start | bytes 786440 | tf_op jit(solution)/shard_map/s_c2/ppermute | solution.py:50
  26.6 22.9 %collective-permute-start.15 = (bf16[4,256,128]{2,1,0:T(8,128)(2,1)S(1)}, bf16[4,256,128]{2,1,0:T(8,128)(2,1)S(1)}, u32[]{:S(2)}, u32[]{:S(2)}) collective-permute-start(bf16[4,256,128]{2,1,0:T(8,128)(2,1)S(1)} %pad_maximum_fusion.2), channel_id=1, source_target_pairs={{0,3},{1,0},{2,1},{3,2},{4,7},{5,4},{6,5},{7,6},{8,11},{9,8},{10,9... | collective-permute-start | bytes 786440 | tf_op jit(solution)/shard_map/s_c2/ppermute | solution.py:50
  27.7 16.3 %collective-permute-start = (bf16[8,2,64,256]{3,2,0,1:T(8,128)(2,1)S(1)}, bf16[8,2,64,256]{3,2,0,1:T(8,128)(2,1)S(1)}, u32[]{:S(2)}, u32[]{:S(2)}) collective-permute-start(bf16[8,2,64,256]{3,2,0,1:T(8,128)(2,1)S(1)} %copy.13), channel_id=1, source_target_pairs={{0,4},{1,5},{2,6},{3,7},{4,8},{5,9},{6,10},{7,11},{8,12},{9,13},{1... | collective-permute-start | bytes 1572872 | tf_op jit(solution)/shard_map/s_p1/ppermute | solution.py:50
  28.3 15.7 %collective-permute-start.2 = (bf16[8,2,64,256]{3,2,0,1:T(8,128)(2,1)S(1)}, bf16[8,2,64,256]{3,2,0,1:T(8,128)(2,1)S(1)}, u32[]{:S(2)}, u32[]{:S(2)}) collective-permute-start(bf16[8,2,64,256]{3,2,0,1:T(8,128)(2,1)S(1)} %copy.13), channel_id=1, source_target_pairs={{0,8},{1,9},{2,10},{3,11},{4,12},{5,13},{6,14},{7,15},{8,0},{9,1},... | collective-permute-start | bytes 1572872 | tf_op jit(solution)/shard_map/s_p1/ppermute | solution.py:50
  44.2 15.5 %collective-permute-start.4 = (bf16[32,64,256]{2,1,0:T(8,128)(2,1)S(1)}, bf16[32,64,256]{2,1,0:T(8,128)(2,1)S(1)}, u32[]{:S(2)}, u32[]{:S(2)}) collective-permute-start(bf16[32,64,256]{2,1,0:T(8,128)(2,1)S(1)} %pad_maximum_fusion.1.refs_1_), channel_id=1, source_target_pairs={{0,3},{1,0},{2,1},{3,2},{4,7},{5,4},{6,5},{7,6},{8,11},{9,8},{10,9... | collective-permute-start | bytes 3145736 | tf_op jit(solution)/shard_map/s_p2a/ppermute | solution.py:50
  45.5 16.0 %collective-permute-start.3 = (bf16[32,64,256]{2,1,0:T(8,128)(2,1)S(1)}, bf16[32,64,256]{2,1,0:T(8,128)(2,1)S(1)}, u32[]{:S(2)}, u32[]{:S(2)}) collective-permute-start(bf16[32,64,256]{2,1,0:T(8,128)(2,1)S(1)} %pad_maximum_fusion.1.refs_1_), channel_id=1, source_target_pairs={{0,1},{1,2},{2,3},{3,0},{4,5},{5,6},{6,7},{7,4},{8,9},{9,10},{10,1... | collective-permute-start | bytes 3145736 | tf_op jit(solution)/shard_map/s_p2a/ppermute | solution.py:50
  51.0 23.1 %collective-permute-start.18 = (bf16[16,256,128]{2,1,0:T(8,128)(2,1)}, bf16[16,256,128]{2,1,0:T(8,128)(2,1)S(1)}, u32[]{:S(2)}, u32[]{:S(2)}) collective-permute-start(bf16[16,256,128]{2,1,0:T(8,128)(2,1)} %constant_dynamic-update-slice_fusion.refs_8_), channel_id=1, source_target_pairs={{0,96},{1,97},{2,98},{3,99},{4,100},{5,101},{6,102},{7,103},{8,104... | collective-permute-start | bytes 3145736 | tf_op jit(solution)/shard_map/s_z1/ppermute | solution.py:50
  53.4 24.4 %collective-permute-start.17 = (bf16[16,256,128]{2,1,0:T(8,128)(2,1)}, bf16[16,256,128]{2,1,0:T(8,128)(2,1)S(1)}, u32[]{:S(2)}, u32[]{:S(2)}) collective-permute-start(bf16[16,256,128]{2,1,0:T(8,128)(2,1)} %constant_dynamic-update-slice_fusion.refs_8_), channel_id=1, source_target_pairs={{0,32},{1,33},{2,34},{3,35},{4,36},{5,37},{6,38},{7,39},{8,40},{9,... | collective-permute-start | bytes 3145736 | tf_op jit(solution)/shard_map/s_z1/ppermute | solution.py:50
  59.7 9.2 %collective-permute-start.8 = (bf16[16,64,256]{2,1,0:T(8,128)(2,1)S(1)}, bf16[16,64,256]{2,1,0:T(8,128)(2,1)S(1)}, u32[]{:S(2)}, u32[]{:S(2)}) collective-permute-start(bf16[16,64,256]{2,1,0:T(8,128)(2,1)S(1)} %slice.65), channel_id=1, source_target_pairs={{0,3},{1,0},{2,1},{3,2},{4,7},{5,4},{6,5},{7,6},{8,11},{9,8},{10,9... | collective-permute-start | bytes 1572872 | tf_op jit(solution)/shard_map/s_f2a/ppermute | solution.py:50
  61.6 12.5 %collective-permute-start.7 = (bf16[16,64,256]{2,1,0:T(8,128)(2,1)S(1)}, bf16[16,64,256]{2,1,0:T(8,128)(2,1)S(1)}, u32[]{:S(2)}, u32[]{:S(2)}) collective-permute-start(bf16[16,64,256]{2,1,0:T(8,128)(2,1)S(1)} %slice.64), channel_id=1, source_target_pairs={{0,1},{1,2},{2,3},{3,0},{4,5},{5,6},{6,7},{7,4},{8,9},{9,10},{10,1... | collective-permute-start | bytes 1572872 | tf_op jit(solution)/shard_map/s_f2a/ppermute | solution.py:50
  62.7 28.5 %collective-permute-start.6 = (bf16[32,64,256]{2,1,0:T(8,128)(2,1)S(1)}, bf16[32,64,256]{2,1,0:T(8,128)(2,1)}, u32[]{:S(2)}, u32[]{:S(2)}) collective-permute-start(bf16[32,64,256]{2,1,0:T(8,128)(2,1)S(1)} %pad_maximum_fusion.refs_2_), channel_id=1, source_target_pairs={{0,3},{1,0},{2,1},{3,2},{4,7},{5,4},{6,5},{7,6},{8,11},{9,8},{10,9... | collective-permute-start | bytes 3145736 | tf_op jit(solution)/shard_map/s_p2b/ppermute | solution.py:50
  68.9 26.8 %collective-permute-start.5 = (bf16[32,64,256]{2,1,0:T(8,128)(2,1)S(1)}, bf16[32,64,256]{2,1,0:T(8,128)(2,1)}, u32[]{:S(2)}, u32[]{:S(2)}) collective-permute-start(bf16[32,64,256]{2,1,0:T(8,128)(2,1)S(1)} %pad_maximum_fusion.refs_2_), channel_id=1, source_target_pairs={{0,1},{1,2},{2,3},{3,0},{4,5},{5,6},{6,7},{7,4},{8,9},{9,10},{10,1... | collective-permute-start | bytes 3145736 | tf_op jit(solution)/shard_map/s_p2b/ppermute | solution.py:50
  74.0 33.5 %collective-permute-start.21 = (bf16[16,256,128]{2,1,0:T(8,128)(2,1)}, bf16[16,256,128]{2,1,0:T(8,128)(2,1)}, u32[]{:S(2)}, u32[]{:S(2)}) collective-permute-start(bf16[16,256,128]{2,1,0:T(8,128)(2,1)} %constant_dynamic-update-slice_fusion.refs_8_), channel_id=1, source_target_pairs={{0,16},{1,17},{2,18},{3,19},{4,20},{5,21},{6,22},{7,23},{8,24},{9,... | collective-permute-start | bytes 3145736 | tf_op jit(solution)/shard_map/s_swap/ppermute | solution.py:50
  74.1 23.0 %collective-permute-start.20 = (bf16[8,256,128]{2,1,0:T(8,128)(2,1)S(1)}, bf16[8,256,128]{2,1,0:T(8,128)(2,1)S(1)}, u32[]{:S(2)}, u32[]{:S(2)}) collective-permute-start(bf16[8,256,128]{2,1,0:T(8,128)(2,1)S(1)} %slice.55), channel_id=1, source_target_pairs={{0,96},{1,97},{2,98},{3,99},{4,100},{5,101},{6,102},{7,103},{8,104... | collective-permute-start | bytes 1572872 | tf_op jit(solution)/shard_map/s_zf/ppermute | solution.py:50
  78.9 18.4 %collective-permute-start.19 = (bf16[8,256,128]{2,1,0:T(8,128)(2,1)S(1)}, bf16[8,256,128]{2,1,0:T(8,128)(2,1)}, u32[]{:S(2)}, u32[]{:S(2)}) collective-permute-start(bf16[8,256,128]{2,1,0:T(8,128)(2,1)S(1)} %slice.54), channel_id=1, source_target_pairs={{0,32},{1,33},{2,34},{3,35},{4,36},{5,37},{6,38},{7,39},{8,40},{9,... | collective-permute-start | bytes 1572872 | tf_op jit(solution)/shard_map/s_zf/ppermute | solution.py:50
  92.4 10.1 %collective-permute-start.10 = (bf16[16,64,256]{2,1,0:T(8,128)(2,1)S(1)}, bf16[16,64,256]{2,1,0:T(8,128)(2,1)S(1)}, u32[]{:S(2)}, u32[]{:S(2)}) collective-permute-start(bf16[16,64,256]{2,1,0:T(8,128)(2,1)S(1)} %slice.53), channel_id=1, source_target_pairs={{0,3},{1,0},{2,1},{3,2},{4,7},{5,4},{6,5},{7,6},{8,11},{9,8},{10,9... | collective-permute-start | bytes 1572872 | tf_op jit(solution)/shard_map/s_f2b/ppermute | solution.py:50
  96.8 10.6 %collective-permute-start.9 = (bf16[16,64,256]{2,1,0:T(8,128)(2,1)S(1)}, bf16[16,64,256]{2,1,0:T(8,128)(2,1)S(1)}, u32[]{:S(2)}, u32[]{:S(2)}) collective-permute-start(bf16[16,64,256]{2,1,0:T(8,128)(2,1)S(1)} %slice.52), channel_id=1, source_target_pairs={{0,1},{1,2},{2,3},{3,0},{4,5},{5,6},{6,7},{7,4},{8,9},{9,10},{10,1... | collective-permute-start | bytes 1572872 | tf_op jit(solution)/shard_map/s_f2b/ppermute | solution.py:50
  97.1 10.4 %collective-permute-start.23 = (bf16[16,256,128]{2,1,0:T(8,128)(2,1)S(1)}, bf16[16,256,128]{2,1,0:T(8,128)(2,1)S(1)}, u32[]{:S(2)}, u32[]{:S(2)}) collective-permute-start(bf16[16,256,128]{2,1,0:T(8,128)(2,1)S(1)} %collective-permute-done.18.refs_10_), channel_id=1, source_target_pairs={{0,16},{1,17},{2,18},{3,19},{4,20},{5,21},{6,22},{7,23},{8,24},{9,... | collective-permute-start | bytes 3145736 | tf_op jit(solution)/shard_map/s_swap/ppermute | solution.py:50
  97.2 13.2 %collective-permute-start.22 = (bf16[16,256,128]{2,1,0:T(8,128)(2,1)S(1)}, bf16[16,256,128]{2,1,0:T(8,128)(2,1)S(1)}, u32[]{:S(2)}, u32[]{:S(2)}) collective-permute-start(bf16[16,256,128]{2,1,0:T(8,128)(2,1)S(1)} %copy-done.4), channel_id=1, source_target_pairs={{0,16},{1,17},{2,18},{3,19},{4,20},{5,21},{6,22},{7,23},{8,24},{9,... | collective-permute-start | bytes 3145736 | tf_op jit(solution)/shard_map/s_swap/ppermute | solution.py:50
  (20 other events, 154.4 us)

commit v3 on v2

--- a/solution.py
+++ b/solution.py
@@ -384,7 +384,7 @@
         in_specs=[pl.BlockSpec(memory_space=pltpu.SMEM)] + [pl.BlockSpec(memory_space=pltpu.HBM)] * 6,
         out_specs=pl.BlockSpec(memory_space=pltpu.VMEM),
         scratch_shapes=LEFT_SCRATCH,
-        compiler_params=pltpu.CompilerParams(vmem_limit_bytes=VMEM_LIMIT),
+        compiler_params=pltpu.CompilerParams(vmem_limit_bytes=16 << 20),
         cost_estimate=pl.CostEstimate(flops=9_000_000_000, bytes_accessed=7_000_000, transcendentals=0),
         name="left_of_slab",
     )(plan, *halves, panel)
@@ -419,7 +419,7 @@
             pltpu.SemaphoreType.DMA((2,)),
             pltpu.SemaphoreType.DMA,
         ] + LEFT_SCRATCH,
-        compiler_params=pltpu.CompilerParams(vmem_limit_bytes=VMEM_LIMIT),
+        compiler_params=pltpu.CompilerParams(vmem_limit_bytes=28 << 20),
         cost_estimate=pl.CostEstimate(flops=18_000_000_000, bytes_accessed=20_000_000, transcendentals=0),
         name="finish",
     )(plan, place, *halves, panel, *pieces, left)

time: 137 us -> 122 us (0.89)
  local copies, waits for them, and re-layouts: 11.6 us -> 1.34 us
  Pallas kernels: 43.1 us -> 35.4 us
  waiting for transfers between devices: 38.7 us -> 42.3 us
  starting transfers between devices: 41 us -> 39.3 us
    unnamed x40 -> x14, local copies, waits for them, and re-layouts: 7.6 us -> 0.14 us
    pallas_call x1, Pallas kernels: 24.2 us -> 20.2 us  [finish(): pl.pallas_call(finish_kernel, out_shape=jax.ShapeDtypeStruct((2, ROWS, AC...]
    pallas_call x1, Pallas kernels: 12.2 us -> 8.5 us  [left_of_slab(): pl.pallas_call(left_kernel, out_shape=jax.ShapeDtypeStruct((ROWS, NAO), j...]
    ppermute x26, waiting for transfers between devices: 38.2 us -> 40.5 us  [send(): return lax.ppermute(value, AXES, pairs)]
    ppermute x26, starting transfers between devices: 35.5 us -> 33.9 us  [send(): return lax.ppermute(value, AXES, pairs)]
    all_to_all x1, waiting for transfers between devices: 0.44 us -> 1.83 us  [body(): owned = lax.all_to_all(half, 'ao', split_axis=0, concat_axis=0, tiled=True)]
  transfers between devices with their start and end apart: 27 -> 27, of which waited for: 11 -> 11; matrix products, arithmetic and copies ran while one was open for 7% -> 2% of each run, Pallas kernels for 10% -> 9%
where the time goes in v3:
time: 122 us; the launch traced here: 120 us
  waiting for transfers between devices  42.3 us (35%)
  starting transfers between devices  39.3 us (32%)
  Pallas kernels  35.4 us (29%)
  local copies, waits for them, and re-layouts  1.34 us (1%)
    ppermute x26, waiting for transfers between devices, send(): return lax.ppermute(value, AXES, pairs)  40.5 us
    ppermute x26, starting transfers between devices, send(): return lax.ppermute(value, AXES, pairs)  33.9 us
    pallas_call x1, Pallas kernels, finish(): pl.pallas_call(finish_kernel, out_shape=jax.ShapeDtypeStruct((2, ROWS, AC...  20.2 us
    pallas_call x1, Pallas kernels, left_of_slab(): pl.pallas_call(left_kernel, out_shape=jax.ShapeDtypeStruct((ROWS, NAO), j...  8.5 us
    all_to_all x1, starting transfers between devices, body(): owned = lax.all_to_all(half, 'ao', split_axis=0, concat_axis=0, tiled=True)  5.41 us
    pallas_call x1, Pallas kernels, ket_transform(): pl.pallas_call(ket_kernel, out_shape=jax.ShapeDtypeStruct((NJ * 2 * SH, N...  4.64 us
  transfers between devices with their start and end apart: 27, of which 11 were waited for; matrix products, arithmetic and copies ran while one was open for 2% of the time, Pallas kernels for 9%

profile of v3, /device:TPU:0, one launch (start us, length us, event | category | flops | bytes accessed | tf_op | source)
XLA Modules:
  0.0 119.7 jit_solution(5232174534199636572)
XLA Ops:
  0.0 4.6 %ket_transform.1 = bf16[1024,256]{1,0:T(8,128)(2,1)} custom-call(s32[2]{0:T(128)} %slabs_ref.1, bf16[16,32]{1,0:T(8,128)(2,1)} %lam_ref.1, bf16[8,16]{1,0:T(8,128)(2,1)} %bitcast.40, bf16[1,4096,256]{2,1,0:T(8,128)(2,1)} %ints_hbm.1), custom_call_target="tpu_custom_call" | custom-call | flops 140000000 | bytes 3000000 | tf_op jit(solution)/shard_map/ket_transform/pallas_call | solution.py:126
  4.7 5.4 %all-to-all-start = ((bf16[8,2,64,256]{3,2,1,0:T(8,128)(2,1)}), bf16[8,2,64,256]{3,2,1,0:T(8,128)(2,1)S(1)}, u32[]{:S(2)}, u32[]{:S(2)}) async-start(bf16[8,2,64,256]{3,2,1,0:T(8,128)(2,1)} %bitcast.34), calls=%async_computation | async-start | bytes 1048576 | tf_op jit(solution)/shard_map/all_to_all | solution.py:438
  10.1 3.1 %collective-permute-start.13 = (bf16[256,128]{1,0:T(8,128)(2,1)S(1)}, bf16[256,128]{1,0:T(8,128)(2,1)S(1)}, u32[]{:S(2)}, u32[]{:S(2)}) collective-permute-start(bf16[256,128]{1,0:T(8,128)(2,1)S(1)} %get-tuple-element.32), channel_id=1, source_target_pairs={{0,8},{1,9},{2,10},{3,11},{4,12},{5,13},{6,14},{7,15},{8,0},{9,1},... | collective-permute-start | bytes 196616 | tf_op jit(solution)/shard_map/s_c1/ppermute | solution.py:50
  16.6 2.0 %plan_terms.1.refs_0_ = s32[8,256]{1,0:T(8,128)} custom-call(s32[4]{0:T(128)} %pad_add_fusion.place_ref.refs_1_, s32[128,2]{1,0:T(8,128)} %copy.12.pairs_ref, s32[2,128]{1,0:T(2,128)} %bitcast.39), custom_call_target="tpu_custom_call" | custom-call | flops 2000000 | bytes 10000 | tf_op jit(solution)/shard_map/plan_terms/pallas_call | solution.py:206
  18.6 1.8 %all-to-all-done = bf16[8,2,64,256]{3,2,1,0:T(8,128)(2,1)S(1)} async-done(((bf16[8,2,64,256]{3,2,1,0:T(8,128)(2,1)}), bf16[8,2,64,256]{3,2,1,0:T(8,128)(2,1)S(1)}, u32[]{:S(2)}, u32[]{:S(2)}) %all-to-all-start) | async-done | bytes 524320 | tf_op jit(solution)/shard_map/all_to_all | solution.py:438
  20.5 2.8 %collective-permute-start.1 = (bf16[8,2,64,256]{3,2,0,1:T(8,128)(2,1)S(1)}, bf16[8,2,64,256]{3,2,0,1:T(8,128)(2,1)S(1)}, u32[]{:S(2)}, u32[]{:S(2)}) collective-permute-start(bf16[8,2,64,256]{3,2,0,1:T(8,128)(2,1)S(1)} %copy.13), channel_id=1, source_target_pairs={{0,12},{1,13},{2,14},{3,15},{4,0},{5,1},{6,2},{7,3},{8,4},{9,5},{1... | collective-permute-start | bytes 1572872 | tf_op jit(solution)/shard_map/s_p1/ppermute | solution.py:50
  23.3 3.3 %collective-permute-start.16 = (bf16[4,256,128]{2,1,0:T(8,128)(2,1)S(1)}, bf16[4,256,128]{2,1,0:T(8,128)(2,1)S(1)}, u32[]{:S(2)}, u32[]{:S(2)}) collective-permute-start(bf16[4,256,128]{2,1,0:T(8,128)(2,1)S(1)} %pad_maximum_fusion.2), channel_id=1, source_target_pairs={{0,2},{1,3},{2,0},{3,1},{4,6},{5,7},{6,4},{7,5},{8,10},{9,11},{10,... | collective-permute-start | bytes 786440 | tf_op jit(solution)/shard_map/s_c2/ppermute | solution.py:50
  27.7 2.4 %collective-permute-start.2 = (bf16[8,2,64,256]{3,2,0,1:T(8,128)(2,1)S(1)}, bf16[8,2,64,256]{3,2,0,1:T(8,128)(2,1)S(1)}, u32[]{:S(2)}, u32[]{:S(2)}) collective-permute-start(bf16[8,2,64,256]{3,2,0,1:T(8,128)(2,1)S(1)} %copy.13), channel_id=1, source_target_pairs={{0,8},{1,9},{2,10},{3,11},{4,12},{5,13},{6,14},{7,15},{8,0},{9,1},... | collective-permute-start | bytes 1572872 | tf_op jit(solution)/shard_map/s_p1/ppermute | solution.py:50
  30.1 11.1 %collective-permute-done.1 = bf16[8,2,64,256]{3,2,0,1:T(8,128)(2,1)S(1)} collective-permute-done((bf16[8,2,64,256]{3,2,0,1:T(8,128)(2,1)S(1)}, bf16[8,2,64,256]{3,2,0,1:T(8,128)(2,1)S(1)}, u32[]{:S(2)}, u32[]{:S(2)}) %collective-permute-start.1) | collective-permute-done | bytes 524320 | tf_op jit(solution)/shard_map/s_p1/ppermute | solution.py:50
  42.5 1.4 %collective-permute-done = bf16[8,2,64,256]{3,2,0,1:T(8,128)(2,1)S(1)} collective-permute-done((bf16[8,2,64,256]{3,2,0,1:T(8,128)(2,1)S(1)}, bf16[8,2,64,256]{3,2,0,1:T(8,128)(2,1)S(1)}, u32[]{:S(2)}, u32[]{:S(2)}) %collective-permute-start) | collective-permute-done | bytes 524320 | tf_op jit(solution)/shard_map/s_p1/ppermute | solution.py:50
  44.8 2.1 %collective-permute-start.3 = (bf16[32,64,256]{2,1,0:T(8,128)(2,1)S(1)}, bf16[32,64,256]{2,1,0:T(8,128)(2,1)S(1)}, u32[]{:S(2)}, u32[]{:S(2)}) collective-permute-start(bf16[32,64,256]{2,1,0:T(8,128)(2,1)S(1)} %pad_maximum_fusion.1.refs_1_), channel_id=1, source_target_pairs={{0,1},{1,2},{2,3},{3,0},{4,5},{5,6},{6,7},{7,4},{8,9},{9,10},{10,1... | collective-permute-start | bytes 3145736 | tf_op jit(solution)/shard_map/s_p2a/ppermute | solution.py:50
  47.0 1.8 %collective-permute-done.14 = bf16[4,256,128]{2,1,0:T(8,128)(2,1)S(1)} collective-permute-done((bf16[4,256,128]{2,1,0:T(8,128)(2,1)S(1)}, bf16[4,256,128]{2,1,0:T(8,128)(2,1)S(1)}, u32[]{:S(2)}, u32[]{:S(2)}) %collective-permute-start.14) | collective-permute-done | bytes 262176 | tf_op jit(solution)/shard_map/s_c2/ppermute | solution.py:50
  51.0 8.6 %collective-permute-done.4.refs_3_ = bf16[32,64,256]{2,1,0:T(8,128)(2,1)S(1)} collective-permute-done((bf16[32,64,256]{2,1,0:T(8,128)(2,1)S(1)}, bf16[32,64,256]{2,1,0:T(8,128)(2,1)S(1)}, u32[]{:S(2)}, u32[]{:S(2)}) %collective-permute-start.4) | collective-permute-done | bytes 1048608 | tf_op jit(solution)/shard_map/s_p2a/ppermute | solution.py:50
  62.1 2.5 %collective-permute-start.6 = (bf16[32,64,256]{2,1,0:T(8,128)(2,1)S(1)}, bf16[32,64,256]{2,1,0:T(8,128)(2,1)S(1)}, u32[]{:S(2)}, u32[]{:S(2)}) collective-permute-start(bf16[32,64,256]{2,1,0:T(8,128)(2,1)S(1)} %pad_maximum_fusion.refs_2_), channel_id=1, source_target_pairs={{0,3},{1,0},{2,1},{3,2},{4,7},{5,4},{6,5},{7,6},{8,11},{9,8},{10,9... | collective-permute-start | bytes 3145736 | tf_op jit(solution)/shard_map/s_p2b/ppermute | solution.py:50
  64.5 4.4 %collective-permute-done.8.refs_5_ = bf16[16,64,256]{2,1,0:T(8,128)(2,1)S(1)} collective-permute-done((bf16[16,64,256]{2,1,0:T(8,128)(2,1)S(1)}, bf16[16,64,256]{2,1,0:T(8,128)(2,1)S(1)}, u32[]{:S(2)}, u32[]{:S(2)}) %collective-permute-start.8) | collective-permute-done | bytes 524320 | tf_op jit(solution)/shard_map/s_f2a/ppermute | solution.py:50
  69.0 2.0 %collective-permute-start.5 = (bf16[32,64,256]{2,1,0:T(8,128)(2,1)S(1)}, bf16[32,64,256]{2,1,0:T(8,128)(2,1)S(1)}, u32[]{:S(2)}, u32[]{:S(2)}) collective-permute-start(bf16[32,64,256]{2,1,0:T(8,128)(2,1)S(1)} %pad_maximum_fusion.refs_2_), channel_id=1, source_target_pairs={{0,1},{1,2},{2,3},{3,0},{4,5},{5,6},{6,7},{7,4},{8,9},{9,10},{10,1... | collective-permute-start | bytes 3145736 | tf_op jit(solution)/shard_map/s_p2b/ppermute | solution.py:50
  71.9 2.4 %collective-permute-start.20 = (bf16[8,256,128]{2,1,0:T(8,128)(2,1)S(1)}, bf16[8,256,128]{2,1,0:T(8,128)(2,1)S(1)}, u32[]{:S(2)}, u32[]{:S(2)}) collective-permute-start(bf16[8,256,128]{2,1,0:T(8,128)(2,1)S(1)} %slice.55), channel_id=1, source_target_pairs={{0,96},{1,97},{2,98},{3,99},{4,100},{5,101},{6,102},{7,103},{8,104... | collective-permute-start | bytes 1572872 | tf_op jit(solution)/shard_map/s_zf/ppermute | solution.py:50
  74.5 8.5 %left_of_slab.1.refs_18_ = bf16[512,2048]{1,0:T(8,128)(2,1)S(1)} custom-call(s32[8,256]{1,0:T(8,128)S(1)} %copy-done.1, bf16[32,64,256]{2,1,0:T(8,128)(2,1)S(1)} %pad_maximum_fusion.1.refs_1_, bf16[32,64,256]{2,1,0:T(8,128)(2,1)S(1)} %collective-permute-done.3.refs_2_, bf16[32,64,256]{2,1,0:T(8,128)(2,1)S(1)} %collective-permute-done.4.refs_3_, ...), custom_call_target="tpu_custom_call" | custom-call | flops 8999999488 | bytes 7000000 | tf_op jit(solution)/shard_map/left_of_slab/pallas_call | solution.py:381
  83.1 3.6 %collective-permute-start.10 = (bf16[16,64,256]{2,1,0:T(8,128)(2,1)S(1)}, bf16[16,64,256]{2,1,0:T(8,128)(2,1)S(1)}, u32[]{:S(2)}, u32[]{:S(2)}) collective-permute-start(bf16[16,64,256]{2,1,0:T(8,128)(2,1)S(1)} %slice.53), channel_id=1, source_target_pairs={{0,3},{1,0},{2,1},{3,2},{4,7},{5,4},{6,5},{7,6},{8,11},{9,8},{10,9... | collective-permute-start | bytes 1572872 | tf_op jit(solution)/shard_map/s_f2b/ppermute | solution.py:50
  87.1 2.7 %collective-permute-done.19.refs_11_ = bf16[8,256,128]{2,1,0:T(8,128)(2,1)S(1)} collective-permute-done((bf16[8,256,128]{2,1,0:T(8,128)(2,1)S(1)}, bf16[8,256,128]{2,1,0:T(8,128)(2,1)S(1)}, u32[]{:S(2)}, u32[]{:S(2)}) %collective-permute-start.19) | collective-permute-done | bytes 524320 | tf_op jit(solution)/shard_map/s_zf/ppermute | solution.py:50
  89.8 3.6 %collective-permute-done.10.refs_6_ = bf16[16,64,256]{2,1,0:T(8,128)(2,1)S(1)} collective-permute-done((bf16[16,64,256]{2,1,0:T(8,128)(2,1)S(1)}, bf16[16,64,256]{2,1,0:T(8,128)(2,1)S(1)}, u32[]{:S(2)}, u32[]{:S(2)}) %collective-permute-start.10) | collective-permute-done | bytes 524320 | tf_op jit(solution)/shard_map/s_f2b/ppermute | solution.py:50
  93.4 4.0 %collective-permute-done.9.refs_5_ = bf16[16,64,256]{2,1,0:T(8,128)(2,1)S(1)} collective-permute-done((bf16[16,64,256]{2,1,0:T(8,128)(2,1)S(1)}, bf16[16,64,256]{2,1,0:T(8,128)(2,1)S(1)}, u32[]{:S(2)}, u32[]{:S(2)}) %collective-permute-start.9) | collective-permute-done | bytes 524320 | tf_op jit(solution)/shard_map/s_f2b/ppermute | solution.py:50
  97.4 1.9 %collective-permute-done.24.refs_16_ = bf16[8,256,128]{2,1,0:T(8,128)(2,1)S(1)} collective-permute-done((bf16[8,256,128]{2,1,0:T(8,128)(2,1)S(1)}, bf16[8,256,128]{2,1,0:T(8,128)(2,1)S(1)}, u32[]{:S(2)}, u32[]{:S(2)}) %collective-permute-start.24) | collective-permute-done | bytes 524320 | tf_op jit(solution)/shard_map/s_swap/ppermute | solution.py:50
  99.3 20.2 %finish.1 = bf16[2,512,2048]{2,1,0:T(8,128)(2,1)} custom-call(s32[8,256]{1,0:T(8,128)S(1)} %copy-done.1, s32[4]{0:T(128)S(1)} %copy-done.2, bf16[32,64,256]{2,1,0:T(8,128)(2,1)S(1)} %pad_maximum_fusion.refs_2_, bf16[32,64,256]{2,1,0:T(8,128)(2,1)S(1)} %collective-permute-done.5.refs_3_, bf16[32,64,256]{2,1,0:T(8,128)(2,1)S(1)} %collective-permute-done.6.refs_4_, ...), custom_call_target="tpu_custom_call" | custom-call | flops 17999998976 | bytes 20000000 | tf_op jit(solution)/shard_map/finish/pallas_call | solution.py:409
  (65 shorter events, 12.9 us)
Async XLA Ops:
  4.7 15.8 %all-to-all-start = ((bf16[8,2,64,256]{3,2,1,0:T(8,128)(2,1)}), bf16[8,2,64,256]{3,2,1,0:T(8,128)(2,1)S(1)}, u32[]{:S(2)}, u32[]{:S(2)}) async-start(bf16[8,2,64,256]{3,2,1,0:T(8,128)(2,1)} %bitcast.34), calls=%async_computation | async-start | bytes 1048576 | tf_op jit(solution)/shard_map/all_to_all | solution.py:438
  10.1 13.2 %collective-permute-start.13 = (bf16[256,128]{1,0:T(8,128)(2,1)S(1)}, bf16[256,128]{1,0:T(8,128)(2,1)S(1)}, u32[]{:S(2)}, u32[]{:S(2)}) collective-permute-start(bf16[256,128]{1,0:T(8,128)(2,1)S(1)} %get-tuple-element.32), channel_id=1, source_target_pairs={{0,8},{1,9},{2,10},{3,11},{4,12},{5,13},{6,14},{7,15},{8,0},{9,1},... | collective-permute-start | bytes 196616 | tf_op jit(solution)/shard_map/s_c1/ppermute | solution.py:50
  13.2 10.1 %collective-permute-start.12 = (bf16[256,128]{1,0:T(8,128)(2,1)S(1)}, bf16[256,128]{1,0:T(8,128)(2,1)S(1)}, u32[]{:S(2)}, u32[]{:S(2)}) collective-permute-start(bf16[256,128]{1,0:T(8,128)(2,1)S(1)} %get-tuple-element.32), channel_id=1, source_target_pairs={{0,12},{1,13},{2,14},{3,15},{4,0},{5,1},{6,2},{7,3},{8,4},{9,5},{1... | collective-permute-start | bytes 196616 | tf_op jit(solution)/shard_map/s_c1/ppermute | solution.py:50
  14.3 9.0 %collective-permute-start.11 = (bf16[256,128]{1,0:T(8,128)(2,1)S(1)}, bf16[256,128]{1,0:T(8,128)(2,1)S(1)}, u32[]{:S(2)}, u32[]{:S(2)}) collective-permute-start(bf16[256,128]{1,0:T(8,128)(2,1)S(1)} %get-tuple-element.32), channel_id=1, source_target_pairs={{0,4},{1,5},{2,6},{3,7},{4,8},{5,9},{6,10},{7,11},{8,12},{9,13},{1... | collective-permute-start | bytes 196616 | tf_op jit(solution)/shard_map/s_c1/ppermute | solution.py:50
  20.5 20.8 %collective-permute-start.1 = (bf16[8,2,64,256]{3,2,0,1:T(8,128)(2,1)S(1)}, bf16[8,2,64,256]{3,2,0,1:T(8,128)(2,1)S(1)}, u32[]{:S(2)}, u32[]{:S(2)}) collective-permute-start(bf16[8,2,64,256]{3,2,0,1:T(8,128)(2,1)S(1)} %copy.13), channel_id=1, source_target_pairs={{0,12},{1,13},{2,14},{3,15},{4,0},{5,1},{6,2},{7,3},{8,4},{9,5},{1... | collective-permute-start | bytes 1572872 | tf_op jit(solution)/shard_map/s_p1/ppermute | solution.py:50
  23.3 25.6 %collective-permute-start.16 = (bf16[4,256,128]{2,1,0:T(8,128)(2,1)S(1)}, bf16[4,256,128]{2,1,0:T(8,128)(2,1)S(1)}, u32[]{:S(2)}, u32[]{:S(2)}) collective-permute-start(bf16[4,256,128]{2,1,0:T(8,128)(2,1)S(1)} %pad_maximum_fusion.2), channel_id=1, source_target_pairs={{0,2},{1,3},{2,0},{3,1},{4,6},{5,7},{6,4},{7,5},{8,10},{9,11},{10,... | collective-permute-start | bytes 786440 | tf_op jit(solution)/shard_map/s_c2/ppermute | solution.py:50
  26.6 22.2 %collective-permute-start.15 = (bf16[4,256,128]{2,1,0:T(8,128)(2,1)S(1)}, bf16[4,256,128]{2,1,0:T(8,128)(2,1)S(1)}, u32[]{:S(2)}, u32[]{:S(2)}) collective-permute-start(bf16[4,256,128]{2,1,0:T(8,128)(2,1)S(1)} %pad_maximum_fusion.2), channel_id=1, source_target_pairs={{0,3},{1,0},{2,1},{3,2},{4,7},{5,4},{6,5},{7,6},{8,11},{9,8},{10,9... | collective-permute-start | bytes 786440 | tf_op jit(solution)/shard_map/s_c2/ppermute | solution.py:50
  27.7 16.3 %collective-permute-start = (bf16[8,2,64,256]{3,2,0,1:T(8,128)(2,1)S(1)}, bf16[8,2,64,256]{3,2,0,1:T(8,128)(2,1)S(1)}, u32[]{:S(2)}, u32[]{:S(2)}) collective-permute-start(bf16[8,2,64,256]{3,2,0,1:T(8,128)(2,1)S(1)} %copy.13), channel_id=1, source_target_pairs={{0,4},{1,5},{2,6},{3,7},{4,8},{5,9},{6,10},{7,11},{8,12},{9,13},{1... | collective-permute-start | bytes 1572872 | tf_op jit(solution)/shard_map/s_p1/ppermute | solution.py:50
  27.7 16.3 %collective-permute-start.2 = (bf16[8,2,64,256]{3,2,0,1:T(8,128)(2,1)S(1)}, bf16[8,2,64,256]{3,2,0,1:T(8,128)(2,1)S(1)}, u32[]{:S(2)}, u32[]{:S(2)}) collective-permute-start(bf16[8,2,64,256]{3,2,0,1:T(8,128)(2,1)S(1)} %copy.13), channel_id=1, source_target_pairs={{0,8},{1,9},{2,10},{3,11},{4,12},{5,13},{6,14},{7,15},{8,0},{9,1},... | collective-permute-start | bytes 1572872 | tf_op jit(solution)/shard_map/s_p1/ppermute | solution.py:50
  44.2 15.5 %collective-permute-start.4 = (bf16[32,64,256]{2,1,0:T(8,128)(2,1)S(1)}, bf16[32,64,256]{2,1,0:T(8,128)(2,1)S(1)}, u32[]{:S(2)}, u32[]{:S(2)}) collective-permute-start(bf16[32,64,256]{2,1,0:T(8,128)(2,1)S(1)} %pad_maximum_fusion.1.refs_1_), channel_id=1, source_target_pairs={{0,3},{1,0},{2,1},{3,2},{4,7},{5,4},{6,5},{7,6},{8,11},{9,8},{10,9... | collective-permute-start | bytes 3145736 | tf_op jit(solution)/shard_map/s_p2a/ppermute | solution.py:50
  44.8 16.1 %collective-permute-start.3 = (bf16[32,64,256]{2,1,0:T(8,128)(2,1)S(1)}, bf16[32,64,256]{2,1,0:T(8,128)(2,1)S(1)}, u32[]{:S(2)}, u32[]{:S(2)}) collective-permute-start(bf16[32,64,256]{2,1,0:T(8,128)(2,1)S(1)} %pad_maximum_fusion.1.refs_1_), channel_id=1, source_target_pairs={{0,1},{1,2},{2,3},{3,0},{4,5},{5,6},{6,7},{7,4},{8,9},{9,10},{10,1... | collective-permute-start | bytes 3145736 | tf_op jit(solution)/shard_map/s_p2a/ppermute | solution.py:50
  48.9 22.9 %collective-permute-start.18 = (bf16[16,256,128]{2,1,0:T(8,128)(2,1)S(1)}, bf16[16,256,128]{2,1,0:T(8,128)(2,1)S(1)}, u32[]{:S(2)}, u32[]{:S(2)}) collective-permute-start(bf16[16,256,128]{2,1,0:T(8,128)(2,1)S(1)} %constant_dynamic-update-slice_fusion.refs_8_), channel_id=1, source_target_pairs={{0,96},{1,97},{2,98},{3,99},{4,100},{5,101},{6,102},{7,103},{8,104... | collective-permute-start | bytes 3145736 | tf_op jit(solution)/shard_map/s_z1/ppermute | solution.py:50
  50.2 24.2 %collective-permute-start.17 = (bf16[16,256,128]{2,1,0:T(8,128)(2,1)S(1)}, bf16[16,256,128]{2,1,0:T(8,128)(2,1)S(1)}, u32[]{:S(2)}, u32[]{:S(2)}) collective-permute-start(bf16[16,256,128]{2,1,0:T(8,128)(2,1)S(1)} %constant_dynamic-update-slice_fusion.refs_8_), channel_id=1, source_target_pairs={{0,32},{1,33},{2,34},{3,35},{4,36},{5,37},{6,38},{7,39},{8,40},{9,... | collective-permute-start | bytes 3145736 | tf_op jit(solution)/shard_map/s_z1/ppermute | solution.py:50
  59.7 9.2 %collective-permute-start.8 = (bf16[16,64,256]{2,1,0:T(8,128)(2,1)S(1)}, bf16[16,64,256]{2,1,0:T(8,128)(2,1)S(1)}, u32[]{:S(2)}, u32[]{:S(2)}) collective-permute-start(bf16[16,64,256]{2,1,0:T(8,128)(2,1)S(1)} %slice.65), channel_id=1, source_target_pairs={{0,3},{1,0},{2,1},{3,2},{4,7},{5,4},{6,5},{7,6},{8,11},{9,8},{10,9... | collective-permute-start | bytes 1572872 | tf_op jit(solution)/shard_map/s_f2a/ppermute | solution.py:50
  61.0 10.9 %collective-permute-start.7 = (bf16[16,64,256]{2,1,0:T(8,128)(2,1)S(1)}, bf16[16,64,256]{2,1,0:T(8,128)(2,1)S(1)}, u32[]{:S(2)}, u32[]{:S(2)}) collective-permute-start(bf16[16,64,256]{2,1,0:T(8,128)(2,1)S(1)} %slice.64), channel_id=1, source_target_pairs={{0,1},{1,2},{2,3},{3,0},{4,5},{5,6},{6,7},{7,4},{8,9},{9,10},{10,1... | collective-permute-start | bytes 1572872 | tf_op jit(solution)/shard_map/s_f2a/ppermute | solution.py:50
  62.1 21.0 %collective-permute-start.6 = (bf16[32,64,256]{2,1,0:T(8,128)(2,1)S(1)}, bf16[32,64,256]{2,1,0:T(8,128)(2,1)S(1)}, u32[]{:S(2)}, u32[]{:S(2)}) collective-permute-start(bf16[32,64,256]{2,1,0:T(8,128)(2,1)S(1)} %pad_maximum_fusion.refs_2_), channel_id=1, source_target_pairs={{0,3},{1,0},{2,1},{3,2},{4,7},{5,4},{6,5},{7,6},{8,11},{9,8},{10,9... | collective-permute-start | bytes 3145736 | tf_op jit(solution)/shard_map/s_p2b/ppermute | solution.py:50
  69.0 17.7 %collective-permute-start.5 = (bf16[32,64,256]{2,1,0:T(8,128)(2,1)S(1)}, bf16[32,64,256]{2,1,0:T(8,128)(2,1)S(1)}, u32[]{:S(2)}, u32[]{:S(2)}) collective-permute-start(bf16[32,64,256]{2,1,0:T(8,128)(2,1)S(1)} %pad_maximum_fusion.refs_2_), channel_id=1, source_target_pairs={{0,1},{1,2},{2,3},{3,0},{4,5},{5,6},{6,7},{7,4},{8,9},{9,10},{10,1... | collective-permute-start | bytes 3145736 | tf_op jit(solution)/shard_map/s_p2b/ppermute | solution.py:50
  71.9 25.5 %collective-permute-start.21 = (bf16[16,256,128]{2,1,0:T(8,128)(2,1)S(1)}, bf16[16,256,128]{2,1,0:T(8,128)(2,1)S(1)}, u32[]{:S(2)}, u32[]{:S(2)}) collective-permute-start(bf16[16,256,128]{2,1,0:T(8,128)(2,1)S(1)} %constant_dynamic-update-slice_fusion.refs_8_), channel_id=1, source_target_pairs={{0,16},{1,17},{2,18},{3,19},{4,20},{5,21},{6,22},{7,23},{8,24},{9,... | collective-permute-start | bytes 3145736 | tf_op jit(solution)/shard_map/s_swap/ppermute | solution.py:50
  71.9 15.1 %collective-permute-start.20 = (bf16[8,256,128]{2,1,0:T(8,128)(2,1)S(1)}, bf16[8,256,128]{2,1,0:T(8,128)(2,1)S(1)}, u32[]{:S(2)}, u32[]{:S(2)}) collective-permute-start(bf16[8,256,128]{2,1,0:T(8,128)(2,1)S(1)} %slice.55), channel_id=1, source_target_pairs={{0,96},{1,97},{2,98},{3,99},{4,100},{5,101},{6,102},{7,103},{8,104... | collective-permute-start | bytes 1572872 | tf_op jit(solution)/shard_map/s_zf/ppermute | solution.py:50
  74.4 15.3 %collective-permute-start.19 = (bf16[8,256,128]{2,1,0:T(8,128)(2,1)S(1)}, bf16[8,256,128]{2,1,0:T(8,128)(2,1)S(1)}, u32[]{:S(2)}, u32[]{:S(2)}) collective-permute-start(bf16[8,256,128]{2,1,0:T(8,128)(2,1)S(1)} %slice.54), channel_id=1, source_target_pairs={{0,32},{1,33},{2,34},{3,35},{4,36},{5,37},{6,38},{7,39},{8,40},{9,... | collective-permute-start | bytes 1572872 | tf_op jit(solution)/shard_map/s_zf/ppermute | solution.py:50
  83.1 10.3 %collective-permute-start.10 = (bf16[16,64,256]{2,1,0:T(8,128)(2,1)S(1)}, bf16[16,64,256]{2,1,0:T(8,128)(2,1)S(1)}, u32[]{:S(2)}, u32[]{:S(2)}) collective-permute-start(bf16[16,64,256]{2,1,0:T(8,128)(2,1)S(1)} %slice.53), channel_id=1, source_target_pairs={{0,3},{1,0},{2,1},{3,2},{4,7},{5,4},{6,5},{7,6},{8,11},{9,8},{10,9... | collective-permute-start | bytes 1572872 | tf_op jit(solution)/shard_map/s_f2b/ppermute | solution.py:50
  86.7 10.6 %collective-permute-start.9 = (bf16[16,64,256]{2,1,0:T(8,128)(2,1)S(1)}, bf16[16,64,256]{2,1,0:T(8,128)(2,1)S(1)}, u32[]{:S(2)}, u32[]{:S(2)}) collective-permute-start(bf16[16,64,256]{2,1,0:T(8,128)(2,1)S(1)} %slice.52), channel_id=1, source_target_pairs={{0,1},{1,2},{2,3},{3,0},{4,5},{5,6},{6,7},{7,4},{8,9},{9,10},{10,1... | collective-permute-start | bytes 1572872 | tf_op jit(solution)/shard_map/s_f2b/ppermute | solution.py:50
  87.0 10.4 %collective-permute-start.23 = (bf16[16,256,128]{2,1,0:T(8,128)(2,1)S(1)}, bf16[16,256,128]{2,1,0:T(8,128)(2,1)S(1)}, u32[]{:S(2)}, u32[]{:S(2)}) collective-permute-start(bf16[16,256,128]{2,1,0:T(8,128)(2,1)S(1)} %collective-permute-done.18.refs_10_), channel_id=1, source_target_pairs={{0,16},{1,17},{2,18},{3,19},{4,20},{5,21},{6,22},{7,23},{8,24},{9,... | collective-permute-start | bytes 3145736 | tf_op jit(solution)/shard_map/s_swap/ppermute | solution.py:50
  89.8 9.5 %collective-permute-start.22 = (bf16[16,256,128]{2,1,0:T(8,128)(2,1)S(1)}, bf16[16,256,128]{2,1,0:T(8,128)(2,1)S(1)}, u32[]{:S(2)}, u32[]{:S(2)}) collective-permute-start(bf16[16,256,128]{2,1,0:T(8,128)(2,1)S(1)} %collective-permute-done.17.refs_9_), channel_id=1, source_target_pairs={{0,16},{1,17},{2,18},{3,19},{4,20},{5,21},{6,22},{7,23},{8,24},{9,... | collective-permute-start | bytes 3145736 | tf_op jit(solution)/shard_map/s_swap/ppermute | solution.py:50
  (7 other events, 67.6 us)

commit v4 on v3

--- a/solution.py
+++ b/solution.py
@@ -218,7 +218,7 @@
     )(place, shell_pairs, shell_pairs.T)
 
 
-UNROLL = 8
+UNROLL = 14
 FIRSTS = (0, 32, 64, 96, 112, 128)
 
 
@@ -279,16 +279,16 @@
             preferred_element_type=jnp.float32,
         )
 
-    for kind in range(2):
-        steps = (plan_ref[2 + kind, NBLK] + UNROLL - 1) // UNROLL
-
-        @pl.loop(0, steps)
-        def _(step):
-            for u in range(UNROLL):
+    most = jnp.maximum(plan_ref[2, NBLK], plan_ref[3, NBLK])
+
+    @pl.loop(0, (most + UNROLL - 1) // UNROLL)
+    def _(step):
+        for u in range(UNROLL):
+            for kind in range(2):
                 target, sums = terms(kind, step * UNROLL + u)
                 acc[target] += sums
 
-    @pl.loop(0, NSH // 2)
+    @pl.loop(0, NSH // 2, unroll=4)
     def _(t):
         for rp in range(2):
             even = acc[2 * t, :, rp * 128:rp * 128 + 128]
@@ -348,7 +348,7 @@
             sem_out.at[slot],
         )
 
-    @pl.loop(0, ACT // 256)
+    @pl.loop(0, ACT // 256, unroll=2)
     def _(n):
         slot = n % 2
 
@@ -436,7 +436,7 @@
 
     half = ket_transform(pair_ints, occ_lam, occ_sig, slabs)
     owned = lax.all_to_all(half, "ao", split_axis=0, concat_axis=0, tiled=True)
-    chunk = lax.dynamic_slice_in_dim(after(coef_act, half), ao_index * 256, 256, 0)
+    chunk = lax.dynamic_slice_in_dim(coef_act, ao_index * 256, 256, 0)
     with jax.named_scope("s_c1"):
         row = jnp.stack(direct(chunk, 0))
     with jax.named_scope("s_c2"):

time: 122 us -> 119 us (0.975)
  Pallas kernels: 35.4 us -> 33.5 us
  transfers between devices with their start and end apart: 27 -> 27, of which waited for: 11 -> 12; matrix products, arithmetic and copies ran while one was open for 2% -> 2% of each run, Pallas kernels for 9% -> 8%
where the time goes in v4:
time: 119 us; the launch traced here: 118 us
  waiting for transfers between devices  42.4 us (36%)
  starting transfers between devices  39.2 us (33%)
  Pallas kernels  33.5 us (28%)
  local copies, waits for them, and re-layouts  1.34 us (1%)
    ppermute x26, waiting for transfers between devices, send(): return lax.ppermute(value, AXES, pairs)  40.6 us
    ppermute x26, starting transfers between devices, send(): return lax.ppermute(value, AXES, pairs)  33.8 us
    pallas_call x1, Pallas kernels, finish(): pl.pallas_call(finish_kernel, out_shape=jax.ShapeDtypeStruct((2, ROWS, AC...  19.3 us
    pallas_call x1, Pallas kernels, left_of_slab(): pl.pallas_call(left_kernel, out_shape=jax.ShapeDtypeStruct((ROWS, NAO), j...  7.58 us
    all_to_all x1, starting transfers between devices, body(): owned = lax.all_to_all(half, 'ao', split_axis=0, concat_axis=0, tiled=True)  5.41 us
    pallas_call x1, Pallas kernels, ket_transform(): pl.pallas_call(ket_kernel, out_shape=jax.ShapeDtypeStruct((NJ * 2 * SH, N...  4.64 us
  transfers between devices with their start and end apart: 27, of which 12 were waited for; matrix products, arithmetic and copies ran while one was open for 2% of the time, Pallas kernels for 8%

profile of v4, /device:TPU:0, one launch (start us, length us, event | category | flops | bytes accessed | tf_op | source)
XLA Modules:
  0.0 117.8 jit_solution(15073824922496837255)
XLA Ops:
  0.0 4.6 %ket_transform.1 = bf16[1024,256]{1,0:T(8,128)(2,1)} custom-call(s32[2]{0:T(128)} %slabs_ref.1, bf16[16,32]{1,0:T(8,128)(2,1)} %lam_ref.1, bf16[8,16]{1,0:T(8,128)(2,1)} %bitcast.40, bf16[1,4096,256]{2,1,0:T(8,128)(2,1)} %ints_hbm.1), custom_call_target="tpu_custom_call" | custom-call | flops 140000000 | bytes 3000000 | tf_op jit(solution)/shard_map/ket_transform/pallas_call | solution.py:126
  4.7 5.4 %all-to-all-start = ((bf16[8,2,64,256]{3,2,1,0:T(8,128)(2,1)}), bf16[8,2,64,256]{3,2,1,0:T(8,128)(2,1)S(1)}, u32[]{:S(2)}, u32[]{:S(2)}) async-start(bf16[8,2,64,256]{3,2,1,0:T(8,128)(2,1)} %bitcast.34), calls=%async_computation | async-start | bytes 1048576 | tf_op jit(solution)/shard_map/all_to_all | solution.py:438
  10.1 3.1 %collective-permute-start.13 = (bf16[256,128]{1,0:T(8,128)(2,1)S(1)}, bf16[256,128]{1,0:T(8,128)(2,1)S(1)}, u32[]{:S(2)}, u32[]{:S(2)}) collective-permute-start(bf16[256,128]{1,0:T(8,128)(2,1)S(1)} %get-tuple-element.30), channel_id=1, source_target_pairs={{0,8},{1,9},{2,10},{3,11},{4,12},{5,13},{6,14},{7,15},{8,0},{9,1},... | collective-permute-start | bytes 196616 | tf_op jit(solution)/shard_map/s_c1/ppermute | solution.py:50
  16.6 2.0 %plan_terms.1.refs_0_ = s32[8,256]{1,0:T(8,128)} custom-call(s32[4]{0:T(128)} %pad_add_fusion.place_ref.refs_1_, s32[128,2]{1,0:T(8,128)} %copy.12.pairs_ref, s32[2,128]{1,0:T(2,128)} %bitcast.39), custom_call_target="tpu_custom_call" | custom-call | flops 2000000 | bytes 10000 | tf_op jit(solution)/shard_map/plan_terms/pallas_call | solution.py:206
  18.6 1.8 %all-to-all-done = bf16[8,2,64,256]{3,2,1,0:T(8,128)(2,1)S(1)} async-done(((bf16[8,2,64,256]{3,2,1,0:T(8,128)(2,1)}), bf16[8,2,64,256]{3,2,1,0:T(8,128)(2,1)S(1)}, u32[]{:S(2)}, u32[]{:S(2)}) %all-to-all-start) | async-done | bytes 524320 | tf_op jit(solution)/shard_map/all_to_all | solution.py:438
  20.5 2.8 %collective-permute-start.1 = (bf16[8,2,64,256]{3,2,0,1:T(8,128)(2,1)S(1)}, bf16[8,2,64,256]{3,2,0,1:T(8,128)(2,1)S(1)}, u32[]{:S(2)}, u32[]{:S(2)}) collective-permute-start(bf16[8,2,64,256]{3,2,0,1:T(8,128)(2,1)S(1)} %copy.13), channel_id=1, source_target_pairs={{0,12},{1,13},{2,14},{3,15},{4,0},{5,1},{6,2},{7,3},{8,4},{9,5},{1... | collective-permute-start | bytes 1572872 | tf_op jit(solution)/shard_map/s_p1/ppermute | solution.py:50
  23.3 3.3 %collective-permute-start.16 = (bf16[4,256,128]{2,1,0:T(8,128)(2,1)S(1)}, bf16[4,256,128]{2,1,0:T(8,128)(2,1)S(1)}, u32[]{:S(2)}, u32[]{:S(2)}) collective-permute-start(bf16[4,256,128]{2,1,0:T(8,128)(2,1)S(1)} %pad_maximum_fusion.2), channel_id=1, source_target_pairs={{0,2},{1,3},{2,0},{3,1},{4,6},{5,7},{6,4},{7,5},{8,10},{9,11},{10,... | collective-permute-start | bytes 786440 | tf_op jit(solution)/shard_map/s_c2/ppermute | solution.py:50
  27.7 2.4 %collective-permute-start.2 = (bf16[8,2,64,256]{3,2,0,1:T(8,128)(2,1)S(1)}, bf16[8,2,64,256]{3,2,0,1:T(8,128)(2,1)S(1)}, u32[]{:S(2)}, u32[]{:S(2)}) collective-permute-start(bf16[8,2,64,256]{3,2,0,1:T(8,128)(2,1)S(1)} %copy.13), channel_id=1, source_target_pairs={{0,8},{1,9},{2,10},{3,11},{4,12},{5,13},{6,14},{7,15},{8,0},{9,1},... | collective-permute-start | bytes 1572872 | tf_op jit(solution)/shard_map/s_p1/ppermute | solution.py:50
  30.1 11.1 %collective-permute-done.1 = bf16[8,2,64,256]{3,2,0,1:T(8,128)(2,1)S(1)} collective-permute-done((bf16[8,2,64,256]{3,2,0,1:T(8,128)(2,1)S(1)}, bf16[8,2,64,256]{3,2,0,1:T(8,128)(2,1)S(1)}, u32[]{:S(2)}, u32[]{:S(2)}) %collective-permute-start.1) | collective-permute-done | bytes 524320 | tf_op jit(solution)/shard_map/s_p1/ppermute | solution.py:50
  42.5 1.4 %collective-permute-done = bf16[8,2,64,256]{3,2,0,1:T(8,128)(2,1)S(1)} collective-permute-done((bf16[8,2,64,256]{3,2,0,1:T(8,128)(2,1)S(1)}, bf16[8,2,64,256]{3,2,0,1:T(8,128)(2,1)S(1)}, u32[]{:S(2)}, u32[]{:S(2)}) %collective-permute-start) | collective-permute-done | bytes 524320 | tf_op jit(solution)/shard_map/s_p1/ppermute | solution.py:50
  44.8 2.1 %collective-permute-start.3 = (bf16[32,64,256]{2,1,0:T(8,128)(2,1)S(1)}, bf16[32,64,256]{2,1,0:T(8,128)(2,1)S(1)}, u32[]{:S(2)}, u32[]{:S(2)}) collective-permute-start(bf16[32,64,256]{2,1,0:T(8,128)(2,1)S(1)} %pad_maximum_fusion.1.refs_1_), channel_id=1, source_target_pairs={{0,1},{1,2},{2,3},{3,0},{4,5},{5,6},{6,7},{7,4},{8,9},{9,10},{10,1... | collective-permute-start | bytes 3145736 | tf_op jit(solution)/shard_map/s_p2a/ppermute | solution.py:50
  47.0 1.8 %collective-permute-done.14 = bf16[4,256,128]{2,1,0:T(8,128)(2,1)S(1)} collective-permute-done((bf16[4,256,128]{2,1,0:T(8,128)(2,1)S(1)}, bf16[4,256,128]{2,1,0:T(8,128)(2,1)S(1)}, u32[]{:S(2)}, u32[]{:S(2)}) %collective-permute-start.14) | collective-permute-done | bytes 262176 | tf_op jit(solution)/shard_map/s_c2/ppermute | solution.py:50
  51.0 8.6 %collective-permute-done.4.refs_3_ = bf16[32,64,256]{2,1,0:T(8,128)(2,1)S(1)} collective-permute-done((bf16[32,64,256]{2,1,0:T(8,128)(2,1)S(1)}, bf16[32,64,256]{2,1,0:T(8,128)(2,1)S(1)}, u32[]{:S(2)}, u32[]{:S(2)}) %collective-permute-start.4) | collective-permute-done | bytes 1048608 | tf_op jit(solution)/shard_map/s_p2a/ppermute | solution.py:50
  62.1 2.5 %collective-permute-start.6 = (bf16[32,64,256]{2,1,0:T(8,128)(2,1)S(1)}, bf16[32,64,256]{2,1,0:T(8,128)(2,1)S(1)}, u32[]{:S(2)}, u32[]{:S(2)}) collective-permute-start(bf16[32,64,256]{2,1,0:T(8,128)(2,1)S(1)} %pad_maximum_fusion.refs_2_), channel_id=1, source_target_pairs={{0,3},{1,0},{2,1},{3,2},{4,7},{5,4},{6,5},{7,6},{8,11},{9,8},{10,9... | collective-permute-start | bytes 3145736 | tf_op jit(solution)/shard_map/s_p2b/ppermute | solution.py:50
  64.5 4.4 %collective-permute-done.8.refs_5_ = bf16[16,64,256]{2,1,0:T(8,128)(2,1)S(1)} collective-permute-done((bf16[16,64,256]{2,1,0:T(8,128)(2,1)S(1)}, bf16[16,64,256]{2,1,0:T(8,128)(2,1)S(1)}, u32[]{:S(2)}, u32[]{:S(2)}) %collective-permute-start.8) | collective-permute-done | bytes 524320 | tf_op jit(solution)/shard_map/s_f2a/ppermute | solution.py:50
  69.0 2.0 %collective-permute-start.5 = (bf16[32,64,256]{2,1,0:T(8,128)(2,1)S(1)}, bf16[32,64,256]{2,1,0:T(8,128)(2,1)S(1)}, u32[]{:S(2)}, u32[]{:S(2)}) collective-permute-start(bf16[32,64,256]{2,1,0:T(8,128)(2,1)S(1)} %pad_maximum_fusion.refs_2_), channel_id=1, source_target_pairs={{0,1},{1,2},{2,3},{3,0},{4,5},{5,6},{6,7},{7,4},{8,9},{9,10},{10,1... | collective-permute-start | bytes 3145736 | tf_op jit(solution)/shard_map/s_p2b/ppermute | solution.py:50
  71.9 2.4 %collective-permute-start.20 = (bf16[8,256,128]{2,1,0:T(8,128)(2,1)S(1)}, bf16[8,256,128]{2,1,0:T(8,128)(2,1)S(1)}, u32[]{:S(2)}, u32[]{:S(2)}) collective-permute-start(bf16[8,256,128]{2,1,0:T(8,128)(2,1)S(1)} %slice.55), channel_id=1, source_target_pairs={{0,96},{1,97},{2,98},{3,99},{4,100},{5,101},{6,102},{7,103},{8,104... | collective-permute-start | bytes 1572872 | tf_op jit(solution)/shard_map/s_zf/ppermute | solution.py:50
  74.5 7.6 %left_of_slab.1.refs_18_ = bf16[512,2048]{1,0:T(8,128)(2,1)S(1)} custom-call(s32[8,256]{1,0:T(8,128)S(1)} %copy-done.1, bf16[32,64,256]{2,1,0:T(8,128)(2,1)S(1)} %pad_maximum_fusion.1.refs_1_, bf16[32,64,256]{2,1,0:T(8,128)(2,1)S(1)} %collective-permute-done.3.refs_2_, bf16[32,64,256]{2,1,0:T(8,128)(2,1)S(1)} %collective-permute-done.4.refs_3_, ...), custom_call_target="tpu_custom_call" | custom-call | flops 8999999488 | bytes 7000000 | tf_op jit(solution)/shard_map/left_of_slab/pallas_call | solution.py:381
  82.2 3.8 %collective-permute-start.10 = (bf16[16,64,256]{2,1,0:T(8,128)(2,1)S(1)}, bf16[16,64,256]{2,1,0:T(8,128)(2,1)S(1)}, u32[]{:S(2)}, u32[]{:S(2)}) collective-permute-start(bf16[16,64,256]{2,1,0:T(8,128)(2,1)S(1)} %slice.53), channel_id=1, source_target_pairs={{0,3},{1,0},{2,1},{3,2},{4,7},{5,4},{6,5},{7,6},{8,11},{9,8},{10,9... | collective-permute-start | bytes 1572872 | tf_op jit(solution)/shard_map/s_f2b/ppermute | solution.py:50
  86.3 3.4 %collective-permute-done.19.refs_11_ = bf16[8,256,128]{2,1,0:T(8,128)(2,1)S(1)} collective-permute-done((bf16[8,256,128]{2,1,0:T(8,128)(2,1)S(1)}, bf16[8,256,128]{2,1,0:T(8,128)(2,1)S(1)}, u32[]{:S(2)}, u32[]{:S(2)}) %collective-permute-start.19) | collective-permute-done | bytes 524320 | tf_op jit(solution)/shard_map/s_zf/ppermute | solution.py:50
  89.8 2.9 %collective-permute-done.10.refs_6_ = bf16[16,64,256]{2,1,0:T(8,128)(2,1)S(1)} collective-permute-done((bf16[16,64,256]{2,1,0:T(8,128)(2,1)S(1)}, bf16[16,64,256]{2,1,0:T(8,128)(2,1)S(1)}, u32[]{:S(2)}, u32[]{:S(2)}) %collective-permute-start.10) | collective-permute-done | bytes 524320 | tf_op jit(solution)/shard_map/s_f2b/ppermute | solution.py:50
  92.6 3.8 %collective-permute-done.9.refs_5_ = bf16[16,64,256]{2,1,0:T(8,128)(2,1)S(1)} collective-permute-done((bf16[16,64,256]{2,1,0:T(8,128)(2,1)S(1)}, bf16[16,64,256]{2,1,0:T(8,128)(2,1)S(1)}, u32[]{:S(2)}, u32[]{:S(2)}) %collective-permute-start.9) | collective-permute-done | bytes 524320 | tf_op jit(solution)/shard_map/s_f2b/ppermute | solution.py:50
  96.5 1.9 %collective-permute-done.24.refs_16_ = bf16[8,256,128]{2,1,0:T(8,128)(2,1)S(1)} collective-permute-done((bf16[8,256,128]{2,1,0:T(8,128)(2,1)S(1)}, bf16[8,256,128]{2,1,0:T(8,128)(2,1)S(1)}, u32[]{:S(2)}, u32[]{:S(2)}) %collective-permute-start.24) | collective-permute-done | bytes 524320 | tf_op jit(solution)/shard_map/s_swap/ppermute | solution.py:50
  98.4 19.3 %finish.1 = bf16[2,512,2048]{2,1,0:T(8,128)(2,1)} custom-call(s32[8,256]{1,0:T(8,128)S(1)} %copy-done.1, s32[4]{0:T(128)S(1)} %copy-done.2, bf16[32,64,256]{2,1,0:T(8,128)(2,1)S(1)} %pad_maximum_fusion.refs_2_, bf16[32,64,256]{2,1,0:T(8,128)(2,1)S(1)} %collective-permute-done.5.refs_3_, bf16[32,64,256]{2,1,0:T(8,128)(2,1)S(1)} %collective-permute-done.6.refs_4_, ...), custom_call_target="tpu_custom_call" | custom-call | flops 17999998976 | bytes 20000000 | tf_op jit(solution)/shard_map/finish/pallas_call | solution.py:409
  (65 shorter events, 12.9 us)
Async XLA Ops:
  4.7 15.8 %all-to-all-start = ((bf16[8,2,64,256]{3,2,1,0:T(8,128)(2,1)}), bf16[8,2,64,256]{3,2,1,0:T(8,128)(2,1)S(1)}, u32[]{:S(2)}, u32[]{:S(2)}) async-start(bf16[8,2,64,256]{3,2,1,0:T(8,128)(2,1)} %bitcast.34), calls=%async_computation | async-start | bytes 1048576 | tf_op jit(solution)/shard_map/all_to_all | solution.py:438
  10.1 13.2 %collective-permute-start.13 = (bf16[256,128]{1,0:T(8,128)(2,1)S(1)}, bf16[256,128]{1,0:T(8,128)(2,1)S(1)}, u32[]{:S(2)}, u32[]{:S(2)}) collective-permute-start(bf16[256,128]{1,0:T(8,128)(2,1)S(1)} %get-tuple-element.30), channel_id=1, source_target_pairs={{0,8},{1,9},{2,10},{3,11},{4,12},{5,13},{6,14},{7,15},{8,0},{9,1},... | collective-permute-start | bytes 196616 | tf_op jit(solution)/shard_map/s_c1/ppermute | solution.py:50
  13.2 10.1 %collective-permute-start.12 = (bf16[256,128]{1,0:T(8,128)(2,1)S(1)}, bf16[256,128]{1,0:T(8,128)(2,1)S(1)}, u32[]{:S(2)}, u32[]{:S(2)}) collective-permute-start(bf16[256,128]{1,0:T(8,128)(2,1)S(1)} %get-tuple-element.30), channel_id=1, source_target_pairs={{0,12},{1,13},{2,14},{3,15},{4,0},{5,1},{6,2},{7,3},{8,4},{9,5},{1... | collective-permute-start | bytes 196616 | tf_op jit(solution)/shard_map/s_c1/ppermute | solution.py:50
  14.3 9.0 %collective-permute-start.11 = (bf16[256,128]{1,0:T(8,128)(2,1)S(1)}, bf16[256,128]{1,0:T(8,128)(2,1)S(1)}, u32[]{:S(2)}, u32[]{:S(2)}) collective-permute-start(bf16[256,128]{1,0:T(8,128)(2,1)S(1)} %get-tuple-element.30), channel_id=1, source_target_pairs={{0,4},{1,5},{2,6},{3,7},{4,8},{5,9},{6,10},{7,11},{8,12},{9,13},{1... | collective-permute-start | bytes 196616 | tf_op jit(solution)/shard_map/s_c1/ppermute | solution.py:50
  20.5 20.8 %collective-permute-start.1 = (bf16[8,2,64,256]{3,2,0,1:T(8,128)(2,1)S(1)}, bf16[8,2,64,256]{3,2,0,1:T(8,128)(2,1)S(1)}, u32[]{:S(2)}, u32[]{:S(2)}) collective-permute-start(bf16[8,2,64,256]{3,2,0,1:T(8,128)(2,1)S(1)} %copy.13), channel_id=1, source_target_pairs={{0,12},{1,13},{2,14},{3,15},{4,0},{5,1},{6,2},{7,3},{8,4},{9,5},{1... | collective-permute-start | bytes 1572872 | tf_op jit(solution)/shard_map/s_p1/ppermute | solution.py:50
  23.3 25.6 %collective-permute-start.16 = (bf16[4,256,128]{2,1,0:T(8,128)(2,1)S(1)}, bf16[4,256,128]{2,1,0:T(8,128)(2,1)S(1)}, u32[]{:S(2)}, u32[]{:S(2)}) collective-permute-start(bf16[4,256,128]{2,1,0:T(8,128)(2,1)S(1)} %pad_maximum_fusion.2), channel_id=1, source_target_pairs={{0,2},{1,3},{2,0},{3,1},{4,6},{5,7},{6,4},{7,5},{8,10},{9,11},{10,... | collective-permute-start | bytes 786440 | tf_op jit(solution)/shard_map/s_c2/ppermute | solution.py:50
  26.6 22.2 %collective-permute-start.15 = (bf16[4,256,128]{2,1,0:T(8,128)(2,1)S(1)}, bf16[4,256,128]{2,1,0:T(8,128)(2,1)S(1)}, u32[]{:S(2)}, u32[]{:S(2)}) collective-permute-start(bf16[4,256,128]{2,1,0:T(8,128)(2,1)S(1)} %pad_maximum_fusion.2), channel_id=1, source_target_pairs={{0,3},{1,0},{2,1},{3,2},{4,7},{5,4},{6,5},{7,6},{8,11},{9,8},{10,9... | collective-permute-start | bytes 786440 | tf_op jit(solution)/shard_map/s_c2/ppermute | solution.py:50
  27.7 16.3 %collective-permute-start = (bf16[8,2,64,256]{3,2,0,1:T(8,128)(2,1)S(1)}, bf16[8,2,64,256]{3,2,0,1:T(8,128)(2,1)S(1)}, u32[]{:S(2)}, u32[]{:S(2)}) collective-permute-start(bf16[8,2,64,256]{3,2,0,1:T(8,128)(2,1)S(1)} %copy.13), channel_id=1, source_target_pairs={{0,4},{1,5},{2,6},{3,7},{4,8},{5,9},{6,10},{7,11},{8,12},{9,13},{1... | collective-permute-start | bytes 1572872 | tf_op jit(solution)/shard_map/s_p1/ppermute | solution.py:50
  27.7 16.3 %collective-permute-start.2 = (bf16[8,2,64,256]{3,2,0,1:T(8,128)(2,1)S(1)}, bf16[8,2,64,256]{3,2,0,1:T(8,128)(2,1)S(1)}, u32[]{:S(2)}, u32[]{:S(2)}) collective-permute-start(bf16[8,2,64,256]{3,2,0,1:T(8,128)(2,1)S(1)} %copy.13), channel_id=1, source_target_pairs={{0,8},{1,9},{2,10},{3,11},{4,12},{5,13},{6,14},{7,15},{8,0},{9,1},... | collective-permute-start | bytes 1572872 | tf_op jit(solution)/shard_map/s_p1/ppermute | solution.py:50
  44.2 15.5 %collective-permute-start.4 = (bf16[32,64,256]{2,1,0:T(8,128)(2,1)S(1)}, bf16[32,64,256]{2,1,0:T(8,128)(2,1)S(1)}, u32[]{:S(2)}, u32[]{:S(2)}) collective-permute-start(bf16[32,64,256]{2,1,0:T(8,128)(2,1)S(1)} %pad_maximum_fusion.1.refs_1_), channel_id=1, source_target_pairs={{0,3},{1,0},{2,1},{3,2},{4,7},{5,4},{6,5},{7,6},{8,11},{9,8},{10,9... | collective-permute-start | bytes 3145736 | tf_op jit(solution)/shard_map/s_p2a/ppermute | solution.py:50
  44.8 16.1 %collective-permute-start.3 = (bf16[32,64,256]{2,1,0:T(8,128)(2,1)S(1)}, bf16[32,64,256]{2,1,0:T(8,128)(2,1)S(1)}, u32[]{:S(2)}, u32[]{:S(2)}) collective-permute-start(bf16[32,64,256]{2,1,0:T(8,128)(2,1)S(1)} %pad_maximum_fusion.1.refs_1_), channel_id=1, source_target_pairs={{0,1},{1,2},{2,3},{3,0},{4,5},{5,6},{6,7},{7,4},{8,9},{9,10},{10,1... | collective-permute-start | bytes 3145736 | tf_op jit(solution)/shard_map/s_p2a/ppermute | solution.py:50
  48.9 22.9 %collective-permute-start.18 = (bf16[16,256,128]{2,1,0:T(8,128)(2,1)S(1)}, bf16[16,256,128]{2,1,0:T(8,128)(2,1)S(1)}, u32[]{:S(2)}, u32[]{:S(2)}) collective-permute-start(bf16[16,256,128]{2,1,0:T(8,128)(2,1)S(1)} %constant_dynamic-update-slice_fusion.refs_8_), channel_id=1, source_target_pairs={{0,96},{1,97},{2,98},{3,99},{4,100},{5,101},{6,102},{7,103},{8,104... | collective-permute-start | bytes 3145736 | tf_op jit(solution)/shard_map/s_z1/ppermute | solution.py:50
  50.2 24.2 %collective-permute-start.17 = (bf16[16,256,128]{2,1,0:T(8,128)(2,1)S(1)}, bf16[16,256,128]{2,1,0:T(8,128)(2,1)S(1)}, u32[]{:S(2)}, u32[]{:S(2)}) collective-permute-start(bf16[16,256,128]{2,1,0:T(8,128)(2,1)S(1)} %constant_dynamic-update-slice_fusion.refs_8_), channel_id=1, source_target_pairs={{0,32},{1,33},{2,34},{3,35},{4,36},{5,37},{6,38},{7,39},{8,40},{9,... | collective-permute-start | bytes 3145736 | tf_op jit(solution)/shard_map/s_z1/ppermute | solution.py:50
  59.7 9.2 %collective-permute-start.8 = (bf16[16,64,256]{2,1,0:T(8,128)(2,1)S(1)}, bf16[16,64,256]{2,1,0:T(8,128)(2,1)S(1)}, u32[]{:S(2)}, u32[]{:S(2)}) collective-permute-start(bf16[16,64,256]{2,1,0:T(8,128)(2,1)S(1)} %slice.65), channel_id=1, source_target_pairs={{0,3},{1,0},{2,1},{3,2},{4,7},{5,4},{6,5},{7,6},{8,11},{9,8},{10,9... | collective-permute-start | bytes 1572872 | tf_op jit(solution)/shard_map/s_f2a/ppermute | solution.py:50
  61.0 10.9 %collective-permute-start.7 = (bf16[16,64,256]{2,1,0:T(8,128)(2,1)S(1)}, bf16[16,64,256]{2,1,0:T(8,128)(2,1)S(1)}, u32[]{:S(2)}, u32[]{:S(2)}) collective-permute-start(bf16[16,64,256]{2,1,0:T(8,128)(2,1)S(1)} %slice.64), channel_id=1, source_target_pairs={{0,1},{1,2},{2,3},{3,0},{4,5},{5,6},{6,7},{7,4},{8,9},{9,10},{10,1... | collective-permute-start | bytes 1572872 | tf_op jit(solution)/shard_map/s_f2a/ppermute | solution.py:50
  62.1 20.0 %collective-permute-start.6 = (bf16[32,64,256]{2,1,0:T(8,128)(2,1)S(1)}, bf16[32,64,256]{2,1,0:T(8,128)(2,1)S(1)}, u32[]{:S(2)}, u32[]{:S(2)}) collective-permute-start(bf16[32,64,256]{2,1,0:T(8,128)(2,1)S(1)} %pad_maximum_fusion.refs_2_), channel_id=1, source_target_pairs={{0,3},{1,0},{2,1},{3,2},{4,7},{5,4},{6,5},{7,6},{8,11},{9,8},{10,9... | collective-permute-start | bytes 3145736 | tf_op jit(solution)/shard_map/s_p2b/ppermute | solution.py:50
  69.0 17.0 %collective-permute-start.5 = (bf16[32,64,256]{2,1,0:T(8,128)(2,1)S(1)}, bf16[32,64,256]{2,1,0:T(8,128)(2,1)S(1)}, u32[]{:S(2)}, u32[]{:S(2)}) collective-permute-start(bf16[32,64,256]{2,1,0:T(8,128)(2,1)S(1)} %pad_maximum_fusion.refs_2_), channel_id=1, source_target_pairs={{0,1},{1,2},{2,3},{3,0},{4,5},{5,6},{6,7},{7,4},{8,9},{9,10},{10,1... | collective-permute-start | bytes 3145736 | tf_op jit(solution)/shard_map/s_p2b/ppermute | solution.py:50
  71.9 24.6 %collective-permute-start.21 = (bf16[16,256,128]{2,1,0:T(8,128)(2,1)S(1)}, bf16[16,256,128]{2,1,0:T(8,128)(2,1)S(1)}, u32[]{:S(2)}, u32[]{:S(2)}) collective-permute-start(bf16[16,256,128]{2,1,0:T(8,128)(2,1)S(1)} %constant_dynamic-update-slice_fusion.refs_8_), channel_id=1, source_target_pairs={{0,16},{1,17},{2,18},{3,19},{4,20},{5,21},{6,22},{7,23},{8,24},{9,... | collective-permute-start | bytes 3145736 | tf_op jit(solution)/shard_map/s_swap/ppermute | solution.py:50
  71.9 14.4 %collective-permute-start.20 = (bf16[8,256,128]{2,1,0:T(8,128)(2,1)S(1)}, bf16[8,256,128]{2,1,0:T(8,128)(2,1)S(1)}, u32[]{:S(2)}, u32[]{:S(2)}) collective-permute-start(bf16[8,256,128]{2,1,0:T(8,128)(2,1)S(1)} %slice.55), channel_id=1, source_target_pairs={{0,96},{1,97},{2,98},{3,99},{4,100},{5,101},{6,102},{7,103},{8,104... | collective-permute-start | bytes 1572872 | tf_op jit(solution)/shard_map/s_zf/ppermute | solution.py:50
  74.4 15.3 %collective-permute-start.19 = (bf16[8,256,128]{2,1,0:T(8,128)(2,1)S(1)}, bf16[8,256,128]{2,1,0:T(8,128)(2,1)S(1)}, u32[]{:S(2)}, u32[]{:S(2)}) collective-permute-start(bf16[8,256,128]{2,1,0:T(8,128)(2,1)S(1)} %slice.54), channel_id=1, source_target_pairs={{0,32},{1,33},{2,34},{3,35},{4,36},{5,37},{6,38},{7,39},{8,40},{9,... | collective-permute-start | bytes 1572872 | tf_op jit(solution)/shard_map/s_zf/ppermute | solution.py:50
  82.2 10.5 %collective-permute-start.10 = (bf16[16,64,256]{2,1,0:T(8,128)(2,1)S(1)}, bf16[16,64,256]{2,1,0:T(8,128)(2,1)S(1)}, u32[]{:S(2)}, u32[]{:S(2)}) collective-permute-start(bf16[16,64,256]{2,1,0:T(8,128)(2,1)S(1)} %slice.53), channel_id=1, source_target_pairs={{0,3},{1,0},{2,1},{3,2},{4,7},{5,4},{6,5},{7,6},{8,11},{9,8},{10,9... | collective-permute-start | bytes 1572872 | tf_op jit(solution)/shard_map/s_f2b/ppermute | solution.py:50
  86.0 10.5 %collective-permute-start.9 = (bf16[16,64,256]{2,1,0:T(8,128)(2,1)S(1)}, bf16[16,64,256]{2,1,0:T(8,128)(2,1)S(1)}, u32[]{:S(2)}, u32[]{:S(2)}) collective-permute-start(bf16[16,64,256]{2,1,0:T(8,128)(2,1)S(1)} %slice.52), channel_id=1, source_target_pairs={{0,1},{1,2},{2,3},{3,0},{4,5},{5,6},{6,7},{7,4},{8,9},{9,10},{10,1... | collective-permute-start | bytes 1572872 | tf_op jit(solution)/shard_map/s_f2b/ppermute | solution.py:50
  86.3 10.1 %collective-permute-start.23 = (bf16[16,256,128]{2,1,0:T(8,128)(2,1)S(1)}, bf16[16,256,128]{2,1,0:T(8,128)(2,1)S(1)}, u32[]{:S(2)}, u32[]{:S(2)}) collective-permute-start(bf16[16,256,128]{2,1,0:T(8,128)(2,1)S(1)} %collective-permute-done.18.refs_10_), channel_id=1, source_target_pairs={{0,16},{1,17},{2,18},{3,19},{4,20},{5,21},{6,22},{7,23},{8,24},{9,... | collective-permute-start | bytes 3145736 | tf_op jit(solution)/shard_map/s_swap/ppermute | solution.py:50
  89.8 8.6 %collective-permute-start.22 = (bf16[16,256,128]{2,1,0:T(8,128)(2,1)S(1)}, bf16[16,256,128]{2,1,0:T(8,128)(2,1)S(1)}, u32[]{:S(2)}, u32[]{:S(2)}) collective-permute-start(bf16[16,256,128]{2,1,0:T(8,128)(2,1)S(1)} %collective-permute-done.17.refs_9_), channel_id=1, source_target_pairs={{0,16},{1,17},{2,18},{3,19},{4,20},{5,21},{6,22},{7,23},{8,24},{9,... | collective-permute-start | bytes 3145736 | tf_op jit(solution)/shard_map/s_swap/ppermute | solution.py:50
  (7 other events, 67.4 us)

commit v5 on v4

--- a/solution.py
+++ b/solution.py
@@ -288,7 +288,7 @@
                 target, sums = terms(kind, step * UNROLL + u)
                 acc[target] += sums
 
-    @pl.loop(0, NSH // 2, unroll=4)
+    @pl.loop(0, NSH // 2, unroll=8)
     def _(t):
         for rp in range(2):
             even = acc[2 * t, :, rp * 128:rp * 128 + 128]
@@ -348,7 +348,7 @@
             sem_out.at[slot],
         )
 
-    @pl.loop(0, ACT // 256, unroll=2)
+    @pl.loop(0, ACT // 256, unroll=4)
     def _(n):
         slot = n % 2
 

time: 119 us -> 119 us (level)
  no operation moved by 1% of the time
where the time goes in v5:
time: 119 us; the launch traced here: 118 us
  waiting for transfers between devices  42.4 us (36%)
  starting transfers between devices  39 us (33%)
  Pallas kernels  33.5 us (28%)
  local copies, waits for them, and re-layouts  1.34 us (1%)
    ppermute x26, waiting for transfers between devices, send(): return lax.ppermute(value, AXES, pairs)  40.6 us
    ppermute x26, starting transfers between devices, send(): return lax.ppermute(value, AXES, pairs)  33.6 us
    pallas_call x1, Pallas kernels, finish(): pl.pallas_call(finish_kernel, out_shape=jax.ShapeDtypeStruct((2, ROWS, AC...  19.2 us
    pallas_call x1, Pallas kernels, left_of_slab(): pl.pallas_call(left_kernel, out_shape=jax.ShapeDtypeStruct((ROWS, NAO), j...  7.63 us
    all_to_all x1, starting transfers between devices, body(): owned = lax.all_to_all(half, 'ao', split_axis=0, concat_axis=0, tiled=True)  5.41 us
    pallas_call x1, Pallas kernels, ket_transform(): pl.pallas_call(ket_kernel, out_shape=jax.ShapeDtypeStruct((NJ * 2 * SH, N...  4.64 us
  transfers between devices with their start and end apart: 27, of which 12 were waited for; matrix products, arithmetic and copies ran while one was open for 2% of the time, Pallas kernels for 8%

profile of v5, /device:TPU:0, one launch (start us, length us, event | category | flops | bytes accessed | tf_op | source)
XLA Modules:
  0.0 117.6 jit_solution(12170760573726787381)
XLA Ops:
  0.0 4.6 %ket_transform.1 = bf16[1024,256]{1,0:T(8,128)(2,1)} custom-call(s32[2]{0:T(128)} %slabs_ref.1, bf16[16,32]{1,0:T(8,128)(2,1)} %lam_ref.1, bf16[8,16]{1,0:T(8,128)(2,1)} %bitcast.40, bf16[1,4096,256]{2,1,0:T(8,128)(2,1)} %ints_hbm.1), custom_call_target="tpu_custom_call" | custom-call | flops 140000000 | bytes 3000000 | tf_op jit(solution)/shard_map/ket_transform/pallas_call | solution.py:126
  4.7 5.4 %all-to-all-start = ((bf16[8,2,64,256]{3,2,1,0:T(8,128)(2,1)}), bf16[8,2,64,256]{3,2,1,0:T(8,128)(2,1)S(1)}, u32[]{:S(2)}, u32[]{:S(2)}) async-start(bf16[8,2,64,256]{3,2,1,0:T(8,128)(2,1)} %bitcast.34), calls=%async_computation | async-start | bytes 1048576 | tf_op jit(solution)/shard_map/all_to_all | solution.py:438
  10.1 3.1 %collective-permute-start.13 = (bf16[256,128]{1,0:T(8,128)(2,1)S(1)}, bf16[256,128]{1,0:T(8,128)(2,1)S(1)}, u32[]{:S(2)}, u32[]{:S(2)}) collective-permute-start(bf16[256,128]{1,0:T(8,128)(2,1)S(1)} %get-tuple-element.30), channel_id=1, source_target_pairs={{0,8},{1,9},{2,10},{3,11},{4,12},{5,13},{6,14},{7,15},{8,0},{9,1},... | collective-permute-start | bytes 196616 | tf_op jit(solution)/shard_map/s_c1/ppermute | solution.py:50
  16.6 2.0 %plan_terms.1.refs_0_ = s32[8,256]{1,0:T(8,128)} custom-call(s32[4]{0:T(128)} %pad_add_fusion.place_ref.refs_1_, s32[128,2]{1,0:T(8,128)} %copy.12.pairs_ref, s32[2,128]{1,0:T(2,128)} %bitcast.39), custom_call_target="tpu_custom_call" | custom-call | flops 2000000 | bytes 10000 | tf_op jit(solution)/shard_map/plan_terms/pallas_call | solution.py:206
  18.6 1.8 %all-to-all-done = bf16[8,2,64,256]{3,2,1,0:T(8,128)(2,1)S(1)} async-done(((bf16[8,2,64,256]{3,2,1,0:T(8,128)(2,1)}), bf16[8,2,64,256]{3,2,1,0:T(8,128)(2,1)S(1)}, u32[]{:S(2)}, u32[]{:S(2)}) %all-to-all-start) | async-done | bytes 524320 | tf_op jit(solution)/shard_map/all_to_all | solution.py:438
  20.5 2.8 %collective-permute-start.1 = (bf16[8,2,64,256]{3,2,0,1:T(8,128)(2,1)S(1)}, bf16[8,2,64,256]{3,2,0,1:T(8,128)(2,1)S(1)}, u32[]{:S(2)}, u32[]{:S(2)}) collective-permute-start(bf16[8,2,64,256]{3,2,0,1:T(8,128)(2,1)S(1)} %copy.13), channel_id=1, source_target_pairs={{0,12},{1,13},{2,14},{3,15},{4,0},{5,1},{6,2},{7,3},{8,4},{9,5},{1... | collective-permute-start | bytes 1572872 | tf_op jit(solution)/shard_map/s_p1/ppermute | solution.py:50
  23.3 3.3 %collective-permute-start.16 = (bf16[4,256,128]{2,1,0:T(8,128)(2,1)S(1)}, bf16[4,256,128]{2,1,0:T(8,128)(2,1)S(1)}, u32[]{:S(2)}, u32[]{:S(2)}) collective-permute-start(bf16[4,256,128]{2,1,0:T(8,128)(2,1)S(1)} %pad_maximum_fusion.2), channel_id=1, source_target_pairs={{0,2},{1,3},{2,0},{3,1},{4,6},{5,7},{6,4},{7,5},{8,10},{9,11},{10,... | collective-permute-start | bytes 786440 | tf_op jit(solution)/shard_map/s_c2/ppermute | solution.py:50
  27.7 2.4 %collective-permute-start.2 = (bf16[8,2,64,256]{3,2,0,1:T(8,128)(2,1)S(1)}, bf16[8,2,64,256]{3,2,0,1:T(8,128)(2,1)S(1)}, u32[]{:S(2)}, u32[]{:S(2)}) collective-permute-start(bf16[8,2,64,256]{3,2,0,1:T(8,128)(2,1)S(1)} %copy.13), channel_id=1, source_target_pairs={{0,8},{1,9},{2,10},{3,11},{4,12},{5,13},{6,14},{7,15},{8,0},{9,1},... | collective-permute-start | bytes 1572872 | tf_op jit(solution)/shard_map/s_p1/ppermute | solution.py:50
  30.1 11.1 %collective-permute-done.1 = bf16[8,2,64,256]{3,2,0,1:T(8,128)(2,1)S(1)} collective-permute-done((bf16[8,2,64,256]{3,2,0,1:T(8,128)(2,1)S(1)}, bf16[8,2,64,256]{3,2,0,1:T(8,128)(2,1)S(1)}, u32[]{:S(2)}, u32[]{:S(2)}) %collective-permute-start.1) | collective-permute-done | bytes 524320 | tf_op jit(solution)/shard_map/s_p1/ppermute | solution.py:50
  42.5 1.4 %collective-permute-done = bf16[8,2,64,256]{3,2,0,1:T(8,128)(2,1)S(1)} collective-permute-done((bf16[8,2,64,256]{3,2,0,1:T(8,128)(2,1)S(1)}, bf16[8,2,64,256]{3,2,0,1:T(8,128)(2,1)S(1)}, u32[]{:S(2)}, u32[]{:S(2)}) %collective-permute-start) | collective-permute-done | bytes 524320 | tf_op jit(solution)/shard_map/s_p1/ppermute | solution.py:50
  44.8 2.1 %collective-permute-start.3 = (bf16[32,64,256]{2,1,0:T(8,128)(2,1)S(1)}, bf16[32,64,256]{2,1,0:T(8,128)(2,1)S(1)}, u32[]{:S(2)}, u32[]{:S(2)}) collective-permute-start(bf16[32,64,256]{2,1,0:T(8,128)(2,1)S(1)} %pad_maximum_fusion.1.refs_1_), channel_id=1, source_target_pairs={{0,1},{1,2},{2,3},{3,0},{4,5},{5,6},{6,7},{7,4},{8,9},{9,10},{10,1... | collective-permute-start | bytes 3145736 | tf_op jit(solution)/shard_map/s_p2a/ppermute | solution.py:50
  47.0 1.8 %collective-permute-done.14 = bf16[4,256,128]{2,1,0:T(8,128)(2,1)S(1)} collective-permute-done((bf16[4,256,128]{2,1,0:T(8,128)(2,1)S(1)}, bf16[4,256,128]{2,1,0:T(8,128)(2,1)S(1)}, u32[]{:S(2)}, u32[]{:S(2)}) %collective-permute-start.14) | collective-permute-done | bytes 262176 | tf_op jit(solution)/shard_map/s_c2/ppermute | solution.py:50
  51.0 8.6 %collective-permute-done.4.refs_3_ = bf16[32,64,256]{2,1,0:T(8,128)(2,1)S(1)} collective-permute-done((bf16[32,64,256]{2,1,0:T(8,128)(2,1)S(1)}, bf16[32,64,256]{2,1,0:T(8,128)(2,1)S(1)}, u32[]{:S(2)}, u32[]{:S(2)}) %collective-permute-start.4) | collective-permute-done | bytes 1048608 | tf_op jit(solution)/shard_map/s_p2a/ppermute | solution.py:50
  62.1 2.5 %collective-permute-start.6 = (bf16[32,64,256]{2,1,0:T(8,128)(2,1)S(1)}, bf16[32,64,256]{2,1,0:T(8,128)(2,1)S(1)}, u32[]{:S(2)}, u32[]{:S(2)}) collective-permute-start(bf16[32,64,256]{2,1,0:T(8,128)(2,1)S(1)} %pad_maximum_fusion.refs_2_), channel_id=1, source_target_pairs={{0,3},{1,0},{2,1},{3,2},{4,7},{5,4},{6,5},{7,6},{8,11},{9,8},{10,9... | collective-permute-start | bytes 3145736 | tf_op jit(solution)/shard_map/s_p2b/ppermute | solution.py:50
  64.5 4.4 %collective-permute-done.8.refs_5_ = bf16[16,64,256]{2,1,0:T(8,128)(2,1)S(1)} collective-permute-done((bf16[16,64,256]{2,1,0:T(8,128)(2,1)S(1)}, bf16[16,64,256]{2,1,0:T(8,128)(2,1)S(1)}, u32[]{:S(2)}, u32[]{:S(2)}) %collective-permute-start.8) | collective-permute-done | bytes 524320 | tf_op jit(solution)/shard_map/s_f2a/ppermute | solution.py:50
  69.0 2.0 %collective-permute-start.5 = (bf16[32,64,256]{2,1,0:T(8,128)(2,1)S(1)}, bf16[32,64,256]{2,1,0:T(8,128)(2,1)S(1)}, u32[]{:S(2)}, u32[]{:S(2)}) collective-permute-start(bf16[32,64,256]{2,1,0:T(8,128)(2,1)S(1)} %pad_maximum_fusion.refs_2_), channel_id=1, source_target_pairs={{0,1},{1,2},{2,3},{3,0},{4,5},{5,6},{6,7},{7,4},{8,9},{9,10},{10,1... | collective-permute-start | bytes 3145736 | tf_op jit(solution)/shard_map/s_p2b/ppermute | solution.py:50
  71.9 2.4 %collective-permute-start.20 = (bf16[8,256,128]{2,1,0:T(8,128)(2,1)S(1)}, bf16[8,256,128]{2,1,0:T(8,128)(2,1)S(1)}, u32[]{:S(2)}, u32[]{:S(2)}) collective-permute-start(bf16[8,256,128]{2,1,0:T(8,128)(2,1)S(1)} %slice.55), channel_id=1, source_target_pairs={{0,96},{1,97},{2,98},{3,99},{4,100},{5,101},{6,102},{7,103},{8,104... | collective-permute-start | bytes 1572872 | tf_op jit(solution)/shard_map/s_zf/ppermute | solution.py:50
  74.5 7.6 %left_of_slab.1.refs_18_ = bf16[512,2048]{1,0:T(8,128)(2,1)S(1)} custom-call(s32[8,256]{1,0:T(8,128)S(1)} %copy-done.1, bf16[32,64,256]{2,1,0:T(8,128)(2,1)S(1)} %pad_maximum_fusion.1.refs_1_, bf16[32,64,256]{2,1,0:T(8,128)(2,1)S(1)} %collective-permute-done.3.refs_2_, bf16[32,64,256]{2,1,0:T(8,128)(2,1)S(1)} %collective-permute-done.4.refs_3_, ...), custom_call_target="tpu_custom_call" | custom-call | flops 8999999488 | bytes 7000000 | tf_op jit(solution)/shard_map/left_of_slab/pallas_call | solution.py:381
  82.2 3.6 %collective-permute-start.10 = (bf16[16,64,256]{2,1,0:T(8,128)(2,1)S(1)}, bf16[16,64,256]{2,1,0:T(8,128)(2,1)S(1)}, u32[]{:S(2)}, u32[]{:S(2)}) collective-permute-start(bf16[16,64,256]{2,1,0:T(8,128)(2,1)S(1)} %slice.53), channel_id=1, source_target_pairs={{0,3},{1,0},{2,1},{3,2},{4,7},{5,4},{6,5},{7,6},{8,11},{9,8},{10,9... | collective-permute-start | bytes 1572872 | tf_op jit(solution)/shard_map/s_f2b/ppermute | solution.py:50
  86.3 3.4 %collective-permute-done.19.refs_11_ = bf16[8,256,128]{2,1,0:T(8,128)(2,1)S(1)} collective-permute-done((bf16[8,256,128]{2,1,0:T(8,128)(2,1)S(1)}, bf16[8,256,128]{2,1,0:T(8,128)(2,1)S(1)}, u32[]{:S(2)}, u32[]{:S(2)}) %collective-permute-start.19) | collective-permute-done | bytes 524320 | tf_op jit(solution)/shard_map/s_zf/ppermute | solution.py:50
  89.8 2.7 %collective-permute-done.10.refs_6_ = bf16[16,64,256]{2,1,0:T(8,128)(2,1)S(1)} collective-permute-done((bf16[16,64,256]{2,1,0:T(8,128)(2,1)S(1)}, bf16[16,64,256]{2,1,0:T(8,128)(2,1)S(1)}, u32[]{:S(2)}, u32[]{:S(2)}) %collective-permute-start.10) | collective-permute-done | bytes 524320 | tf_op jit(solution)/shard_map/s_f2b/ppermute | solution.py:50
  92.5 3.8 %collective-permute-done.9.refs_5_ = bf16[16,64,256]{2,1,0:T(8,128)(2,1)S(1)} collective-permute-done((bf16[16,64,256]{2,1,0:T(8,128)(2,1)S(1)}, bf16[16,64,256]{2,1,0:T(8,128)(2,1)S(1)}, u32[]{:S(2)}, u32[]{:S(2)}) %collective-permute-start.9) | collective-permute-done | bytes 524320 | tf_op jit(solution)/shard_map/s_f2b/ppermute | solution.py:50
  96.3 1.9 %collective-permute-done.24.refs_16_ = bf16[8,256,128]{2,1,0:T(8,128)(2,1)S(1)} collective-permute-done((bf16[8,256,128]{2,1,0:T(8,128)(2,1)S(1)}, bf16[8,256,128]{2,1,0:T(8,128)(2,1)S(1)}, u32[]{:S(2)}, u32[]{:S(2)}) %collective-permute-start.24) | collective-permute-done | bytes 524320 | tf_op jit(solution)/shard_map/s_swap/ppermute | solution.py:50
  98.2 19.2 %finish.1 = bf16[2,512,2048]{2,1,0:T(8,128)(2,1)} custom-call(s32[8,256]{1,0:T(8,128)S(1)} %copy-done.1, s32[4]{0:T(128)S(1)} %copy-done.2, bf16[32,64,256]{2,1,0:T(8,128)(2,1)S(1)} %pad_maximum_fusion.refs_2_, bf16[32,64,256]{2,1,0:T(8,128)(2,1)S(1)} %collective-permute-done.5.refs_3_, bf16[32,64,256]{2,1,0:T(8,128)(2,1)S(1)} %collective-permute-done.6.refs_4_, ...), custom_call_target="tpu_custom_call" | custom-call | flops 17999998976 | bytes 20000000 | tf_op jit(solution)/shard_map/finish/pallas_call | solution.py:409
  (65 shorter events, 13.0 us)
Async XLA Ops:
  4.7 15.8 %all-to-all-start = ((bf16[8,2,64,256]{3,2,1,0:T(8,128)(2,1)}), bf16[8,2,64,256]{3,2,1,0:T(8,128)(2,1)S(1)}, u32[]{:S(2)}, u32[]{:S(2)}) async-start(bf16[8,2,64,256]{3,2,1,0:T(8,128)(2,1)} %bitcast.34), calls=%async_computation | async-start | bytes 1048576 | tf_op jit(solution)/shard_map/all_to_all | solution.py:438
  10.1 13.2 %collective-permute-start.13 = (bf16[256,128]{1,0:T(8,128)(2,1)S(1)}, bf16[256,128]{1,0:T(8,128)(2,1)S(1)}, u32[]{:S(2)}, u32[]{:S(2)}) collective-permute-start(bf16[256,128]{1,0:T(8,128)(2,1)S(1)} %get-tuple-element.30), channel_id=1, source_target_pairs={{0,8},{1,9},{2,10},{3,11},{4,12},{5,13},{6,14},{7,15},{8,0},{9,1},... | collective-permute-start | bytes 196616 | tf_op jit(solution)/shard_map/s_c1/ppermute | solution.py:50
  13.2 10.1 %collective-permute-start.12 = (bf16[256,128]{1,0:T(8,128)(2,1)S(1)}, bf16[256,128]{1,0:T(8,128)(2,1)S(1)}, u32[]{:S(2)}, u32[]{:S(2)}) collective-permute-start(bf16[256,128]{1,0:T(8,128)(2,1)S(1)} %get-tuple-element.30), channel_id=1, source_target_pairs={{0,12},{1,13},{2,14},{3,15},{4,0},{5,1},{6,2},{7,3},{8,4},{9,5},{1... | collective-permute-start | bytes 196616 | tf_op jit(solution)/shard_map/s_c1/ppermute | solution.py:50
  14.3 9.0 %collective-permute-start.11 = (bf16[256,128]{1,0:T(8,128)(2,1)S(1)}, bf16[256,128]{1,0:T(8,128)(2,1)S(1)}, u32[]{:S(2)}, u32[]{:S(2)}) collective-permute-start(bf16[256,128]{1,0:T(8,128)(2,1)S(1)} %get-tuple-element.30), channel_id=1, source_target_pairs={{0,4},{1,5},{2,6},{3,7},{4,8},{5,9},{6,10},{7,11},{8,12},{9,13},{1... | collective-permute-start | bytes 196616 | tf_op jit(solution)/shard_map/s_c1/ppermute | solution.py:50
  20.5 20.8 %collective-permute-start.1 = (bf16[8,2,64,256]{3,2,0,1:T(8,128)(2,1)S(1)}, bf16[8,2,64,256]{3,2,0,1:T(8,128)(2,1)S(1)}, u32[]{:S(2)}, u32[]{:S(2)}) collective-permute-start(bf16[8,2,64,256]{3,2,0,1:T(8,128)(2,1)S(1)} %copy.13), channel_id=1, source_target_pairs={{0,12},{1,13},{2,14},{3,15},{4,0},{5,1},{6,2},{7,3},{8,4},{9,5},{1... | collective-permute-start | bytes 1572872 | tf_op jit(solution)/shard_map/s_p1/ppermute | solution.py:50
  23.3 25.6 %collective-permute-start.16 = (bf16[4,256,128]{2,1,0:T(8,128)(2,1)S(1)}, bf16[4,256,128]{2,1,0:T(8,128)(2,1)S(1)}, u32[]{:S(2)}, u32[]{:S(2)}) collective-permute-start(bf16[4,256,128]{2,1,0:T(8,128)(2,1)S(1)} %pad_maximum_fusion.2), channel_id=1, source_target_pairs={{0,2},{1,3},{2,0},{3,1},{4,6},{5,7},{6,4},{7,5},{8,10},{9,11},{10,... | collective-permute-start | bytes 786440 | tf_op jit(solution)/shard_map/s_c2/ppermute | solution.py:50
  26.6 22.2 %collective-permute-start.15 = (bf16[4,256,128]{2,1,0:T(8,128)(2,1)S(1)}, bf16[4,256,128]{2,1,0:T(8,128)(2,1)S(1)}, u32[]{:S(2)}, u32[]{:S(2)}) collective-permute-start(bf16[4,256,128]{2,1,0:T(8,128)(2,1)S(1)} %pad_maximum_fusion.2), channel_id=1, source_target_pairs={{0,3},{1,0},{2,1},{3,2},{4,7},{5,4},{6,5},{7,6},{8,11},{9,8},{10,9... | collective-permute-start | bytes 786440 | tf_op jit(solution)/shard_map/s_c2/ppermute | solution.py:50
  27.7 16.3 %collective-permute-start = (bf16[8,2,64,256]{3,2,0,1:T(8,128)(2,1)S(1)}, bf16[8,2,64,256]{3,2,0,1:T(8,128)(2,1)S(1)}, u32[]{:S(2)}, u32[]{:S(2)}) collective-permute-start(bf16[8,2,64,256]{3,2,0,1:T(8,128)(2,1)S(1)} %copy.13), channel_id=1, source_target_pairs={{0,4},{1,5},{2,6},{3,7},{4,8},{5,9},{6,10},{7,11},{8,12},{9,13},{1... | collective-permute-start | bytes 1572872 | tf_op jit(solution)/shard_map/s_p1/ppermute | solution.py:50
  27.7 16.3 %collective-permute-start.2 = (bf16[8,2,64,256]{3,2,0,1:T(8,128)(2,1)S(1)}, bf16[8,2,64,256]{3,2,0,1:T(8,128)(2,1)S(1)}, u32[]{:S(2)}, u32[]{:S(2)}) collective-permute-start(bf16[8,2,64,256]{3,2,0,1:T(8,128)(2,1)S(1)} %copy.13), channel_id=1, source_target_pairs={{0,8},{1,9},{2,10},{3,11},{4,12},{5,13},{6,14},{7,15},{8,0},{9,1},... | collective-permute-start | bytes 1572872 | tf_op jit(solution)/shard_map/s_p1/ppermute | solution.py:50
  44.2 15.5 %collective-permute-start.4 = (bf16[32,64,256]{2,1,0:T(8,128)(2,1)S(1)}, bf16[32,64,256]{2,1,0:T(8,128)(2,1)S(1)}, u32[]{:S(2)}, u32[]{:S(2)}) collective-permute-start(bf16[32,64,256]{2,1,0:T(8,128)(2,1)S(1)} %pad_maximum_fusion.1.refs_1_), channel_id=1, source_target_pairs={{0,3},{1,0},{2,1},{3,2},{4,7},{5,4},{6,5},{7,6},{8,11},{9,8},{10,9... | collective-permute-start | bytes 3145736 | tf_op jit(solution)/shard_map/s_p2a/ppermute | solution.py:50
  44.8 16.1 %collective-permute-start.3 = (bf16[32,64,256]{2,1,0:T(8,128)(2,1)S(1)}, bf16[32,64,256]{2,1,0:T(8,128)(2,1)S(1)}, u32[]{:S(2)}, u32[]{:S(2)}) collective-permute-start(bf16[32,64,256]{2,1,0:T(8,128)(2,1)S(1)} %pad_maximum_fusion.1.refs_1_), channel_id=1, source_target_pairs={{0,1},{1,2},{2,3},{3,0},{4,5},{5,6},{6,7},{7,4},{8,9},{9,10},{10,1... | collective-permute-start | bytes 3145736 | tf_op jit(solution)/shard_map/s_p2a/ppermute | solution.py:50
  48.9 22.9 %collective-permute-start.18 = (bf16[16,256,128]{2,1,0:T(8,128)(2,1)S(1)}, bf16[16,256,128]{2,1,0:T(8,128)(2,1)S(1)}, u32[]{:S(2)}, u32[]{:S(2)}) collective-permute-start(bf16[16,256,128]{2,1,0:T(8,128)(2,1)S(1)} %constant_dynamic-update-slice_fusion.refs_8_), channel_id=1, source_target_pairs={{0,96},{1,97},{2,98},{3,99},{4,100},{5,101},{6,102},{7,103},{8,104... | collective-permute-start | bytes 3145736 | tf_op jit(solution)/shard_map/s_z1/ppermute | solution.py:50
  50.2 24.2 %collective-permute-start.17 = (bf16[16,256,128]{2,1,0:T(8,128)(2,1)S(1)}, bf16[16,256,128]{2,1,0:T(8,128)(2,1)S(1)}, u32[]{:S(2)}, u32[]{:S(2)}) collective-permute-start(bf16[16,256,128]{2,1,0:T(8,128)(2,1)S(1)} %constant_dynamic-update-slice_fusion.refs_8_), channel_id=1, source_target_pairs={{0,32},{1,33},{2,34},{3,35},{4,36},{5,37},{6,38},{7,39},{8,40},{9,... | collective-permute-start | bytes 3145736 | tf_op jit(solution)/shard_map/s_z1/ppermute | solution.py:50
  59.7 9.2 %collective-permute-start.8 = (bf16[16,64,256]{2,1,0:T(8,128)(2,1)S(1)}, bf16[16,64,256]{2,1,0:T(8,128)(2,1)S(1)}, u32[]{:S(2)}, u32[]{:S(2)}) collective-permute-start(bf16[16,64,256]{2,1,0:T(8,128)(2,1)S(1)} %slice.65), channel_id=1, source_target_pairs={{0,3},{1,0},{2,1},{3,2},{4,7},{5,4},{6,5},{7,6},{8,11},{9,8},{10,9... | collective-permute-start | bytes 1572872 | tf_op jit(solution)/shard_map/s_f2a/ppermute | solution.py:50
  61.0 10.9 %collective-permute-start.7 = (bf16[16,64,256]{2,1,0:T(8,128)(2,1)S(1)}, bf16[16,64,256]{2,1,0:T(8,128)(2,1)S(1)}, u32[]{:S(2)}, u32[]{:S(2)}) collective-permute-start(bf16[16,64,256]{2,1,0:T(8,128)(2,1)S(1)} %slice.64), channel_id=1, source_target_pairs={{0,1},{1,2},{2,3},{3,0},{4,5},{5,6},{6,7},{7,4},{8,9},{9,10},{10,1... | collective-permute-start | bytes 1572872 | tf_op jit(solution)/shard_map/s_f2a/ppermute | solution.py:50
  62.1 20.1 %collective-permute-start.6 = (bf16[32,64,256]{2,1,0:T(8,128)(2,1)S(1)}, bf16[32,64,256]{2,1,0:T(8,128)(2,1)S(1)}, u32[]{:S(2)}, u32[]{:S(2)}) collective-permute-start(bf16[32,64,256]{2,1,0:T(8,128)(2,1)S(1)} %pad_maximum_fusion.refs_2_), channel_id=1, source_target_pairs={{0,3},{1,0},{2,1},{3,2},{4,7},{5,4},{6,5},{7,6},{8,11},{9,8},{10,9... | collective-permute-start | bytes 3145736 | tf_op jit(solution)/shard_map/s_p2b/ppermute | solution.py:50
  69.0 16.9 %collective-permute-start.5 = (bf16[32,64,256]{2,1,0:T(8,128)(2,1)S(1)}, bf16[32,64,256]{2,1,0:T(8,128)(2,1)S(1)}, u32[]{:S(2)}, u32[]{:S(2)}) collective-permute-start(bf16[32,64,256]{2,1,0:T(8,128)(2,1)S(1)} %pad_maximum_fusion.refs_2_), channel_id=1, source_target_pairs={{0,1},{1,2},{2,3},{3,0},{4,5},{5,6},{6,7},{7,4},{8,9},{9,10},{10,1... | collective-permute-start | bytes 3145736 | tf_op jit(solution)/shard_map/s_p2b/ppermute | solution.py:50
  71.9 24.4 %collective-permute-start.21 = (bf16[16,256,128]{2,1,0:T(8,128)(2,1)S(1)}, bf16[16,256,128]{2,1,0:T(8,128)(2,1)S(1)}, u32[]{:S(2)}, u32[]{:S(2)}) collective-permute-start(bf16[16,256,128]{2,1,0:T(8,128)(2,1)S(1)} %constant_dynamic-update-slice_fusion.refs_8_), channel_id=1, source_target_pairs={{0,16},{1,17},{2,18},{3,19},{4,20},{5,21},{6,22},{7,23},{8,24},{9,... | collective-permute-start | bytes 3145736 | tf_op jit(solution)/shard_map/s_swap/ppermute | solution.py:50
  71.9 14.4 %collective-permute-start.20 = (bf16[8,256,128]{2,1,0:T(8,128)(2,1)S(1)}, bf16[8,256,128]{2,1,0:T(8,128)(2,1)S(1)}, u32[]{:S(2)}, u32[]{:S(2)}) collective-permute-start(bf16[8,256,128]{2,1,0:T(8,128)(2,1)S(1)} %slice.55), channel_id=1, source_target_pairs={{0,96},{1,97},{2,98},{3,99},{4,100},{5,101},{6,102},{7,103},{8,104... | collective-permute-start | bytes 1572872 | tf_op jit(solution)/shard_map/s_zf/ppermute | solution.py:50
  74.4 15.3 %collective-permute-start.19 = (bf16[8,256,128]{2,1,0:T(8,128)(2,1)S(1)}, bf16[8,256,128]{2,1,0:T(8,128)(2,1)S(1)}, u32[]{:S(2)}, u32[]{:S(2)}) collective-permute-start(bf16[8,256,128]{2,1,0:T(8,128)(2,1)S(1)} %slice.54), channel_id=1, source_target_pairs={{0,32},{1,33},{2,34},{3,35},{4,36},{5,37},{6,38},{7,39},{8,40},{9,... | collective-permute-start | bytes 1572872 | tf_op jit(solution)/shard_map/s_zf/ppermute | solution.py:50
  82.2 10.3 %collective-permute-start.10 = (bf16[16,64,256]{2,1,0:T(8,128)(2,1)S(1)}, bf16[16,64,256]{2,1,0:T(8,128)(2,1)S(1)}, u32[]{:S(2)}, u32[]{:S(2)}) collective-permute-start(bf16[16,64,256]{2,1,0:T(8,128)(2,1)S(1)} %slice.53), channel_id=1, source_target_pairs={{0,3},{1,0},{2,1},{3,2},{4,7},{5,4},{6,5},{7,6},{8,11},{9,8},{10,9... | collective-permute-start | bytes 1572872 | tf_op jit(solution)/shard_map/s_f2b/ppermute | solution.py:50
  85.8 10.5 %collective-permute-start.9 = (bf16[16,64,256]{2,1,0:T(8,128)(2,1)S(1)}, bf16[16,64,256]{2,1,0:T(8,128)(2,1)S(1)}, u32[]{:S(2)}, u32[]{:S(2)}) collective-permute-start(bf16[16,64,256]{2,1,0:T(8,128)(2,1)S(1)} %slice.52), channel_id=1, source_target_pairs={{0,1},{1,2},{2,3},{3,0},{4,5},{5,6},{6,7},{7,4},{8,9},{9,10},{10,1... | collective-permute-start | bytes 1572872 | tf_op jit(solution)/shard_map/s_f2b/ppermute | solution.py:50
  86.3 10.0 %collective-permute-start.23 = (bf16[16,256,128]{2,1,0:T(8,128)(2,1)S(1)}, bf16[16,256,128]{2,1,0:T(8,128)(2,1)S(1)}, u32[]{:S(2)}, u32[]{:S(2)}) collective-permute-start(bf16[16,256,128]{2,1,0:T(8,128)(2,1)S(1)} %collective-permute-done.18.refs_10_), channel_id=1, source_target_pairs={{0,16},{1,17},{2,18},{3,19},{4,20},{5,21},{6,22},{7,23},{8,24},{9,... | collective-permute-start | bytes 3145736 | tf_op jit(solution)/shard_map/s_swap/ppermute | solution.py:50
  89.8 8.5 %collective-permute-start.22 = (bf16[16,256,128]{2,1,0:T(8,128)(2,1)S(1)}, bf16[16,256,128]{2,1,0:T(8,128)(2,1)S(1)}, u32[]{:S(2)}, u32[]{:S(2)}) collective-permute-start(bf16[16,256,128]{2,1,0:T(8,128)(2,1)S(1)} %collective-permute-done.17.refs_9_), channel_id=1, source_target_pairs={{0,16},{1,17},{2,18},{3,19},{4,20},{5,21},{6,22},{7,23},{8,24},{9,... | collective-permute-start | bytes 3145736 | tf_op jit(solution)/shard_map/s_swap/ppermute | solution.py:50
  (7 other events, 67.2 us)
